TPU v7x, 128 devices: a whole 4x4x4 slice. The times are simulated.
128 devices in a mesh: row: 16 (over z_hi, x, core), col: 8 (over y, z_lo).
Axes of the slice: x: 4, y: 4, z: 4 (z_hi: 2, z_lo: 2; z = z_hi * 2 + z_lo), core: 2. Of those that a mesh axis runs over, the one named last changes fastest.
Arguments:
- a_blocks: bfloat16 [128, 128, 9216], P('row', 'col'), may hold values from -0.625 to 0.625
- a_mask: int32 [128, 128], P('row', 'col'), may hold values from 0 to 1, as said below
- p_blocks: bfloat16 [128, 64, 9216], P('row', 'col'), may hold values from -3 to 3
- p_mask: int32 [128, 64], P('row', 'col'), may hold values from 0 to 1, as said below
- section_owner: int32 [2], replicated, may hold values from 0 to 7, as said below
- agg_order: int32 [64], replicated, may hold values from 0 to 63, as said below
Outputs:
- coarse: float32 [6144, 6144], P(('row', 'col'))
Inputs may be any that keep to these rules, and one draw needn't show every extreme that they name: `a_mask`: each tile of 8 x 16 blocks (the fine block rows of one index of row and the fine block columns of one index of col) holds between 32 and 96 ones, and in every index of row some tile holds exactly 96. `section_owner`: distinct indices of col; one of the sections takes index 7. `agg_order`: each coarse block once. `p_mask`: with c = i // 2: fine block row i feeds aggregate agg_order[c] always, agg_order[c - 1] and agg_order[c + 1] possibly, agg_order[(c + 32) mod 64] always where i is a multiple of 2, aggregate ((i // 16 + 8 // 2) mod 8) * 8 + (i mod 8) always, and nothing else.
All inputs are finite; a program needn't handle non-finite values.
Results may differ from a plain program's by a relative error of at most 0.0029.
Values may be sent and summed in bfloat16 or wider, within the bound.
No kernel may reach another device: no remote copies, remote signals or barrier semaphores. Data moves between devices by JAX's collectives and lax.ppermute only.
A program may use at most 128 MiB of HBM per device.

v0:
```python
import jax
import jax.numpy as jnp
from jax import lax
from jax.experimental import pallas as pl
from jax.experimental.pallas import tpu as pltpu
from jax.sharding import PartitionSpec as P

BS = 96
BR = 8
NCB = 64
KK = 4
WIDE = KK * BS
ROWS = 16
COLS = 8
PIECE = BS // ROWS
LANES = PIECE * WIDE
USLOTS = 5
PW = 512
OUTSLOTS = 18
F32 = jnp.float32
BF16 = jnp.bfloat16


def lookup(table, index):
    hit = index[..., None] == jnp.arange(table.shape[0], dtype=jnp.int32)
    return jnp.sum(jnp.where(hit, table, 0), axis=-1)


def shift(value, axis, by):
    size = lax.axis_size(axis)
    return lax.ppermute(value, axis, [(i, (i + by) % size) for i in range(size)])


def band_columns(rows, agg_order):
    center = rows // 2
    places = jnp.stack(
        [(center + NCB - 1) % NCB, center, (center + 1) % NCB, (center + NCB // 2) % NCB], axis=-1
    )
    return lookup(agg_order, places)


def partial_kernel(p_ref, a_ref, x_ref, own_ref, prev_ref, next_ref, far_ref, scr):
    total = [None] * 6
    for i in range(BR):
        q = lax.dot_general(
            p_ref[i], a_ref[i], (((0,), (0,)), ((), ())), preferred_element_type=F32
        )
        local = i // 2
        for u in range(3):
            w = local + u
            value = q[u * BS : (u + 1) * BS]
            total[w] = value if total[w] is None else total[w] + value
            last = min(local, w) == min(3, w) and i % 2 == 1
            if last and w == 0:
                prev_ref[...] = total[w].astype(BF16)
            elif last and w == 5:
                next_ref[...] = total[w].astype(BF16)
            elif last:
                own_ref[w - 1] = total[w]
        if i % 2 == 0:
            far_ref[local] = q[3 * BS : 4 * BS].astype(BF16)
        scr[i] = q[4 * BS : 5 * BS]
    for octet in range(BS // 8):
        chunk = jnp.swapaxes(scr[:, octet * 8 : octet * 8 + 8, :], 0, 1)
        for e in range(8):
            j, pp = divmod(octet * 8 + e, PIECE)
            x_ref[j, :, pp * WIDE : (pp + 1) * WIDE] = chunk[e].astype(BF16)


def product_kernel(c_ref, r_ref, own_ref, prev_ref, next_ref, far_ref, p_ref, o_ref, x_ref, scr, held):
    for octet in range(BS // 8):
        rows = []
        for e in range(8):
            j, pp = divmod(octet * 8 + e, PIECE)
            rows.append(r_ref[j, :, pp * WIDE : (pp + 1) * WIDE].astype(F32))
        scr[:, octet * 8 : octet * 8 + 8, :] = jnp.swapaxes(jnp.stack(rows), 0, 1)
    for t in range(4):
        g = own_ref[t] + far_ref[t].astype(F32)
        if t == 0:
            g = g + prev_ref[...].astype(F32)
        if t == 3:
            g = g + next_ref[...].astype(F32)
        scr[t] = g + (scr[t] + scr[4 + t])
    for kk in range(KK):
        here = c_ref[0] == kk % 2
        right = jnp.where(here, p_ref[kk // 2], o_ref[kk // 2])[:, : USLOTS * BS]
        for t in range(4):
            g = scr[t, :, kk * BS : (kk + 1) * BS]
            high = g.astype(BF16)
            low = (g - high.astype(F32)).astype(BF16)
            out = jnp.dot(high, right, preferred_element_type=F32)
            out = out + jnp.dot(low, right, preferred_element_type=F32)
            span = slice(t * BS, (t + 1) * BS)
            x_ref[span, kk * WIDE : (kk + 1) * WIDE] = out[:, :WIDE].astype(BF16)
            if kk % 2 == 0:
                held[t] = out[:, WIDE:]
            else:
                sec = kk // 2
                cross = held[t] + out[:, WIDE:]
                x_ref[span, 4 * WIDE + sec * BS : 4 * WIDE + (sec + 1) * BS] = cross.astype(BF16)


def place_kernel(j_ref, r_ref, out_ref, acc):
    acc[...] = jnp.zeros_like(acc)

    def step(c, carry):
        for s in range(OUTSLOTS):
            at = j_ref[c, s]
            acc[at] += r_ref[c, :, s * BS : (s + 1) * BS].astype(F32)
        return carry

    lax.fori_loop(0, COLS, step, 0)
    for block in range(NCB):
        out_ref[:, block * BS : (block + 1) * BS] = acc[block]


VMEM = pl.BlockSpec(memory_space=pltpu.VMEM)
SMEM = pl.BlockSpec(memory_space=pltpu.SMEM)


def inner(a_blocks, a_mask, p_blocks, p_mask, section_owner, agg_order):
    area = a_blocks.shape[2]
    row, col = lax.axis_index("row"), lax.axis_index("col")
    rows = row * BR + jnp.arange(BR, dtype=jnp.int32)

    band = band_columns(rows, agg_order)
    cross = ((rows // 16 + 4) % COLS) * BR + rows % BR
    live = jnp.stack([jnp.ones_like(rows)] * 3 + [1 - rows % 2], axis=-1) > 0
    fresh = ~jnp.any((band == cross[:, None]) & live, axis=1)
    wanted = jnp.concatenate([band, cross[:, None]], axis=1)
    usable = jnp.concatenate([live, fresh[:, None]], axis=1)
    local = wanted[:, :, None] == col * BR + jnp.arange(BR, dtype=jnp.int32)
    pick = local & usable[:, :, None] & (p_mask[:, None, :] != 0)
    compact = jnp.einsum(
        "iuj,ijf->iuf", pick.astype(BF16), p_blocks, preferred_element_type=F32
    ).astype(BF16)

    sent = lax.all_to_all(
        compact.reshape(COLS, USLOTS * area // 128, 128), "col", 0, 0, tiled=True
    )
    tiles = (a_blocks * a_mask[:, :, None].astype(BF16)).reshape(BR, 2, COLS, area)
    got = []
    for d in range(COLS):
        piece = lax.dynamic_index_in_dim(tiles, (col + d) % COLS, 2, keepdims=False)
        piece = piece.reshape(2 * BR, area)
        got.append(shift(piece, "col", d) if d else piece)
    mine = jnp.sum(sent.astype(F32), axis=0).astype(BF16)
    mine = mine.reshape(USLOTS, BS, BS).transpose(1, 0, 2).reshape(BS, USLOTS * BS)
    mine = jnp.pad(mine, ((0, 0), (0, PW - USLOTS * BS)))
    p_rows = lax.all_to_all(jnp.broadcast_to(mine[None], (COLS, BS, PW)), "col", 0, 0, tiled=True)
    chosen = jnp.stack([mine, mine])
    for bit in range(3):
        moved = lax.ppermute(chosen, "row", [(r, r ^ (2 << bit)) for r in range(ROWS)])
        wrong = (((row // 2) ^ section_owner) >> bit) & 1
        chosen = jnp.where(wrong[:, None, None] == 1, moved, chosen)
    swapped = lax.ppermute(chosen, "row", [(r, r ^ 1) for r in range(ROWS)])

    parts = []
    for s in range(2):
        away = (col - section_owner[s]) % COLS
        kept = got[0]
        for d in range(1, COLS):
            kept = jnp.where(away == d, got[d], kept)
        parts.append(kept)
    a_part = jnp.stack(parts).reshape(2, BR, 2, BS, BS).transpose(1, 3, 0, 2, 4).reshape(BR, BS, WIDE)

    spread, own, prev_part, next_part, far_part = pl.pallas_call(
        partial_kernel,
        out_shape=(
            jax.ShapeDtypeStruct((ROWS, BR, LANES), BF16),
            jax.ShapeDtypeStruct((4, BS, WIDE), F32),
            jax.ShapeDtypeStruct((BS, WIDE), BF16),
            jax.ShapeDtypeStruct((BS, WIDE), BF16),
            jax.ShapeDtypeStruct((4, BS, WIDE), BF16),
        ),
        in_specs=[VMEM] * 2,
        out_specs=(VMEM,) * 5,
        scratch_shapes=[pltpu.VMEM((BR, BS, WIDE), F32)],
        name="partial",
    )(p_rows, a_part)
    spread = lax.all_to_all(spread, "row", 0, 0, tiled=True)
    from_next = shift(prev_part, "row", -1)
    from_prev = shift(next_part, "row", 1)
    from_far = shift(far_part, "row", ROWS // 2)

    row_id = jnp.arange(ROWS, dtype=jnp.int32)[:, None]
    source = ((row_id // 2 + 4) % COLS) * BR + jnp.arange(BR, dtype=jnp.int32)[None]
    home = agg_order.reshape(ROWS, 4)
    near = jnp.concatenate([home, home], axis=1)
    choose = near.reshape(-1)[:, None] == source.reshape(-1)[None]
    total = jnp.dot(
        choose.astype(BF16), spread.reshape(ROWS * BR, LANES), preferred_element_type=F32
    )
    high = lax.reduce_precision(total, 8, 7)
    is_low = (jnp.arange(ROWS * BR) % BR // 4 == 1)[:, None]
    back = jnp.where(is_low, total - high, high).astype(BF16).reshape(ROWS, BR, LANES)
    back = lax.all_to_all(back, "row", 0, 0, tiled=True)

    outs = pl.pallas_call(
        product_kernel,
        out_shape=jax.ShapeDtypeStruct((4 * BS, OUTSLOTS * BS), BF16),
        in_specs=[SMEM] + [VMEM] * 7,
        out_specs=VMEM,
        scratch_shapes=[pltpu.VMEM((BR, BS, WIDE), F32), pltpu.VMEM((4, BS, BS), F32)],
        name="product",
    )((row % 2)[None], back, own, from_prev, from_next, from_far, chosen, swapped)
    outs = lax.all_to_all(outs.reshape(COLS, 4 * BS // COLS, OUTSLOTS * BS), "col", 0, 0, tiled=True)

    k_col = jnp.arange(COLS, dtype=jnp.int32)[:, None, None]
    k_sec = section_owner[None, :, None]
    k_half = jnp.arange(2, dtype=jnp.int32)[None, None, :]
    k_rows = 2 * BR * k_sec + BR * k_half + k_col
    j_band = band_columns(k_rows, agg_order).reshape(COLS, 4 * KK)
    j_cross = ((k_sec + 4) % COLS)[:, :, 0] * BR + k_col[:, :, 0]
    j_table = jnp.concatenate([j_band, j_cross], axis=1)
    return pl.pallas_call(
        place_kernel,
        out_shape=jax.ShapeDtypeStruct((4 * BS // COLS, NCB * BS), F32),
        in_specs=[SMEM, VMEM],
        out_specs=VMEM,
        scratch_shapes=[pltpu.VMEM((NCB, 4 * BS // COLS, BS), F32)],
        name="place",
    )(j_table, outs)


def solution(mesh):
    in_specs = (
        P("row", "col", None),
        P("row", "col"),
        P("row", "col", None),
        P("row", "col"),
        P(),
        P(),
    )
    out_specs = P(("row", "col"), None)
    return jax.shard_map(inner, mesh=mesh, in_specs=in_specs, out_specs=out_specs, check_vma=False)
```

profile of v0, /device:TPU:0, one launch (start us, length us, event | category | flops | bytes accessed | tf_op | source)
XLA Modules:
  0.0 180.3 jit_solution(7496658280801873690)
XLA Ops:
  0.1 0.9 select_reduce_fusion.1
  1.5 0.7 broadcast_compare_fusion
  2.1 0.5 convolution_convert_fusion
  2.7 2.0 %reshape.690 = bf16[8,360,128]{2,1,0:T(8,128)(2,1)} reshape(bf16[8,5,9216]{2,1,0:T(8,128)(2,1)S(1)} %convolution_convert_fusion) | data formatting | bytes 1474560 | tf_op jit(solution)/shard_map/reshape | solution.py:139
  4.6 6.1 %all-to-all-start = ((bf16[8,360,128]{2,1,0:T(8,128)(2,1)}), bf16[8,360,128]{2,1,0:T(8,128)(2,1)}, u32[]{:S(2)}, u32[]{:S(2)}) async-start(bf16[8,360,128]{2,1,0:T(8,128)(2,1)} %reshape.690), calls=%async_computation | async-start | bytes 1474560 | tf_op jit(solution)/shard_map/all_to_all | solution.py:138
  10.8 1.9 %multiply_bitcast_fusion = bf16[8,2,8,9216]{3,2,1,0:T(8,128)(2,1)S(1)} fusion(bf16[8,16,9216]{2,1,0:T(8,128)(2,1)} %param.6, bf16[8,16]{1,0:T(8,128)(2,1)S(1)} %convert_element_type.17), kind=kLoop, calls=%fused_computation.1 | loop fusion | flops 1179648 | bytes 4718848 | tf_op jit(solution)/shard_map/reshape | solution.py:141
  12.7 17.0 %dynamic-slice_reduce_fusion = (bf16[8,2,9216]{2,1,0:T(2,128)(2,1)}, bf16[8,2,9216]{2,1,0:T(2,128)(2,1)}, bf16[8,2,9216]{2,1,0:T(2,128)(2,1)}, bf16[8,2,9216]{2,...) fusion(bf16[8,2,8,9216]{3,2,1,0:T(8,128)(2,1)S(1)} %multiply_bi, ...), kind=kLoop, calls=%fused_computation.8 | loop fusion | bytes 4718624 | tf_op jit(solution)/shard_map/jit(dynamic_index_in_dim)/dynamic_slice | solution.py:144
  29.7 1.9 %reshape.694 = bf16[16,9216]{1,0:T(8,128)(2,1)} reshape(bf16[8,2,9216]{2,1,0:T(2,128)(2,1)} %get-tuple-element.22) | data formatting | bytes 589824 | tf_op jit(solution)/shard_map/reshape | solution.py:145
  31.6 4.1 %collective-permute-start = (bf16[16,9216]{1,0:T(8,128)(2,1)}, bf16[16,9216]{1,0:T(8,128)(2,1)S(1)}, u32[]{:S(2)}, u32[]{:S(2)}) collective-permute-start(bf16[16,9216]{1,0:T(8,128)(2,1)} %reshape.694), channel_id=1, source_target_pairs={{0,7},{1,0},{2,1},{3,2},{4,3},{5,4},{6,5},{7,6},{8,15},{9,8},{10,9... | collective-permute-start | bytes 884744 | tf_op jit(solution)/shard_map/ppermute | solution.py:31
  35.7 1.8 %reshape.695 = bf16[16,9216]{1,0:T(8,128)(2,1)} reshape(bf16[8,2,9216]{2,1,0:T(2,128)(2,1)} %get-tuple-element.21) | data formatting | bytes 589824 | tf_op jit(solution)/shard_map/reshape | solution.py:145
  37.5 0.9 collective-permute-start.1
  38.4 0.8 reshape.696
  39.2 0.6 collective-permute-start.2
  39.8 0.8 reshape.697
  40.6 2.7 %collective-permute-start.3 = (bf16[16,9216]{1,0:T(8,128)(2,1)}, bf16[16,9216]{1,0:T(8,128)(2,1)S(1)}, u32[]{:S(2)}, u32[]{:S(2)}) collective-permute-start(bf16[16,9216]{1,0:T(8,128)(2,1)} %reshape.697), channel_id=1, source_target_pairs={{0,4},{1,5},{2,6},{3,7},{4,0},{5,1},{6,2},{7,3},{8,12},{9,13},{10,... | collective-permute-start | bytes 884744 | tf_op jit(solution)/shard_map/ppermute | solution.py:31
  43.3 0.8 reshape.698
  44.1 0.6 fusion.37
  46.1 0.8 reshape.699
  47.2 0.5 and_compare_fusion.2
  47.7 1.7 collective-permute-start.5
  49.4 11.3 %collective-permute-done.1 = bf16[16,9216]{1,0:T(8,128)(2,1)S(1)} collective-permute-done((bf16[16,9216]{1,0:T(8,128)(2,1)}, bf16[16,9216]{1,0:T(8,128)(2,1)S(1)}, u32[]{:S(2)}, u32[]{:S(2)}) %collective-permute-start.1) | collective-permute-done | bytes 294944 | tf_op jit(solution)/shard_map/ppermute | solution.py:31
  60.8 1.8 %collective-permute-done.4 = bf16[16,9216]{1,0:T(8,128)(2,1)S(1)} collective-permute-done((bf16[16,9216]{1,0:T(8,128)(2,1)}, bf16[16,9216]{1,0:T(8,128)(2,1)S(1)}, u32[]{:S(2)}, u32[]{:S(2)}) %collective-permute-start.4) | collective-permute-done | bytes 294944 | tf_op jit(solution)/shard_map/ppermute | solution.py:31
  62.6 5.2 %collective-permute-done.5 = bf16[16,9216]{1,0:T(8,128)(2,1)} collective-permute-done((bf16[16,9216]{1,0:T(8,128)(2,1)}, bf16[16,9216]{1,0:T(8,128)(2,1)}, u32[]{:S(2)}, u32[]{:S(2)}) %collective-permute-start.5) | collective-permute-done | bytes 294944 | tf_op jit(solution)/shard_map/ppermute | solution.py:31
  67.9 1.7 collective-permute-done.6
  69.5 0.7 copy-done.6
  70.3 0.8 select_select_fusion.1
  71.1 1.2 reduce_sum.32
  72.3 0.1 reshape.691
  72.5 0.1 copy.25
  72.8 0.7 pad_maximum_fusion
  73.5 1.5 collective-permute-start.10
  75.0 0.9 broadcast_in_dim.80
  75.9 4.4 %all-to-all-start.1 = ((bf16[8,96,512]{2,1,0:T(8,128)(2,1)}), bf16[8,96,512]{2,1,0:T(8,128)(2,1)S(1)}, u32[]{:S(2)}, u32[]{:S(2)}) async-start(bf16[8,96,512]{2,1,0:T(8,128)(2,1)} %broadcast_in_dim.80), calls=%async_computation.1 | async-start | bytes 1572864 | tf_op jit(solution)/shard_map/all_to_all | solution.py:150
  80.3 1.8 %select_select_fusion = bf16[16,9216]{1,0:T(8,128)(2,1)} fusion(bf16[16,9216]{1,0:T(8,128)(2,1)S(1)} %collective-permute-done, bf16[16,9216]{1,0:T(8,128)(2,1)S(1)} %collective-permute-done.1, bf16[16,9216]{1,0:T(8,128)(2,1)S(1)} %collective-permute-done.2, bf16[16,9216]{1,0:T(8,128)(2,1)} %copy-done.4, bf16[16,9216]{1,0:T(8,128)(2,1)} %copy-done.5, ...), kind=kLoop, calls=%fused_computation.16 | loop fusion | flops 1032192 | bytes 2654215 | tf_op jit(solution)/shard_map/jit(_where)/select_n | solution.py:163
  82.1 1.4 stack.17
  83.5 1.4 stack.36
  84.9 0.2 maximum_bitcast_fusion
  85.1 0.7 copy.35
  85.7 1.4 reshape.702.a_ref
  87.1 5.0 %all-to-all-done.1.p_ref = bf16[8,96,512]{2,1,0:T(8,128)(2,1)S(1)} async-done(((bf16[8,96,512]{2,1,0:T(8,128)(2,1)}), bf16[8,96,512]{2,1,0:T(8,128)(2,1)S(1)}, u32[]{:S(2)}, u32[]{:S(2)}) %all-to-all-start.1) | async-done | bytes 786464 | tf_op jit(solution)/shard_map/all_to_all | solution.py:150
  92.1 0.9 copy-done.2
  93.0 3.5 %partial.1 = (bf16[16,8,2304]{2,1,0:T(8,128)(2,1)}, f32[4,96,384]{2,1,0:T(8,128)}, bf16[96,384]{1,0:T(8,128)(2,1)}, bf16[96,384]{1,0:T(8,128)(2,1)}, bf16[4,96,384]{2,1,0:T(8,128)(2,1)}) custom-call(bf16[8,96,512]{2,1,0:T(8,128)(2,1)} %copy-done.2, bf16[8,96,384]{2,1,0:T(8,128)(2,1)} %reshape.702.a_ref), custom_call_target="tpu_custom_call" | custom-call | tf_op jit(solution)/shard_map/partial/pallas_call | solution.py:167
  96.5 7.3 %all-to-all-start.2 = ((bf16[16,8,2304]{2,1,0:T(8,128)(2,1)}), bf16[16,8,2304]{2,1,0:T(8,128)(2,1)S(1)}, u32[]{:S(2)}, u32[]{:S(2)}) async-start(bf16[16,8,2304]{2,1,0:T(8,128)(2,1)} %get-tuple-element.10), calls=%async_computation.2 | async-start | bytes 1179648 | tf_op jit(solution)/shard_map/all_to_all | solution.py:181
  103.8 1.0 broadcast_select_fusion
  104.8 3.5 %collective-permute-start.11 = (bf16[2,96,512]{2,1,0:T(8,128)(2,1)S(1)}, bf16[2,96,512]{2,1,0:T(8,128)(2,1)S(1)}, u32[]{:S(2)}, u32[]{:S(2)}) collective-permute-start(bf16[2,96,512]{2,1,0:T(8,128)(2,1)S(1)} %broadcast_select_fusion), channel_id=1, source_target_pairs={{0,32},{8,40},{16,48},{24,56},{32,0},{40,8},{48,16},{56,24},{64,96... | collective-permute-start | bytes 589832 | tf_op jit(solution)/shard_map/ppermute | solution.py:153
  108.6 10.3 %collective-permute-done.11 = bf16[2,96,512]{2,1,0:T(8,128)(2,1)S(1)} collective-permute-done((bf16[2,96,512]{2,1,0:T(8,128)(2,1)S(1)}, bf16[2,96,512]{2,1,0:T(8,128)(2,1)S(1)}, u32[]{:S(2)}, u32[]{:S(2)}) %collective-permute-start.11) | collective-permute-done | bytes 196640 | tf_op jit(solution)/shard_map/ppermute | solution.py:153
  118.9 1.0 broadcast_select_fusion.1
  119.9 3.1 %collective-permute-start.12 = (bf16[2,96,512]{2,1,0:T(8,128)(2,1)S(1)}, bf16[2,96,512]{2,1,0:T(8,128)(2,1)S(1)}, u32[]{:S(2)}, u32[]{:S(2)}) collective-permute-start(bf16[2,96,512]{2,1,0:T(8,128)(2,1)S(1)} %broadcast_select_fusion.1), channel_id=1, source_target_pairs={{0,64},{8,72},{16,80},{24,88},{32,96},{40,104},{48,112},{56,120},{... | collective-permute-start | bytes 589832 | tf_op jit(solution)/shard_map/ppermute | solution.py:153
  123.0 1.2 fusion.1
  124.2 3.7 %all-to-all-start.3 = ((bf16[16,8,2304]{2,1,0:T(8,128)(2,1)}), bf16[16,8,2304]{2,1,0:T(8,128)(2,1)S(1)}, u32[]{:S(2)}, u32[]{:S(2)}) async-start(bf16[16,8,2304]{2,1,0:T(8,128)(2,1)} %fusion.1), calls=%async_computation.3 | async-start | bytes 1179648 | tf_op jit(solution)/shard_map/all_to_all | solution.py:197
  127.9 3.4 %collective-permute-start.9 = (bf16[4,96,384]{2,1,0:T(8,128)(2,1)S(1)}, bf16[4,96,384]{2,1,0:T(8,128)(2,1)S(1)}, u32[]{:S(2)}, u32[]{:S(2)}) collective-permute-start(bf16[4,96,384]{2,1,0:T(8,128)(2,1)S(1)} %copy-done.26), channel_id=1, source_target_pairs={{0,64},{8,72},{16,80},{24,88},{32,96},{40,104},{48,112},{56,120},{... | collective-permute-start | bytes 884744 | tf_op jit(solution)/shard_map/ppermute | solution.py:31
  131.6 0.5 collective-permute-start.7
  132.1 4.9 %collective-permute-start.8 = (bf16[96,384]{1,0:T(8,128)(2,1)S(1)}, bf16[96,384]{1,0:T(8,128)(2,1)S(1)}, u32[]{:S(2)}, u32[]{:S(2)}) collective-permute-start(bf16[96,384]{1,0:T(8,128)(2,1)S(1)} %copy-done.27), channel_id=1, source_target_pairs={{0,120},{8,0},{16,8},{24,16},{32,24},{40,32},{48,40},{56,48},{64,5... | collective-permute-start | bytes 221192 | tf_op jit(solution)/shard_map/ppermute | solution.py:31
  137.0 4.7 %collective-permute-done.7.prev_ref = bf16[96,384]{1,0:T(8,128)(2,1)S(1)} collective-permute-done((bf16[96,384]{1,0:T(8,128)(2,1)S(1)}, bf16[96,384]{1,0:T(8,128)(2,1)S(1)}, u32[]{:S(2)}, u32[]{:S(2)}) %collective-permute-start.7) | collective-permute-done | bytes 73760 | tf_op jit(solution)/shard_map/ppermute | solution.py:31
  141.7 4.1 %collective-permute-done.9.far_ref = bf16[4,96,384]{2,1,0:T(8,128)(2,1)S(1)} collective-permute-done((bf16[4,96,384]{2,1,0:T(8,128)(2,1)S(1)}, bf16[4,96,384]{2,1,0:T(8,128)(2,1)S(1)}, u32[]{:S(2)}, u32[]{:S(2)}) %collective-permute-start.9) | collective-permute-done | bytes 294944 | tf_op jit(solution)/shard_map/ppermute | solution.py:31
  145.9 0.7 copy-done.14
  146.6 0.2 copy-done.3
  146.8 3.7 %product.1 = bf16[384,1728]{1,0:T(8,128)(2,1)} custom-call(s32[1]{0:T(128)} %bitcast.1.c_ref, bf16[16,8,2304]{2,1,0:T(8,128)(2,1)} %copy-done.3, f32[4,96,384]{2,1,0:T(8,128)} %get-tuple-element.11.own_ref, bf16[96,384]{1,0:T(8,128)(2,1)} %copy-done.16, bf16[96,384]{1,0:T(8,128)(2,1)} %copy-done.17, bf16[4,96,384]{2,1,0:T(8,128)(2,1)} %copy-done.14, ...), custom_call_target="tpu_custom_call" | custom-call | tf_op jit(solution)/shard_map/product/pallas_call | solution.py:199
  150.5 3.7 %all-to-all-start.4 = ((bf16[8,48,1728]{2,1,0:T(8,128)(2,1)}), bf16[8,48,1728]{2,1,0:T(8,128)(2,1)S(1)}, u32[]{:S(2)}, u32[]{:S(2)}) async-start(bf16[8,48,1728]{2,1,0:T(8,128)(2,1)} %bitcast.23), calls=%async_computation.4 | async-start | bytes 2752512 | tf_op jit(solution)/shard_map/all_to_all | solution.py:207
  154.5 0.4 select_reduce_fusion
  155.0 0.7 pad_add_fusion.2.j_ref
  155.7 19.4 %all-to-all-done.4.r_ref = bf16[8,48,1728]{2,1,0:T(8,128)(2,1)S(1)} async-done(((bf16[8,48,1728]{2,1,0:T(8,128)(2,1)}), bf16[8,48,1728]{2,1,0:T(8,128)(2,1)S(1)}, u32[]{:S(2)}, u32[]{:S(2)}) %all-to-all-start.4) | async-done | bytes 1327136 | tf_op jit(solution)/shard_map/all_to_all | solution.py:207
  175.1 1.1 copy-done.1
  176.2 4.1 %place.1 = f32[48,6144]{1,0:T(8,128)} custom-call(s32[8,18]{1,0:T(8,128)} %pad_add_fusion.2.j_ref, bf16[8,48,1728]{2,1,0:T(8,128)(2,1)} %copy-done.1), custom_call_target="tpu_custom_call" | custom-call | tf_op jit(solution)/shard_map/place/pallas_call | solution.py:216
  (101 shorter events, 1.8 us)
Async XLA Ops:
  0.0 2.1 %copy-start = (bf16[8,8,9216]{2,1,0:T(8,128)(2,1)S(1)}, bf16[8,8,9216]{2,1,0:T(8,128)(2,1)}, u32[]{:S(2)}) copy-start(bf16[8,8,9216]{2,1,0:T(8,128)(2,1)} %param.8) | copy-start | bytes 3538948
  4.6 6.1 %copy-start.23 = (s32[8,16]{1,0:T(8,128)S(1)}, s32[8,16]{1,0:T(8,128)}, u32[]{:S(2)}) copy-start(s32[8,16]{1,0:T(8,128)} %param.7) | copy-start | bytes 1540
  4.6 66.5 %all-to-all-start = ((bf16[8,360,128]{2,1,0:T(8,128)(2,1)}), bf16[8,360,128]{2,1,0:T(8,128)(2,1)}, u32[]{:S(2)}, u32[]{:S(2)}) async-start(bf16[8,360,128]{2,1,0:T(8,128)(2,1)} %reshape.690), calls=%async_computation | async-start | bytes 1474560 | tf_op jit(solution)/shard_map/all_to_all | solution.py:138
  29.7 8.7 %copy-start.12 = (bf16[8,2,9216]{2,1,0:T(2,128)(2,1)S(1)}, bf16[8,2,9216]{2,1,0:T(2,128)(2,1)}, u32[]{:S(2)}) copy-start(bf16[8,2,9216]{2,1,0:T(2,128)(2,1)} %get-tuple-element.20) | copy-start | bytes 884740
  29.7 10.1 %copy-start.11 = (bf16[8,2,9216]{2,1,0:T(2,128)(2,1)S(1)}, bf16[8,2,9216]{2,1,0:T(2,128)(2,1)}, u32[]{:S(2)}) copy-start(bf16[8,2,9216]{2,1,0:T(2,128)(2,1)} %get-tuple-element.19) | copy-start | bytes 884740
  29.7 13.6 %copy-start.10 = (bf16[8,2,9216]{2,1,0:T(2,128)(2,1)S(1)}, bf16[8,2,9216]{2,1,0:T(2,128)(2,1)}, u32[]{:S(2)}) copy-start(bf16[8,2,9216]{2,1,0:T(2,128)(2,1)} %get-tuple-element.18) | copy-start | bytes 884740
  31.6 16.1 %collective-permute-start = (bf16[16,9216]{1,0:T(8,128)(2,1)}, bf16[16,9216]{1,0:T(8,128)(2,1)S(1)}, u32[]{:S(2)}, u32[]{:S(2)}) collective-permute-start(bf16[16,9216]{1,0:T(8,128)(2,1)} %reshape.694), channel_id=1, source_target_pairs={{0,7},{1,0},{2,1},{3,2},{4,3},{5,4},{6,5},{7,6},{8,15},{9,8},{10,9... | collective-permute-start | bytes 884744 | tf_op jit(solution)/shard_map/ppermute | solution.py:31
  35.7 8.4 %copy-start.20 = (s32[2]{0:T(128)S(1)}, s32[2]{0:T(128)}, u32[]{:S(2)}) copy-start(s32[2]{0:T(128)} %param.10) | copy-start | bytes 28
  35.7 10.3 %copy-start.18 = (s32[64]{0:T(128)S(1)}, s32[64]{0:T(128)}, u32[]{:S(2)}) copy-start(s32[64]{0:T(128)} %param.11) | copy-start | bytes 772
  35.7 10.4 %copy-start.9 = (bf16[8,2,9216]{2,1,0:T(2,128)(2,1)S(1)}, bf16[8,2,9216]{2,1,0:T(2,128)(2,1)}, u32[]{:S(2)}) copy-start(bf16[8,2,9216]{2,1,0:T(2,128)(2,1)} %get-tuple-element.17) | copy-start | bytes 884740
  37.5 23.2 %collective-permute-start.1 = (bf16[16,9216]{1,0:T(8,128)(2,1)}, bf16[16,9216]{1,0:T(8,128)(2,1)S(1)}, u32[]{:S(2)}, u32[]{:S(2)}) collective-permute-start(bf16[16,9216]{1,0:T(8,128)(2,1)} %reshape.695), channel_id=1, source_target_pairs={{0,6},{1,7},{2,0},{3,1},{4,2},{5,3},{6,4},{7,5},{8,14},{9,15},{10,... | collective-permute-start | bytes 884744 | tf_op jit(solution)/shard_map/ppermute | solution.py:31
  38.4 8.5 %copy-start.8 = (bf16[8,2,9216]{2,1,0:T(2,128)(2,1)S(1)}, bf16[8,2,9216]{2,1,0:T(2,128)(2,1)}, u32[]{:S(2)}) copy-start(bf16[8,2,9216]{2,1,0:T(2,128)(2,1)} %get-tuple-element.16) | copy-start | bytes 884740
  39.2 21.6 %collective-permute-start.2 = (bf16[16,9216]{1,0:T(8,128)(2,1)}, bf16[16,9216]{1,0:T(8,128)(2,1)S(1)}, u32[]{:S(2)}, u32[]{:S(2)}) collective-permute-start(bf16[16,9216]{1,0:T(8,128)(2,1)} %reshape.696), channel_id=1, source_target_pairs={{0,5},{1,6},{2,7},{3,0},{4,1},{5,2},{6,3},{7,4},{8,13},{9,14},{10,... | collective-permute-start | bytes 884744 | tf_op jit(solution)/shard_map/ppermute | solution.py:31
  39.8 7.2 %copy-start.7 = (bf16[8,2,9216]{2,1,0:T(2,128)(2,1)S(1)}, bf16[8,2,9216]{2,1,0:T(2,128)(2,1)}, u32[]{:S(2)}) copy-start(bf16[8,2,9216]{2,1,0:T(2,128)(2,1)} %get-tuple-element.15) | copy-start | bytes 884740
  40.6 20.2 %collective-permute-start.3 = (bf16[16,9216]{1,0:T(8,128)(2,1)}, bf16[16,9216]{1,0:T(8,128)(2,1)S(1)}, u32[]{:S(2)}, u32[]{:S(2)}) collective-permute-start(bf16[16,9216]{1,0:T(8,128)(2,1)} %reshape.697), channel_id=1, source_target_pairs={{0,4},{1,5},{2,6},{3,7},{4,0},{5,1},{6,2},{7,3},{8,12},{9,13},{10,... | collective-permute-start | bytes 884744 | tf_op jit(solution)/shard_map/ppermute | solution.py:31
  44.1 18.5 %collective-permute-start.4 = (bf16[16,9216]{1,0:T(8,128)(2,1)}, bf16[16,9216]{1,0:T(8,128)(2,1)S(1)}, u32[]{:S(2)}, u32[]{:S(2)}) collective-permute-start(bf16[16,9216]{1,0:T(8,128)(2,1)} %reshape.698), channel_id=1, source_target_pairs={{0,3},{1,4},{2,5},{3,6},{4,7},{5,0},{6,1},{7,2},{8,11},{9,12},{10,... | collective-permute-start | bytes 884744 | tf_op jit(solution)/shard_map/ppermute | solution.py:31
  47.7 20.1 %collective-permute-start.5 = (bf16[16,9216]{1,0:T(8,128)(2,1)}, bf16[16,9216]{1,0:T(8,128)(2,1)}, u32[]{:S(2)}, u32[]{:S(2)}) collective-permute-start(bf16[16,9216]{1,0:T(8,128)(2,1)} %reshape.699), channel_id=1, source_target_pairs={{0,2},{1,3},{2,4},{3,5},{4,6},{5,7},{6,0},{7,1},{8,10},{9,11},{10,... | collective-permute-start | bytes 884744 | tf_op jit(solution)/shard_map/ppermute | solution.py:31
  60.7 8.8 %collective-permute-start.6 = (bf16[16,9216]{1,0:T(8,128)(2,1)S(1)}, bf16[16,9216]{1,0:T(8,128)(2,1)S(1)}, u32[]{:S(2)}, u32[]{:S(2)}) collective-permute-start(bf16[16,9216]{1,0:T(8,128)(2,1)S(1)} %reshape.700), channel_id=1, source_target_pairs={{0,1},{1,2},{2,3},{3,4},{4,5},{5,6},{6,7},{7,0},{8,9},{9,10},{10,1... | collective-permute-start | bytes 884744 | tf_op jit(solution)/shard_map/ppermute | solution.py:31
  60.8 11.8 %copy-start.4 = (bf16[16,9216]{1,0:T(8,128)(2,1)}, bf16[16,9216]{1,0:T(8,128)(2,1)S(1)}, u32[]{:S(2)}) copy-start(bf16[16,9216]{1,0:T(8,128)(2,1)S(1)} %collective-permute-done.3) | copy-start | bytes 884740
  62.6 8.5 %copy-start.5 = (bf16[16,9216]{1,0:T(8,128)(2,1)}, bf16[16,9216]{1,0:T(8,128)(2,1)S(1)}, u32[]{:S(2)}) copy-start(bf16[16,9216]{1,0:T(8,128)(2,1)S(1)} %collective-permute-done.4) | copy-start | bytes 884740
  69.5 0.7 copy-start.6
  73.5 30.3 %collective-permute-start.10 = (bf16[2,96,512]{2,1,0:T(8,128)(2,1)}, bf16[2,96,512]{2,1,0:T(8,128)(2,1)}, u32[]{:S(2)}, u32[]{:S(2)}) collective-permute-start(bf16[2,96,512]{2,1,0:T(8,128)(2,1)} %pad_maximum_fusion), channel_id=1, source_target_pairs={{0,16},{8,24},{16,0},{24,8},{32,48},{40,56},{48,32},{56,40},{64,80... | collective-permute-start | bytes 589832 | tf_op jit(solution)/shard_map/ppermute | solution.py:153
  75.9 16.2 %all-to-all-start.1 = ((bf16[8,96,512]{2,1,0:T(8,128)(2,1)}), bf16[8,96,512]{2,1,0:T(8,128)(2,1)S(1)}, u32[]{:S(2)}, u32[]{:S(2)}) async-start(bf16[8,96,512]{2,1,0:T(8,128)(2,1)} %broadcast_in_dim.80), calls=%async_computation.1 | async-start | bytes 1572864 | tf_op jit(solution)/shard_map/all_to_all | solution.py:150
  87.1 16.7 %copy-start.22 = (pred[2]{0:T(512)(128)(4,1)S(1)}, pred[2]{0:T(512)(128)(4,1)}, u32[]{:S(2)}) copy-start(pred[2]{0:T(512)(128)(4,1)} %get-tuple-element.33) | copy-start | bytes 10
  92.1 0.9 copy-start.2
  96.5 22.4 %copy-start.25 = (pred[2]{0:T(512)(128)(4,1)S(1)}, pred[2]{0:T(512)(128)(4,1)}, u32[]{:S(2)}) copy-start(pred[2]{0:T(512)(128)(4,1)} %get-tuple-element.32) | copy-start | bytes 10
  96.5 26.5 %all-to-all-start.2 = ((bf16[16,8,2304]{2,1,0:T(8,128)(2,1)}), bf16[16,8,2304]{2,1,0:T(8,128)(2,1)S(1)}, u32[]{:S(2)}, u32[]{:S(2)}) async-start(bf16[16,8,2304]{2,1,0:T(8,128)(2,1)} %get-tuple-element.10), calls=%async_computation.2 | async-start | bytes 1179648 | tf_op jit(solution)/shard_map/all_to_all | solution.py:181
  104.8 14.1 %collective-permute-start.11 = (bf16[2,96,512]{2,1,0:T(8,128)(2,1)S(1)}, bf16[2,96,512]{2,1,0:T(8,128)(2,1)S(1)}, u32[]{:S(2)}, u32[]{:S(2)}) collective-permute-start(bf16[2,96,512]{2,1,0:T(8,128)(2,1)S(1)} %broadcast_select_fusion), channel_id=1, source_target_pairs={{0,32},{8,40},{16,48},{24,56},{32,0},{40,8},{48,16},{56,24},{64,96... | collective-permute-start | bytes 589832 | tf_op jit(solution)/shard_map/ppermute | solution.py:153
  119.9 8.0 %copy-start.26 = (bf16[4,96,384]{2,1,0:T(8,128)(2,1)S(1)}, bf16[4,96,384]{2,1,0:T(8,128)(2,1)}, u32[]{:S(2)}) copy-start(bf16[4,96,384]{2,1,0:T(8,128)(2,1)} %get-tuple-element.14) | copy-start | bytes 884740
  119.9 11.4 %copy-start.24 = (pred[2]{0:T(512)(128)(4,1)S(1)}, pred[2]{0:T(512)(128)(4,1)}, u32[]{:S(2)}) copy-start(pred[2]{0:T(512)(128)(4,1)} %get-tuple-element.31) | copy-start | bytes 10
  119.9 11.4 %collective-permute-start.12 = (bf16[2,96,512]{2,1,0:T(8,128)(2,1)S(1)}, bf16[2,96,512]{2,1,0:T(8,128)(2,1)S(1)}, u32[]{:S(2)}, u32[]{:S(2)}) collective-permute-start(bf16[2,96,512]{2,1,0:T(8,128)(2,1)S(1)} %broadcast_select_fusion.1), channel_id=1, source_target_pairs={{0,64},{8,72},{16,80},{24,88},{32,96},{40,104},{48,112},{56,120},{... | collective-permute-start | bytes 589832 | tf_op jit(solution)/shard_map/ppermute | solution.py:153
  124.2 7.4 %copy-start.28 = (bf16[96,384]{1,0:T(8,128)(2,1)S(1)}, bf16[96,384]{1,0:T(8,128)(2,1)}, u32[]{:S(2)}) copy-start(bf16[96,384]{1,0:T(8,128)(2,1)} %get-tuple-element.12) | copy-start | bytes 221188
  124.2 7.9 %copy-start.27 = (bf16[96,384]{1,0:T(8,128)(2,1)S(1)}, bf16[96,384]{1,0:T(8,128)(2,1)}, u32[]{:S(2)}) copy-start(bf16[96,384]{1,0:T(8,128)(2,1)} %get-tuple-element.13) | copy-start | bytes 221188
  124.2 21.7 %all-to-all-start.3 = ((bf16[16,8,2304]{2,1,0:T(8,128)(2,1)}), bf16[16,8,2304]{2,1,0:T(8,128)(2,1)S(1)}, u32[]{:S(2)}, u32[]{:S(2)}) async-start(bf16[16,8,2304]{2,1,0:T(8,128)(2,1)} %fusion.1), calls=%async_computation.3 | async-start | bytes 1179648 | tf_op jit(solution)/shard_map/all_to_all | solution.py:197
  127.9 18.0 %collective-permute-start.9 = (bf16[4,96,384]{2,1,0:T(8,128)(2,1)S(1)}, bf16[4,96,384]{2,1,0:T(8,128)(2,1)S(1)}, u32[]{:S(2)}, u32[]{:S(2)}) collective-permute-start(bf16[4,96,384]{2,1,0:T(8,128)(2,1)S(1)} %copy-done.26), channel_id=1, source_target_pairs={{0,64},{8,72},{16,80},{24,88},{32,96},{40,104},{48,112},{56,120},{... | collective-permute-start | bytes 884744 | tf_op jit(solution)/shard_map/ppermute | solution.py:31
  131.4 14.4 %copy-start.13 = (bf16[2,96,512]{2,1,0:T(8,128)(2,1)}, bf16[2,96,512]{2,1,0:T(8,128)(2,1)S(1)}, u32[]{:S(2)}) copy-start(bf16[2,96,512]{2,1,0:T(8,128)(2,1)S(1)} %broadcast_select_fusion.2.p_ref) | copy-start | bytes 589828
  131.5 10.3 %collective-permute-start.13 = (bf16[2,96,512]{2,1,0:T(8,128)(2,1)S(1)}, bf16[2,96,512]{2,1,0:T(8,128)(2,1)S(1)}, u32[]{:S(2)}, u32[]{:S(2)}) collective-permute-start(bf16[2,96,512]{2,1,0:T(8,128)(2,1)S(1)} %broadcast_select_fusion.2.p_ref), channel_id=1, source_target_pairs={{0,8},{8,0},{16,24},{24,16},{32,40},{40,32},{48,56},{56,48},{64,72... | collective-permute-start | bytes 589832 | tf_op jit(solution)/shard_map/ppermute | solution.py:156
  131.6 10.1 %collective-permute-start.7 = (bf16[96,384]{1,0:T(8,128)(2,1)S(1)}, bf16[96,384]{1,0:T(8,128)(2,1)S(1)}, u32[]{:S(2)}, u32[]{:S(2)}) collective-permute-start(bf16[96,384]{1,0:T(8,128)(2,1)S(1)} %copy-done.28), channel_id=1, source_target_pairs={{0,8},{8,16},{16,24},{24,32},{32,40},{40,48},{48,56},{56,64},{64,7... | collective-permute-start | bytes 221192 | tf_op jit(solution)/shard_map/ppermute | solution.py:31
  132.1 9.7 %collective-permute-start.8 = (bf16[96,384]{1,0:T(8,128)(2,1)S(1)}, bf16[96,384]{1,0:T(8,128)(2,1)S(1)}, u32[]{:S(2)}, u32[]{:S(2)}) collective-permute-start(bf16[96,384]{1,0:T(8,128)(2,1)S(1)} %copy-done.27), channel_id=1, source_target_pairs={{0,120},{8,0},{16,8},{24,16},{32,24},{40,32},{48,40},{56,48},{64,5... | collective-permute-start | bytes 221192 | tf_op jit(solution)/shard_map/ppermute | solution.py:31
  141.7 4.2 %copy-start.16 = (bf16[96,384]{1,0:T(8,128)(2,1)}, bf16[96,384]{1,0:T(8,128)(2,1)S(1)}, u32[]{:S(2)}) copy-start(bf16[96,384]{1,0:T(8,128)(2,1)S(1)} %collective-permute-done.7.prev_ref) | copy-start | bytes 221188
  141.7 4.2 %copy-start.17 = (bf16[96,384]{1,0:T(8,128)(2,1)}, bf16[96,384]{1,0:T(8,128)(2,1)S(1)}, u32[]{:S(2)}) copy-start(bf16[96,384]{1,0:T(8,128)(2,1)S(1)} %collective-permute-done.8.next_ref) | copy-start | bytes 221188
  141.7 4.2 %copy-start.15 = (bf16[2,96,512]{2,1,0:T(8,128)(2,1)}, bf16[2,96,512]{2,1,0:T(8,128)(2,1)S(1)}, u32[]{:S(2)}) copy-start(bf16[2,96,512]{2,1,0:T(8,128)(2,1)S(1)} %collective-permute-done.13.o_ref) | copy-start | bytes 589828
  145.9 0.7 copy-start.14
  145.9 0.9 copy-start.3
  150.5 3.7 %copy-start.21 = (s32[2]{0:T(128)S(1)}, s32[2]{0:T(128)}, u32[]{:S(2)}) copy-start(s32[2]{0:T(128)} %param.10) | copy-start | bytes 28
  150.5 4.0 %copy-start.19 = (s32[64]{0:T(128)S(1)}, s32[64]{0:T(128)}, u32[]{:S(2)}) copy-start(s32[64]{0:T(128)} %param.11) | copy-start | bytes 772
  150.5 24.6 %all-to-all-start.4 = ((bf16[8,48,1728]{2,1,0:T(8,128)(2,1)}), bf16[8,48,1728]{2,1,0:T(8,128)(2,1)S(1)}, u32[]{:S(2)}, u32[]{:S(2)}) async-start(bf16[8,48,1728]{2,1,0:T(8,128)(2,1)} %bitcast.23), calls=%async_computation.4 | async-start | bytes 2752512 | tf_op jit(solution)/shard_map/all_to_all | solution.py:207
  175.1 1.1 copy-start.1
where the time goes:
time: 181 us; the launch traced here: 180 us
  waiting for transfers between devices  63.7 us (35%)
  starting transfers between devices  52.1 us (29%)
  local copies, waits for them, and re-layouts  37.2 us (21%)
  other arithmetic  12.6 us (7%)
  Pallas kernels  11.3 us (6%)
    ppermute x10, waiting for transfers between devices, shift(): lax.ppermute(value, axis, [(i, (i + by) % size) for i in range(size)])  28.9 us
    all_to_all x1, waiting for transfers between devices, inner(): lax.all_to_all(outs.reshape(COLS, 4 * BS // COLS, OUTSLOTS * BS), 'col',...  19.4 us
    ppermute x10, starting transfers between devices, shift(): lax.ppermute(value, axis, [(i, (i + by) % size) for i in range(size)])  18.8 us
    dynamic_slice x1, local copies, waits for them, and re-layouts, inner(): piece = lax.dynamic_index_in_dim(tiles, (col + d) % COLS, 2, keepdims=False)  17 us
    ppermute x3, waiting for transfers between devices, inner(): lax.ppermute(chosen, 'row', [(r, r ^ 2 << bit) for r in range(ROWS)])  10.3 us
    ppermute x3, starting transfers between devices, inner(): lax.ppermute(chosen, 'row', [(r, r ^ 2 << bit) for r in range(ROWS)])  8.05 us
    reshape x8, local copies, waits for them, and re-layouts, inner(): piece = piece.reshape(2 * BR, area)  7.26 us
    all_to_all x1, starting transfers between devices, inner(): spread = lax.all_to_all(spread, 'row', 0, 0, tiled=True)  7.26 us
  transfers between devices with their start and end apart: 19, of which 9 were waited for; matrix products, arithmetic and copies ran while one was open for 23% of the time, Pallas kernels for 2%

commit v1 on v0

--- a/solution.py
+++ b/solution.py
@@ -39,11 +39,32 @@
     return lookup(agg_order, places)
 
 
-def partial_kernel(p_ref, a_ref, x_ref, own_ref, prev_ref, next_ref, far_ref, scr):
+def partial_kernel(s_ref, p_ref, *refs):
+    got = refs[:COLS]
+    x_ref, own_ref, prev_ref, next_ref, far_ref, scr, buf, a_ref, sem = refs[COLS:]
+    for sec in range(2):
+        for d in range(COLS):
+
+            @pl.when(s_ref[sec] == d)
+            def _():
+                pltpu.make_async_copy(got[d], buf.at[sec], sem.at[sec]).start()
+
+    for sec in range(2):
+        pltpu.make_async_copy(got[0], buf.at[sec], sem.at[sec]).wait()
+    for octet in range(BS // 8):
+        for sec in range(2):
+            rows = []
+            for e in range(8):
+                at = (octet * 8 + e) * BS
+                rows.append(buf[sec, :, at : at + BS].astype(F32))
+            turned = jnp.swapaxes(jnp.stack(rows), 0, 1)
+            for row in range(2 * BR):
+                kk = 2 * sec + row % 2
+                a_ref[row // 2, octet * 8 : octet * 8 + 8, kk * BS : (kk + 1) * BS] = turned[row]
     total = [None] * 6
     for i in range(BR):
         q = lax.dot_general(
-            p_ref[i], a_ref[i], (((0,), (0,)), ((), ())), preferred_element_type=F32
+            p_ref[i], a_ref[i].astype(BF16), (((0,), (0,)), ((), ())), preferred_element_type=F32
         )
         local = i // 2
         for u in range(3):
@@ -138,11 +159,15 @@
     sent = lax.all_to_all(
         compact.reshape(COLS, USLOTS * area // 128, 128), "col", 0, 0, tiled=True
     )
-    tiles = (a_blocks * a_mask[:, :, None].astype(BF16)).reshape(BR, 2, COLS, area)
+    line = jnp.arange(COLS * 2 * BR, dtype=jnp.int32)
+    want = (line // 2) % BR * 2 * COLS + line % 2 * COLS + (col + line // (2 * BR)) % COLS
+    order = jnp.where(want[:, None] == line[None], a_mask.reshape(1, -1), 0)
+    tiles = jnp.dot(
+        order.astype(BF16), a_blocks.reshape(2 * BR * COLS, area), preferred_element_type=F32
+    ).astype(BF16)
     got = []
     for d in range(COLS):
-        piece = lax.dynamic_index_in_dim(tiles, (col + d) % COLS, 2, keepdims=False)
-        piece = piece.reshape(2 * BR, area)
+        piece = tiles[2 * BR * d : 2 * BR * (d + 1)]
         got.append(shift(piece, "col", d) if d else piece)
     mine = jnp.sum(sent.astype(F32), axis=0).astype(BF16)
     mine = mine.reshape(USLOTS, BS, BS).transpose(1, 0, 2).reshape(BS, USLOTS * BS)
@@ -155,15 +180,7 @@
         chosen = jnp.where(wrong[:, None, None] == 1, moved, chosen)
     swapped = lax.ppermute(chosen, "row", [(r, r ^ 1) for r in range(ROWS)])
 
-    parts = []
-    for s in range(2):
-        away = (col - section_owner[s]) % COLS
-        kept = got[0]
-        for d in range(1, COLS):
-            kept = jnp.where(away == d, got[d], kept)
-        parts.append(kept)
-    a_part = jnp.stack(parts).reshape(2, BR, 2, BS, BS).transpose(1, 3, 0, 2, 4).reshape(BR, BS, WIDE)
-
+    away = (col - section_owner) % COLS
     spread, own, prev_part, next_part, far_part = pl.pallas_call(
         partial_kernel,
         out_shape=(
@@ -173,11 +190,16 @@
             jax.ShapeDtypeStruct((BS, WIDE), BF16),
             jax.ShapeDtypeStruct((4, BS, WIDE), BF16),
         ),
-        in_specs=[VMEM] * 2,
+        in_specs=[SMEM, VMEM] + [pl.BlockSpec(memory_space=pl.ANY)] * COLS,
         out_specs=(VMEM,) * 5,
-        scratch_shapes=[pltpu.VMEM((BR, BS, WIDE), F32)],
+        scratch_shapes=[
+            pltpu.VMEM((BR, BS, WIDE), F32),
+            pltpu.VMEM((2, 2 * BR, area), BF16),
+            pltpu.VMEM((BR, BS, WIDE), F32),
+            pltpu.SemaphoreType.DMA((2,)),
+        ],
         name="partial",
-    )(p_rows, a_part)
+    )(away, p_rows, *got)
     spread = lax.all_to_all(spread, "row", 0, 0, tiled=True)
     from_next = shift(prev_part, "row", -1)
     from_prev = shift(next_part, "row", 1)

time: 181 us -> 155 us (0.86)
  local copies, waits for them, and re-layouts: 37.2 us -> 9.06 us
  starting transfers between devices: 52.1 us -> 73.1 us
  waiting for transfers between devices: 63.7 us -> 46.9 us
  other arithmetic: 12.6 us -> 7.33 us
  matrix products: 1.7 us -> 4.85 us
    dynamic_slice x1 -> x0, local copies, waits for them, and re-layouts: 17 us -> none  [inner(): piece = lax.dynamic_index_in_dim(tiles, (col + d) % COLS, 2, keepdims=False)]
    all_to_all x1, starting transfers between devices: 4.43 us -> 17.3 us  [inner(): lax.all_to_all(jnp.broadcast_to(mine[None], (COLS, BS, PW)), 'col', 0, 0,...]
    ppermute x10, waiting for transfers between devices: 28.9 us -> 16.1 us  [shift(): lax.ppermute(value, axis, [(i, (i + by) % size) for i in range(size)])]
    reshape x9 -> x0, local copies, waits for them, and re-layouts: 8.61 us -> none  [the longest x8 7.26 us: inner(): piece = piece.reshape(2 * BR, area)]
    ppermute x10, starting transfers between devices: 18.8 us -> 24.4 us  [shift(): lax.ppermute(value, axis, [(i, (i + by) % size) for i in range(size)])]
    all_to_all x1, waiting for transfers between devices: 5.05 us -> 0.01 us  [inner(): lax.all_to_all(jnp.broadcast_to(mine[None], (COLS, BS, PW)), 'col', 0, 0,...]
    another operation x3 -> x1, local copies, waits for them, and re-layouts: 2.72 us -> 0.01 us  [the longest x2 2.72 us: inner(): jnp.stack(parts).reshape(2, BR, 2, BS, BS).transpose(1, 3, 0, 2, 4)]
    all_to_all x1, starting transfers between devices: 3.7 us -> 6.36 us  [inner(): lax.all_to_all(outs.reshape(COLS, 4 * BS // COLS, OUTSLOTS * BS), 'col',...]
  transfers between devices with their start and end apart: 19 -> 19, of which waited for: 9 -> 7; matrix products, arithmetic and copies ran while one was open for 23% -> 8% of each run, Pallas kernels for 2% -> 3%
where the time goes in v1:
time: 155 us; the launch traced here: 154 us
  starting transfers between devices  73.1 us (47%)
  waiting for transfers between devices  46.9 us (30%)
  Pallas kernels  12.8 us (8%)
  local copies, waits for them, and re-layouts  9.06 us (6%)
  other arithmetic  7.33 us (5%)
  matrix products  4.85 us (3%)
    ppermute x10, starting transfers between devices, shift(): lax.ppermute(value, axis, [(i, (i + by) % size) for i in range(size)])  24.4 us
    all_to_all x1, waiting for transfers between devices, inner(): lax.all_to_all(outs.reshape(COLS, 4 * BS // COLS, OUTSLOTS * BS), 'col',...  19.1 us
    all_to_all x1, starting transfers between devices, inner(): lax.all_to_all(jnp.broadcast_to(mine[None], (COLS, BS, PW)), 'col', 0, 0,...  17.3 us
    ppermute x10, waiting for transfers between devices, shift(): lax.ppermute(value, axis, [(i, (i + by) % size) for i in range(size)])  16.1 us
    ppermute x3, waiting for transfers between devices, inner(): lax.ppermute(chosen, 'row', [(r, r ^ 2 << bit) for r in range(ROWS)])  11.3 us
    ppermute x3, starting transfers between devices, inner(): lax.ppermute(chosen, 'row', [(r, r ^ 2 << bit) for r in range(ROWS)])  8 us
    all_to_all x1, starting transfers between devices, inner(): spread = lax.all_to_all(spread, 'row', 0, 0, tiled=True)  7.47 us
    all_to_all x1, starting transfers between devices, inner(): lax.all_to_all(outs.reshape(COLS, 4 * BS // COLS, OUTSLOTS * BS), 'col',...  6.36 us
  transfers between devices with their start and end apart: 19, of which 7 were waited for; matrix products, arithmetic and copies ran while one was open for 8% of the time, Pallas kernels for 3%

profile of v1, /device:TPU:0, one launch (start us, length us, event | category | flops | bytes accessed | tf_op | source)
XLA Modules:
  0.0 154.3 jit_solution(12946218851029260677)
XLA Ops:
  0.1 1.0 select_reduce_fusion.1
  1.2 0.1 copy.14
  1.2 0.7 broadcast_compare_fusion
  1.9 0.1 pad.10.clone
  2.0 0.1 and_reduce_fusion
  2.1 0.1 copy.15
  2.2 1.8 %convolution_convert_fusion.1 = bf16[8,5,9216]{2,1,0:T(8,128)(2,1)S(1)} fusion(bf16[8,8,9216]{2,1,0:T(8,128)(2,1)} %param.8, s32[8]{0:T(128)S(1)} %iota_add_fusion.2, s32[8,5]{1,0:T(8,128)S(1)} %copy.14, pred[8,8]{1,0:T(8,128)(4,1)S(1)} %broadcast_compare_fusion, pred[8,5]{1,0:T(8,128)(4,1)S(1)} %copy.15), kind=kOutput, calls=%fused_computation.1 | convolution fusion | flops 6267840 | bytes 1917224 | tf_op jit(solution)/shard_map/iuj,ijf->iuf/dot_general | solution.py:155
  4.0 2.0 %reshape.705 = bf16[8,360,128]{2,1,0:T(8,128)(2,1)} reshape(bf16[8,5,9216]{2,1,0:T(8,128)(2,1)S(1)} %convolution_convert_fusion.1) | data formatting | bytes 1474560 | tf_op jit(solution)/shard_map/reshape | solution.py:160
  6.0 5.9 %all-to-all-start = ((bf16[8,360,128]{2,1,0:T(8,128)(2,1)}), bf16[8,360,128]{2,1,0:T(8,128)(2,1)S(1)}, u32[]{:S(2)}, u32[]{:S(2)}) async-start(bf16[8,360,128]{2,1,0:T(8,128)(2,1)} %reshape.705), calls=%async_computation | async-start | bytes 1474560 | tf_op jit(solution)/shard_map/all_to_all | solution.py:159
  12.0 0.1 broadcast_in_dim.96
  12.0 0.8 convolution_convert_fusion
  12.9 1.3 fusion.49
  14.2 2.0 %collective-permute-start = (bf16[16,9216]{1,0:T(8,128)(2,1)}, bf16[16,9216]{1,0:T(8,128)(2,1)}, u32[]{:S(2)}, u32[]{:S(2)}) collective-permute-start(bf16[16,9216]{1,0:T(8,128)(2,1)} %get-tuple-element.23), channel_id=1, source_target_pairs={{0,1},{1,2},{2,3},{3,4},{4,5},{5,6},{6,7},{7,0},{8,9},{9,10},{10,1... | collective-permute-start | bytes 884744 | tf_op jit(solution)/shard_map/ppermute | solution.py:31
  16.2 1.5 collective-permute-start.1
  17.7 2.1 %collective-permute-start.2 = (bf16[16,9216]{1,0:T(8,128)(2,1)S(1)}, bf16[16,9216]{1,0:T(8,128)(2,1)}, u32[]{:S(2)}, u32[]{:S(2)}) collective-permute-start(bf16[16,9216]{1,0:T(8,128)(2,1)S(1)} %get-tuple-element.21), channel_id=1, source_target_pairs={{0,3},{1,4},{2,5},{3,6},{4,7},{5,0},{6,1},{7,2},{8,11},{9,12},{10,... | collective-permute-start | bytes 884744 | tf_op jit(solution)/shard_map/ppermute | solution.py:31
  19.7 2.1 %collective-permute-start.3 = (bf16[16,9216]{1,0:T(8,128)(2,1)}, bf16[16,9216]{1,0:T(8,128)(2,1)}, u32[]{:S(2)}, u32[]{:S(2)}) collective-permute-start(bf16[16,9216]{1,0:T(8,128)(2,1)} %get-tuple-element.20), channel_id=1, source_target_pairs={{0,4},{1,5},{2,6},{3,7},{4,0},{5,1},{6,2},{7,3},{8,12},{9,13},{10,... | collective-permute-start | bytes 884744 | tf_op jit(solution)/shard_map/ppermute | solution.py:31
  21.8 3.0 %collective-permute-start.4 = (bf16[16,9216]{1,0:T(8,128)(2,1)}, bf16[16,9216]{1,0:T(8,128)(2,1)}, u32[]{:S(2)}, u32[]{:S(2)}) collective-permute-start(bf16[16,9216]{1,0:T(8,128)(2,1)} %get-tuple-element.19), channel_id=1, source_target_pairs={{0,5},{1,6},{2,7},{3,0},{4,1},{5,2},{6,3},{7,4},{8,13},{9,14},{10,... | collective-permute-start | bytes 884744 | tf_op jit(solution)/shard_map/ppermute | solution.py:31
  24.8 0.4 all-to-all-done
  25.1 0.1 reduce_sum.32
  25.3 0.1 reshape.706
  25.4 0.1 copy.16
  25.5 0.1 copy.17
  25.7 0.9 broadcast_in_dim.95
  26.6 17.3 %all-to-all-start.1 = ((bf16[8,96,512]{2,1,0:T(8,128)(2,1)}), bf16[8,96,512]{2,1,0:T(8,128)(2,1)S(1)}, u32[]{:S(2)}, u32[]{:S(2)}) async-start(bf16[8,96,512]{2,1,0:T(8,128)(2,1)} %broadcast_in_dim.95), calls=%async_computation.1 | async-start | bytes 1572864 | tf_op jit(solution)/shard_map/all_to_all | solution.py:175
  44.0 0.7 reshape.704
  44.7 0.7 add.532
  45.4 1.2 and_select_fusion.20
  46.6 3.2 %collective-permute-start.5 = (bf16[16,9216]{1,0:T(8,128)(2,1)}, bf16[16,9216]{1,0:T(8,128)(2,1)S(1)}, u32[]{:S(2)}, u32[]{:S(2)}) collective-permute-start(bf16[16,9216]{1,0:T(8,128)(2,1)} %get-tuple-element.18), channel_id=1, source_target_pairs={{0,6},{1,7},{2,0},{3,1},{4,2},{5,3},{6,4},{7,5},{8,14},{9,15},{10,... | collective-permute-start | bytes 884744 | tf_op jit(solution)/shard_map/ppermute | solution.py:31
  49.8 1.8 %collective-permute-start.6 = (bf16[16,9216]{1,0:T(8,128)(2,1)}, bf16[16,9216]{1,0:T(8,128)(2,1)}, u32[]{:S(2)}, u32[]{:S(2)}) collective-permute-start(bf16[16,9216]{1,0:T(8,128)(2,1)} %get-tuple-element.17), channel_id=1, source_target_pairs={{0,7},{1,0},{2,1},{3,2},{4,3},{5,4},{6,5},{7,6},{8,15},{9,8},{10,9... | collective-permute-start | bytes 884744 | tf_op jit(solution)/shard_map/ppermute | solution.py:31
  51.6 0.7 pad_maximum_fusion
  52.3 1.5 collective-permute-start.10
  53.8 0.7 and_compare_fusion.2
  54.4 6.3 %collective-permute-done.5.refs_6_ = bf16[16,9216]{1,0:T(8,128)(2,1)S(1)} collective-permute-done((bf16[16,9216]{1,0:T(8,128)(2,1)}, bf16[16,9216]{1,0:T(8,128)(2,1)S(1)}, u32[]{:S(2)}, u32[]{:S(2)}) %collective-permute-start.5) | collective-permute-done | bytes 294944 | tf_op jit(solution)/shard_map/ppermute | solution.py:31
  60.7 0.7 copy-done.5
  61.5 1.9 %collective-permute-done.6.refs_7_ = bf16[16,9216]{1,0:T(8,128)(2,1)} collective-permute-done((bf16[16,9216]{1,0:T(8,128)(2,1)}, bf16[16,9216]{1,0:T(8,128)(2,1)}, u32[]{:S(2)}, u32[]{:S(2)}) %collective-permute-start.6) | collective-permute-done | bytes 294944 | tf_op jit(solution)/shard_map/ppermute | solution.py:31
  63.3 0.9 copy-done.1
  64.2 5.0 %partial.1 = (bf16[16,8,2304]{2,1,0:T(8,128)(2,1)}, f32[4,96,384]{2,1,0:T(8,128)}, bf16[96,384]{1,0:T(8,128)(2,1)}, bf16[96,384]{1,0:T(8,128)(2,1)}, bf16[4,96,384]{2,1,0:T(8,128)(2,1)}) custom-call(s32[2]{0:T(128)} %get-tuple-element.34.s_ref, bf16[8,96,512]{2,1,0:T(8,128)(2,1)} %copy-done.1, bf16[16,9216]{1,0:T(8,128)(2,1)} %get-tuple-element.24.refs_0_, ...), custom_call_target="tpu_custom_call" | custom-call | tf_op jit(solution)/shard_map/partial/pallas_call | solution.py:184
  69.3 7.5 %all-to-all-start.2 = ((bf16[16,8,2304]{2,1,0:T(8,128)(2,1)}), bf16[16,8,2304]{2,1,0:T(8,128)(2,1)}, u32[]{:S(2)}, u32[]{:S(2)}) async-start(bf16[16,8,2304]{2,1,0:T(8,128)(2,1)} %get-tuple-element.10), calls=%async_computation.2 | async-start | bytes 1179648 | tf_op jit(solution)/shard_map/all_to_all | solution.py:203
  76.8 0.1 broadcast_select_fusion
  76.8 3.5 %collective-permute-start.11 = (bf16[2,96,512]{2,1,0:T(8,128)(2,1)S(1)}, bf16[2,96,512]{2,1,0:T(8,128)(2,1)S(1)}, u32[]{:S(2)}, u32[]{:S(2)}) collective-permute-start(bf16[2,96,512]{2,1,0:T(8,128)(2,1)S(1)} %broadcast_select_fusion), channel_id=1, source_target_pairs={{0,32},{8,40},{16,48},{24,56},{32,0},{40,8},{48,16},{56,24},{64,96... | collective-permute-start | bytes 589832 | tf_op jit(solution)/shard_map/ppermute | solution.py:178
  80.3 0.1 pad_add_fusion.1
  80.4 0.1 eq.123
  80.5 11.3 %collective-permute-done.11 = bf16[2,96,512]{2,1,0:T(8,128)(2,1)S(1)} collective-permute-done((bf16[2,96,512]{2,1,0:T(8,128)(2,1)S(1)}, bf16[2,96,512]{2,1,0:T(8,128)(2,1)S(1)}, u32[]{:S(2)}, u32[]{:S(2)}) %collective-permute-start.11) | collective-permute-done | bytes 196640 | tf_op jit(solution)/shard_map/ppermute | solution.py:178
  91.8 0.1 broadcast_select_fusion.1
  91.9 3.1 %collective-permute-start.12 = (bf16[2,96,512]{2,1,0:T(8,128)(2,1)S(1)}, bf16[2,96,512]{2,1,0:T(8,128)(2,1)}, u32[]{:S(2)}, u32[]{:S(2)}) collective-permute-start(bf16[2,96,512]{2,1,0:T(8,128)(2,1)S(1)} %broadcast_select_fusion.1), channel_id=1, source_target_pairs={{0,64},{8,72},{16,80},{24,88},{32,96},{40,104},{48,112},{56,120},{... | collective-permute-start | bytes 589832 | tf_op jit(solution)/shard_map/ppermute | solution.py:178
  95.0 2.2 %fusion.1 = bf16[16,8,2304]{2,1,0:T(8,128)(2,1)} fusion(bf16[16,8,2304]{2,1,0:T(8,128)(2,1)} %all-to-all-done.2, pred[128]{0:T(512)(128)(4,1)S(1)} %fusion.47, s32[128]{0:T(128)S(1)} %copy-done.10, s32[128]{0:T(128)S(1)} %eq.123), kind=kOutput, calls=%fused_computation.4 | convolution fusion | flops 76693504 | bytes 1180800 | tf_op jit(solution)/shard_map/dot_general | solution.py:213
  97.2 3.6 %all-to-all-start.3 = ((bf16[16,8,2304]{2,1,0:T(8,128)(2,1)}), bf16[16,8,2304]{2,1,0:T(8,128)(2,1)S(1)}, u32[]{:S(2)}, u32[]{:S(2)}) async-start(bf16[16,8,2304]{2,1,0:T(8,128)(2,1)} %fusion.1), calls=%async_computation.3 | async-start | bytes 1179648 | tf_op jit(solution)/shard_map/all_to_all | solution.py:219
  100.8 3.4 %collective-permute-start.9 = (bf16[4,96,384]{2,1,0:T(8,128)(2,1)}, bf16[4,96,384]{2,1,0:T(8,128)(2,1)S(1)}, u32[]{:S(2)}, u32[]{:S(2)}) collective-permute-start(bf16[4,96,384]{2,1,0:T(8,128)(2,1)} %get-tuple-element.14), channel_id=1, source_target_pairs={{0,64},{8,72},{16,80},{24,88},{32,96},{40,104},{48,112},{56,120},{... | collective-permute-start | bytes 884744 | tf_op jit(solution)/shard_map/ppermute | solution.py:31
  104.2 1.1 broadcast_select_fusion.2.p_ref
  105.3 0.1 collective-permute-start.13
  105.4 0.5 collective-permute-start.7
  105.9 4.9 %collective-permute-start.8 = (bf16[96,384]{1,0:T(8,128)(2,1)}, bf16[96,384]{1,0:T(8,128)(2,1)}, u32[]{:S(2)}, u32[]{:S(2)}) collective-permute-start(bf16[96,384]{1,0:T(8,128)(2,1)} %get-tuple-element.13), channel_id=1, source_target_pairs={{0,120},{8,0},{16,8},{24,16},{32,24},{40,32},{48,40},{56,48},{64,5... | collective-permute-start | bytes 221192 | tf_op jit(solution)/shard_map/ppermute | solution.py:31
  110.8 3.8 %collective-permute-done.7.prev_ref = bf16[96,384]{1,0:T(8,128)(2,1)S(1)} collective-permute-done((bf16[96,384]{1,0:T(8,128)(2,1)}, bf16[96,384]{1,0:T(8,128)(2,1)S(1)}, u32[]{:S(2)}, u32[]{:S(2)}) %collective-permute-start.7) | collective-permute-done | bytes 73760 | tf_op jit(solution)/shard_map/ppermute | solution.py:31
  114.6 4.2 %collective-permute-done.9.far_ref = bf16[4,96,384]{2,1,0:T(8,128)(2,1)S(1)} collective-permute-done((bf16[4,96,384]{2,1,0:T(8,128)(2,1)}, bf16[4,96,384]{2,1,0:T(8,128)(2,1)S(1)}, u32[]{:S(2)}, u32[]{:S(2)}) %collective-permute-start.9) | collective-permute-done | bytes 294944 | tf_op jit(solution)/shard_map/ppermute | solution.py:31
  118.8 0.7 copy-done.6
  119.5 0.2 copy-done.2
  119.7 3.7 %product.1 = bf16[384,1728]{1,0:T(8,128)(2,1)} custom-call(s32[1]{0:T(128)} %bitcast.1.c_ref, bf16[16,8,2304]{2,1,0:T(8,128)(2,1)} %copy-done.2, f32[4,96,384]{2,1,0:T(8,128)} %get-tuple-element.11.own_ref, bf16[96,384]{1,0:T(8,128)(2,1)} %copy-done.7, bf16[96,384]{1,0:T(8,128)(2,1)} %collective-permute-done.8.next_ref, bf16[4,96,384]{2,1,0:T(8,128)(2,1)} %copy-done.6, ...), custom_call_target="tpu_custom_call" | custom-call | tf_op jit(solution)/shard_map/product/pallas_call | solution.py:221
  123.4 6.4 %all-to-all-start.4 = ((bf16[8,48,1728]{2,1,0:T(8,128)(2,1)}), bf16[8,48,1728]{2,1,0:T(8,128)(2,1)}, u32[]{:S(2)}, u32[]{:S(2)}) async-start(bf16[8,48,1728]{2,1,0:T(8,128)(2,1)} %bitcast.20), calls=%async_computation.4 | async-start | bytes 2752512 | tf_op jit(solution)/shard_map/all_to_all | solution.py:229
  129.7 0.1 broadcast_add_fusion
  129.8 0.1 and_select_fusion.2
  129.9 0.4 select_reduce_fusion
  130.5 0.7 pad_add_fusion.2.j_ref
  131.1 19.1 %all-to-all-done.4.r_ref = bf16[8,48,1728]{2,1,0:T(8,128)(2,1)} async-done(((bf16[8,48,1728]{2,1,0:T(8,128)(2,1)}), bf16[8,48,1728]{2,1,0:T(8,128)(2,1)}, u32[]{:S(2)}, u32[]{:S(2)}) %all-to-all-start.4) | async-done | bytes 1327136 | tf_op jit(solution)/shard_map/all_to_all | solution.py:229
  150.2 4.1 %place.1 = f32[48,6144]{1,0:T(8,128)} custom-call(s32[8,18]{1,0:T(8,128)} %pad_add_fusion.2.j_ref, bf16[8,48,1728]{2,1,0:T(8,128)(2,1)} %all-to-all-done.4.r_ref), custom_call_target="tpu_custom_call" | custom-call | tf_op jit(solution)/shard_map/place/pallas_call | solution.py:238
  (50 shorter events, 0.4 us)
Async XLA Ops:
  0.0 12.0 %copy-start = (bf16[8,16,9216]{2,1,0:T(8,128)(2,1)S(1)}, bf16[8,16,9216]{2,1,0:T(8,128)(2,1)}, u32[]{:S(2)}) copy-start(bf16[8,16,9216]{2,1,0:T(8,128)(2,1)} %param.6) | copy-start | bytes 7077892
  4.0 7.9 %copy-start.9 = (s32[8,16]{1,0:T(8,128)S(1)}, s32[8,16]{1,0:T(8,128)}, u32[]{:S(2)}) copy-start(s32[8,16]{1,0:T(8,128)} %param.7) | copy-start | bytes 1540
  6.0 19.2 %all-to-all-start = ((bf16[8,360,128]{2,1,0:T(8,128)(2,1)}), bf16[8,360,128]{2,1,0:T(8,128)(2,1)S(1)}, u32[]{:S(2)}, u32[]{:S(2)}) async-start(bf16[8,360,128]{2,1,0:T(8,128)(2,1)} %reshape.705), calls=%async_computation | async-start | bytes 1474560 | tf_op jit(solution)/shard_map/all_to_all | solution.py:159
  14.2 32.4 %collective-permute-start = (bf16[16,9216]{1,0:T(8,128)(2,1)}, bf16[16,9216]{1,0:T(8,128)(2,1)}, u32[]{:S(2)}, u32[]{:S(2)}) collective-permute-start(bf16[16,9216]{1,0:T(8,128)(2,1)} %get-tuple-element.23), channel_id=1, source_target_pairs={{0,1},{1,2},{2,3},{3,4},{4,5},{5,6},{6,7},{7,0},{8,9},{9,10},{10,1... | collective-permute-start | bytes 884744 | tf_op jit(solution)/shard_map/ppermute | solution.py:31
  16.2 33.6 %collective-permute-start.1 = (bf16[16,9216]{1,0:T(8,128)(2,1)}, bf16[16,9216]{1,0:T(8,128)(2,1)}, u32[]{:S(2)}, u32[]{:S(2)}) collective-permute-start(bf16[16,9216]{1,0:T(8,128)(2,1)} %get-tuple-element.22), channel_id=1, source_target_pairs={{0,2},{1,3},{2,4},{3,5},{4,6},{5,7},{6,0},{7,1},{8,10},{9,11},{10,... | collective-permute-start | bytes 884744 | tf_op jit(solution)/shard_map/ppermute | solution.py:31
  17.7 34.6 %collective-permute-start.2 = (bf16[16,9216]{1,0:T(8,128)(2,1)S(1)}, bf16[16,9216]{1,0:T(8,128)(2,1)}, u32[]{:S(2)}, u32[]{:S(2)}) collective-permute-start(bf16[16,9216]{1,0:T(8,128)(2,1)S(1)} %get-tuple-element.21), channel_id=1, source_target_pairs={{0,3},{1,4},{2,5},{3,6},{4,7},{5,0},{6,1},{7,2},{8,11},{9,12},{10,... | collective-permute-start | bytes 884744 | tf_op jit(solution)/shard_map/ppermute | solution.py:31
  19.7 34.7 %collective-permute-start.3 = (bf16[16,9216]{1,0:T(8,128)(2,1)}, bf16[16,9216]{1,0:T(8,128)(2,1)}, u32[]{:S(2)}, u32[]{:S(2)}) collective-permute-start(bf16[16,9216]{1,0:T(8,128)(2,1)} %get-tuple-element.20), channel_id=1, source_target_pairs={{0,4},{1,5},{2,6},{3,7},{4,0},{5,1},{6,2},{7,3},{8,12},{9,13},{10,... | collective-permute-start | bytes 884744 | tf_op jit(solution)/shard_map/ppermute | solution.py:31
  21.8 32.6 %collective-permute-start.4 = (bf16[16,9216]{1,0:T(8,128)(2,1)}, bf16[16,9216]{1,0:T(8,128)(2,1)}, u32[]{:S(2)}, u32[]{:S(2)}) collective-permute-start(bf16[16,9216]{1,0:T(8,128)(2,1)} %get-tuple-element.19), channel_id=1, source_target_pairs={{0,5},{1,6},{2,7},{3,0},{4,1},{5,2},{6,3},{7,4},{8,13},{9,14},{10,... | collective-permute-start | bytes 884744 | tf_op jit(solution)/shard_map/ppermute | solution.py:31
  26.6 36.7 %all-to-all-start.1 = ((bf16[8,96,512]{2,1,0:T(8,128)(2,1)}), bf16[8,96,512]{2,1,0:T(8,128)(2,1)S(1)}, u32[]{:S(2)}, u32[]{:S(2)}) async-start(bf16[8,96,512]{2,1,0:T(8,128)(2,1)} %broadcast_in_dim.95), calls=%async_computation.1 | async-start | bytes 1572864 | tf_op jit(solution)/shard_map/all_to_all | solution.py:175
  46.6 14.2 %collective-permute-start.5 = (bf16[16,9216]{1,0:T(8,128)(2,1)}, bf16[16,9216]{1,0:T(8,128)(2,1)S(1)}, u32[]{:S(2)}, u32[]{:S(2)}) collective-permute-start(bf16[16,9216]{1,0:T(8,128)(2,1)} %get-tuple-element.18), channel_id=1, source_target_pairs={{0,6},{1,7},{2,0},{3,1},{4,2},{5,3},{6,4},{7,5},{8,14},{9,15},{10,... | collective-permute-start | bytes 884744 | tf_op jit(solution)/shard_map/ppermute | solution.py:31
  49.8 13.5 %collective-permute-start.6 = (bf16[16,9216]{1,0:T(8,128)(2,1)}, bf16[16,9216]{1,0:T(8,128)(2,1)}, u32[]{:S(2)}, u32[]{:S(2)}) collective-permute-start(bf16[16,9216]{1,0:T(8,128)(2,1)} %get-tuple-element.17), channel_id=1, source_target_pairs={{0,7},{1,0},{2,1},{3,2},{4,3},{5,4},{6,5},{7,6},{8,15},{9,8},{10,9... | collective-permute-start | bytes 884744 | tf_op jit(solution)/shard_map/ppermute | solution.py:31
  52.3 24.5 %collective-permute-start.10 = (bf16[2,96,512]{2,1,0:T(8,128)(2,1)}, bf16[2,96,512]{2,1,0:T(8,128)(2,1)S(1)}, u32[]{:S(2)}, u32[]{:S(2)}) collective-permute-start(bf16[2,96,512]{2,1,0:T(8,128)(2,1)} %pad_maximum_fusion), channel_id=1, source_target_pairs={{0,16},{8,24},{16,0},{24,8},{32,48},{40,56},{48,32},{56,40},{64,80... | collective-permute-start | bytes 589832 | tf_op jit(solution)/shard_map/ppermute | solution.py:178
  60.7 0.7 copy-start.5
  63.3 0.9 copy-start.1
  69.3 25.7 %copy-start.10 = (s32[128]{0:T(128)S(1)}, s32[128]{0:T(128)}, u32[]{:S(2)}) copy-start(s32[128]{0:T(128)} %add.532) | copy-start | bytes 1540
  69.3 25.7 %all-to-all-start.2 = ((bf16[16,8,2304]{2,1,0:T(8,128)(2,1)}), bf16[16,8,2304]{2,1,0:T(8,128)(2,1)}, u32[]{:S(2)}, u32[]{:S(2)}) async-start(bf16[16,8,2304]{2,1,0:T(8,128)(2,1)} %get-tuple-element.10), calls=%async_computation.2 | async-start | bytes 1179648 | tf_op jit(solution)/shard_map/all_to_all | solution.py:203
  76.8 15.0 %collective-permute-start.11 = (bf16[2,96,512]{2,1,0:T(8,128)(2,1)S(1)}, bf16[2,96,512]{2,1,0:T(8,128)(2,1)S(1)}, u32[]{:S(2)}, u32[]{:S(2)}) collective-permute-start(bf16[2,96,512]{2,1,0:T(8,128)(2,1)S(1)} %broadcast_select_fusion), channel_id=1, source_target_pairs={{0,32},{8,40},{16,48},{24,56},{32,0},{40,8},{48,16},{56,24},{64,96... | collective-permute-start | bytes 589832 | tf_op jit(solution)/shard_map/ppermute | solution.py:178
  91.9 12.3 %copy-start.4 = (bf16[2,96,512]{2,1,0:T(8,128)(2,1)}, bf16[2,96,512]{2,1,0:T(8,128)(2,1)S(1)}, u32[]{:S(2)}) copy-start(bf16[2,96,512]{2,1,0:T(8,128)(2,1)S(1)} %broadcast_select_fusion.1) | copy-start | bytes 589828
  91.9 12.3 %collective-permute-start.12 = (bf16[2,96,512]{2,1,0:T(8,128)(2,1)S(1)}, bf16[2,96,512]{2,1,0:T(8,128)(2,1)}, u32[]{:S(2)}, u32[]{:S(2)}) collective-permute-start(bf16[2,96,512]{2,1,0:T(8,128)(2,1)S(1)} %broadcast_select_fusion.1), channel_id=1, source_target_pairs={{0,64},{8,72},{16,80},{24,88},{32,96},{40,104},{48,112},{56,120},{... | collective-permute-start | bytes 589832 | tf_op jit(solution)/shard_map/ppermute | solution.py:178
  97.2 21.6 %all-to-all-start.3 = ((bf16[16,8,2304]{2,1,0:T(8,128)(2,1)}), bf16[16,8,2304]{2,1,0:T(8,128)(2,1)S(1)}, u32[]{:S(2)}, u32[]{:S(2)}) async-start(bf16[16,8,2304]{2,1,0:T(8,128)(2,1)} %fusion.1), calls=%async_computation.3 | async-start | bytes 1179648 | tf_op jit(solution)/shard_map/all_to_all | solution.py:219
  100.8 18.0 %collective-permute-start.9 = (bf16[4,96,384]{2,1,0:T(8,128)(2,1)}, bf16[4,96,384]{2,1,0:T(8,128)(2,1)S(1)}, u32[]{:S(2)}, u32[]{:S(2)}) collective-permute-start(bf16[4,96,384]{2,1,0:T(8,128)(2,1)} %get-tuple-element.14), channel_id=1, source_target_pairs={{0,64},{8,72},{16,80},{24,88},{32,96},{40,104},{48,112},{56,120},{... | collective-permute-start | bytes 884744 | tf_op jit(solution)/shard_map/ppermute | solution.py:31
  105.3 13.5 %copy-start.3 = (bf16[2,96,512]{2,1,0:T(8,128)(2,1)}, bf16[2,96,512]{2,1,0:T(8,128)(2,1)S(1)}, u32[]{:S(2)}) copy-start(bf16[2,96,512]{2,1,0:T(8,128)(2,1)S(1)} %broadcast_select_fusion.2.p_ref) | copy-start | bytes 589828
  105.3 9.3 %collective-permute-start.13 = (bf16[2,96,512]{2,1,0:T(8,128)(2,1)S(1)}, bf16[2,96,512]{2,1,0:T(8,128)(2,1)}, u32[]{:S(2)}, u32[]{:S(2)}) collective-permute-start(bf16[2,96,512]{2,1,0:T(8,128)(2,1)S(1)} %broadcast_select_fusion.2.p_ref), channel_id=1, source_target_pairs={{0,8},{8,0},{16,24},{24,16},{32,40},{40,32},{48,56},{56,48},{64,72... | collective-permute-start | bytes 589832 | tf_op jit(solution)/shard_map/ppermute | solution.py:181
  105.4 9.2 %collective-permute-start.7 = (bf16[96,384]{1,0:T(8,128)(2,1)}, bf16[96,384]{1,0:T(8,128)(2,1)S(1)}, u32[]{:S(2)}, u32[]{:S(2)}) collective-permute-start(bf16[96,384]{1,0:T(8,128)(2,1)} %get-tuple-element.12), channel_id=1, source_target_pairs={{0,8},{8,16},{16,24},{24,32},{32,40},{40,48},{48,56},{56,64},{64,7... | collective-permute-start | bytes 221192 | tf_op jit(solution)/shard_map/ppermute | solution.py:31
  105.9 8.7 %collective-permute-start.8 = (bf16[96,384]{1,0:T(8,128)(2,1)}, bf16[96,384]{1,0:T(8,128)(2,1)}, u32[]{:S(2)}, u32[]{:S(2)}) collective-permute-start(bf16[96,384]{1,0:T(8,128)(2,1)} %get-tuple-element.13), channel_id=1, source_target_pairs={{0,120},{8,0},{16,8},{24,16},{32,24},{40,32},{48,40},{56,48},{64,5... | collective-permute-start | bytes 221192 | tf_op jit(solution)/shard_map/ppermute | solution.py:31
  114.6 4.2 %copy-start.7 = (bf16[96,384]{1,0:T(8,128)(2,1)}, bf16[96,384]{1,0:T(8,128)(2,1)S(1)}, u32[]{:S(2)}) copy-start(bf16[96,384]{1,0:T(8,128)(2,1)S(1)} %collective-permute-done.7.prev_ref) | copy-start | bytes 221188
  118.8 0.7 copy-start.6
  118.8 0.9 copy-start.2
  123.4 6.6 %copy-start.8 = (s32[64]{0:T(128)S(1)}, s32[64]{0:T(128)}, u32[]{:S(2)}) copy-start(s32[64]{0:T(128)} %param.11) | copy-start | bytes 772
  123.4 26.8 %all-to-all-start.4 = ((bf16[8,48,1728]{2,1,0:T(8,128)(2,1)}), bf16[8,48,1728]{2,1,0:T(8,128)(2,1)}, u32[]{:S(2)}, u32[]{:S(2)}) async-start(bf16[8,48,1728]{2,1,0:T(8,128)(2,1)} %bitcast.20), calls=%async_computation.4 | async-start | bytes 2752512 | tf_op jit(solution)/shard_map/all_to_all | solution.py:229

commit v2 on v1

--- a/solution.py
+++ b/solution.py
@@ -16,7 +16,7 @@
 LANES = PIECE * WIDE
 USLOTS = 5
 PW = 512
-OUTSLOTS = 18
+OUTSLOTS = 12
 F32 = jnp.float32
 BF16 = jnp.bfloat16
 
@@ -88,7 +88,7 @@
             x_ref[j, :, pp * WIDE : (pp + 1) * WIDE] = chunk[e].astype(BF16)
 
 
-def product_kernel(c_ref, r_ref, own_ref, prev_ref, next_ref, far_ref, p_ref, o_ref, x_ref, scr, held):
+def product_kernel(c_ref, r_ref, own_ref, prev_ref, next_ref, far_ref, p_ref, o_ref, x_ref, scr):
     for octet in range(BS // 8):
         rows = []
         for e in range(8):
@@ -102,23 +102,26 @@
         if t == 3:
             g = g + next_ref[...].astype(F32)
         scr[t] = g + (scr[t] + scr[4 + t])
-    for kk in range(KK):
-        here = c_ref[0] == kk % 2
-        right = jnp.where(here, p_ref[kk // 2], o_ref[kk // 2])[:, : USLOTS * BS]
+    for sec in range(2):
+        rights = []
+        for e in range(2):
+            here = c_ref[0] == e
+            rights.append(jnp.where(here, p_ref[sec], o_ref[sec])[:, : USLOTS * BS])
         for t in range(4):
-            g = scr[t, :, kk * BS : (kk + 1) * BS]
-            high = g.astype(BF16)
-            low = (g - high.astype(F32)).astype(BF16)
-            out = jnp.dot(high, right, preferred_element_type=F32)
-            out = out + jnp.dot(low, right, preferred_element_type=F32)
+            outs = []
+            for e in range(2):
+                kk = 2 * sec + e
+                g = scr[t, :, kk * BS : (kk + 1) * BS]
+                high = g.astype(BF16)
+                low = (g - high.astype(F32)).astype(BF16)
+                out = jnp.dot(high, rights[e], preferred_element_type=F32)
+                outs.append(out + jnp.dot(low, rights[e], preferred_element_type=F32))
             span = slice(t * BS, (t + 1) * BS)
-            x_ref[span, kk * WIDE : (kk + 1) * WIDE] = out[:, :WIDE].astype(BF16)
-            if kk % 2 == 0:
-                held[t] = out[:, WIDE:]
-            else:
-                sec = kk // 2
-                cross = held[t] + out[:, WIDE:]
-                x_ref[span, 4 * WIDE + sec * BS : 4 * WIDE + (sec + 1) * BS] = cross.astype(BF16)
+            base = sec * OUTSLOTS // 2 * BS
+            band = outs[0][:, : 3 * BS] + outs[1][:, : 3 * BS]
+            x_ref[span, base : base + 3 * BS] = band.astype(BF16)
+            x_ref[span, base + 3 * BS : base + 5 * BS] = outs[0][:, 3 * BS :].astype(BF16)
+            x_ref[span, base + 5 * BS : base + 6 * BS] = outs[1][:, 4 * BS :].astype(BF16)
 
 
 def place_kernel(j_ref, r_ref, out_ref, acc):
@@ -156,11 +159,10 @@
         "iuj,ijf->iuf", pick.astype(BF16), p_blocks, preferred_element_type=F32
     ).astype(BF16)
 
-    sent = lax.all_to_all(
-        compact.reshape(COLS, USLOTS * area // 128, 128), "col", 0, 0, tiled=True
-    )
+    sent = lax.all_to_all(compact.reshape(COLS, USLOTS * area // 128, 128), "col", 0, 0, tiled=True)
     line = jnp.arange(COLS * 2 * BR, dtype=jnp.int32)
-    want = (line // 2) % BR * 2 * COLS + line % 2 * COLS + (col + line // (2 * BR)) % COLS
+    heir = (col + line // (2 * BR)) % COLS
+    want = (line // 2) % BR * 2 * COLS + 2 * (heir // 2 + 4 * (heir % 2)) + line % 2
     order = jnp.where(want[:, None] == line[None], a_mask.reshape(1, -1), 0)
     tiles = jnp.dot(
         order.astype(BF16), a_blocks.reshape(2 * BR * COLS, area), preferred_element_type=F32
@@ -173,7 +175,15 @@
     mine = mine.reshape(USLOTS, BS, BS).transpose(1, 0, 2).reshape(BS, USLOTS * BS)
     mine = jnp.pad(mine, ((0, 0), (0, PW - USLOTS * BS)))
     p_rows = lax.all_to_all(jnp.broadcast_to(mine[None], (COLS, BS, PW)), "col", 0, 0, tiled=True)
-    chosen = jnp.stack([mine, mine])
+    pairs = [
+        (r * COLS + c, (r ^ 1) * COLS + (c ^ 1))
+        for r in range(ROWS)
+        for c in range(COLS)
+        if r % 2 != c % 2
+    ]
+    other = lax.ppermute(mine, ("row", "col"), pairs)
+    start = jnp.where(row % 2 == col % 2, mine, other)
+    chosen = jnp.stack([start, start])
     for bit in range(3):
         moved = lax.ppermute(chosen, "row", [(r, r ^ (2 << bit)) for r in range(ROWS)])
         wrong = (((row // 2) ^ section_owner) >> bit) & 1
@@ -223,18 +233,17 @@
         out_shape=jax.ShapeDtypeStruct((4 * BS, OUTSLOTS * BS), BF16),
         in_specs=[SMEM] + [VMEM] * 7,
         out_specs=VMEM,
-        scratch_shapes=[pltpu.VMEM((BR, BS, WIDE), F32), pltpu.VMEM((4, BS, BS), F32)],
+        scratch_shapes=[pltpu.VMEM((BR, BS, WIDE), F32)],
         name="product",
     )((row % 2)[None], back, own, from_prev, from_next, from_far, chosen, swapped)
     outs = lax.all_to_all(outs.reshape(COLS, 4 * BS // COLS, OUTSLOTS * BS), "col", 0, 0, tiled=True)
 
-    k_col = jnp.arange(COLS, dtype=jnp.int32)[:, None, None]
-    k_sec = section_owner[None, :, None]
-    k_half = jnp.arange(2, dtype=jnp.int32)[None, None, :]
-    k_rows = 2 * BR * k_sec + BR * k_half + k_col
-    j_band = band_columns(k_rows, agg_order).reshape(COLS, 4 * KK)
-    j_cross = ((k_sec + 4) % COLS)[:, :, 0] * BR + k_col[:, :, 0]
-    j_table = jnp.concatenate([j_band, j_cross], axis=1)
+    c_id = jnp.arange(COLS, dtype=jnp.int32)[:, None]
+    centre = c_id // 2 + 4 * (c_id % 2)
+    j_band = band_columns(2 * BR * section_owner[None] + 2 * centre, agg_order)
+    e_id = jnp.arange(2, dtype=jnp.int32)
+    j_cross = ((section_owner + 4) % COLS)[None, :, None] * BR + (2 * centre[:, :, None] + e_id) % BR
+    j_table = jnp.concatenate([j_band, j_cross], axis=2).reshape(COLS, OUTSLOTS)
     return pl.pallas_call(
         place_kernel,
         out_shape=jax.ShapeDtypeStruct((4 * BS // COLS, NCB * BS), F32),

time: 155 us -> 153 us (0.987)
  local copies, waits for them, and re-layouts: 9.06 us -> 11.9 us
  waiting for transfers between devices: 46.9 us -> 44.9 us
    all_to_all x1, waiting for transfers between devices: 19.1 us -> 11.7 us  [inner(): lax.all_to_all(outs.reshape(COLS, 4 * BS // COLS, OUTSLOTS * BS), 'col',...]
    ppermute x10, starting transfers between devices: 24.4 us -> 27.6 us  [shift(): lax.ppermute(value, axis, [(i, (i + by) % size) for i in range(size)])]
    all_to_all x1, starting transfers between devices: 17.3 us -> 14.3 us  [inner(): lax.all_to_all(jnp.broadcast_to(mine[None], (COLS, BS, PW)), 'col', 0, 0,...]
    all_to_all x1, waiting for transfers between devices: 0.37 us -> 3.14 us  [inner(): lax.all_to_all(compact.reshape(COLS, USLOTS * area // 128, 128), 'col', 0...]
    ppermute x10, waiting for transfers between devices: 16.1 us -> 18.6 us  [shift(): lax.ppermute(value, axis, [(i, (i + by) % size) for i in range(size)])]
    unnamed x22 -> x40, local copies, waits for them, and re-layouts: 2.52 us -> 4.8 us
  transfers between devices with their start and end apart: 19 -> 20, of which waited for: 7 -> 8; matrix products, arithmetic and copies ran while one was open for 8% -> 7% of each run, Pallas kernels for 3% -> 3%
where the time goes in v2:
time: 153 us; the launch traced here: 152 us
  starting transfers between devices  73.1 us (48%)
  waiting for transfers between devices  44.9 us (29%)
  Pallas kernels  12.4 us (8%)
  local copies, waits for them, and re-layouts  11.9 us (8%)
  other arithmetic  5.85 us (4%)
  matrix products  3.78 us (2%)
    ppermute x10, starting transfers between devices, shift(): lax.ppermute(value, axis, [(i, (i + by) % size) for i in range(size)])  27.6 us
    ppermute x10, waiting for transfers between devices, shift(): lax.ppermute(value, axis, [(i, (i + by) % size) for i in range(size)])  18.6 us
    all_to_all x1, starting transfers between devices, inner(): lax.all_to_all(jnp.broadcast_to(mine[None], (COLS, BS, PW)), 'col', 0, 0,...  14.3 us
    all_to_all x1, waiting for transfers between devices, inner(): lax.all_to_all(outs.reshape(COLS, 4 * BS // COLS, OUTSLOTS * BS), 'col',...  11.7 us
    ppermute x3, waiting for transfers between devices, inner(): lax.ppermute(chosen, 'row', [(r, r ^ 2 << bit) for r in range(ROWS)])  11.5 us
    ppermute x3, starting transfers between devices, inner(): lax.ppermute(chosen, 'row', [(r, r ^ 2 << bit) for r in range(ROWS)])  8.05 us
    all_to_all x1, starting transfers between devices, inner(): spread = lax.all_to_all(spread, 'row', 0, 0, tiled=True)  7.43 us
    all_to_all x1, starting transfers between devices, inner(): lax.all_to_all(compact.reshape(COLS, USLOTS * area // 128, 128), 'col', 0...  6.07 us
  transfers between devices with their start and end apart: 20, of which 8 were waited for; matrix products, arithmetic and copies ran while one was open for 7% of the time, Pallas kernels for 3%

profile of v2, /device:TPU:0, one launch (start us, length us, event | category | flops | bytes accessed | tf_op | source)
XLA Modules:
  0.0 152.3 jit_solution(12557104807860009107)
XLA Ops:
  0.1 1.0 select_reduce_fusion.1
  1.2 0.1 copy.12
  1.2 0.7 broadcast_compare_fusion
  2.0 0.1 and_reduce_fusion
  2.1 0.1 copy.13
  2.2 1.8 %convolution_convert_fusion.1 = bf16[8,5,9216]{2,1,0:T(8,128)(2,1)S(1)} fusion(bf16[8,8,9216]{2,1,0:T(8,128)(2,1)} %param.8, s32[8]{0:T(128)S(1)} %iota_add_fusion.1, s32[8,5]{1,0:T(8,128)S(1)} %copy.12, pred[8,8]{1,0:T(8,128)(4,1)S(1)} %broadcast_compare_fusion, pred[8,5]{1,0:T(8,128)(4,1)S(1)} %copy.13), kind=kOutput, calls=%fused_computation.1 | convolution fusion | flops 6267840 | bytes 1917224 | tf_op jit(solution)/shard_map/iuj,ijf->iuf/dot_general | solution.py:158
  4.0 2.0 %reshape.955 = bf16[8,360,128]{2,1,0:T(8,128)(2,1)} reshape(bf16[8,5,9216]{2,1,0:T(8,128)(2,1)S(1)} %convolution_convert_fusion.1) | data formatting | bytes 1474560 | tf_op jit(solution)/shard_map/reshape | solution.py:162
  6.0 6.1 %all-to-all-start = ((bf16[8,360,128]{2,1,0:T(8,128)(2,1)}), bf16[8,360,128]{2,1,0:T(8,128)(2,1)S(1)}, u32[]{:S(2)}, u32[]{:S(2)}) async-start(bf16[8,360,128]{2,1,0:T(8,128)(2,1)} %reshape.955), calls=%async_computation | async-start | bytes 1474560 | tf_op jit(solution)/shard_map/all_to_all | solution.py:162
  12.1 0.1 broadcast_in_dim.96
  12.2 0.8 convolution_convert_fusion
  13.0 1.4 fusion.54
  14.4 2.0 %collective-permute-start = (bf16[16,9216]{1,0:T(8,128)(2,1)}, bf16[16,9216]{1,0:T(8,128)(2,1)}, u32[]{:S(2)}, u32[]{:S(2)}) collective-permute-start(bf16[16,9216]{1,0:T(8,128)(2,1)} %get-tuple-element.25), channel_id=1, source_target_pairs={{0,1},{1,2},{2,3},{3,4},{4,5},{5,6},{6,7},{7,0},{8,9},{9,10},{10,1... | collective-permute-start | bytes 884744 | tf_op jit(solution)/shard_map/ppermute | solution.py:31
  16.5 1.4 collective-permute-start.1
  17.9 2.1 %collective-permute-start.2 = (bf16[16,9216]{1,0:T(8,128)(2,1)}, bf16[16,9216]{1,0:T(8,128)(2,1)}, u32[]{:S(2)}, u32[]{:S(2)}) collective-permute-start(bf16[16,9216]{1,0:T(8,128)(2,1)} %get-tuple-element.23), channel_id=1, source_target_pairs={{0,3},{1,4},{2,5},{3,6},{4,7},{5,0},{6,1},{7,2},{8,11},{9,12},{10,... | collective-permute-start | bytes 884744 | tf_op jit(solution)/shard_map/ppermute | solution.py:31
  20.0 2.1 %collective-permute-start.3 = (bf16[16,9216]{1,0:T(8,128)(2,1)}, bf16[16,9216]{1,0:T(8,128)(2,1)}, u32[]{:S(2)}, u32[]{:S(2)}) collective-permute-start(bf16[16,9216]{1,0:T(8,128)(2,1)} %get-tuple-element.22), channel_id=1, source_target_pairs={{0,4},{1,5},{2,6},{3,7},{4,0},{5,1},{6,2},{7,3},{8,12},{9,13},{10,... | collective-permute-start | bytes 884744 | tf_op jit(solution)/shard_map/ppermute | solution.py:31
  22.1 3.1 %all-to-all-done = bf16[8,360,128]{2,1,0:T(8,128)(2,1)S(1)} async-done(((bf16[8,360,128]{2,1,0:T(8,128)(2,1)}), bf16[8,360,128]{2,1,0:T(8,128)(2,1)S(1)}, u32[]{:S(2)}, u32[]{:S(2)}) %all-to-all-start) | async-done | bytes 737312 | tf_op jit(solution)/shard_map/all_to_all | solution.py:162
  25.3 0.1 reduce_sum.32
  25.4 0.1 reshape.956
  25.5 0.1 copy.14
  25.7 0.1 copy.15
  25.8 0.9 broadcast_in_dim.95
  26.8 14.3 %all-to-all-start.1 = ((bf16[8,96,512]{2,1,0:T(8,128)(2,1)}), bf16[8,96,512]{2,1,0:T(8,128)(2,1)S(1)}, u32[]{:S(2)}, u32[]{:S(2)}) async-start(bf16[8,96,512]{2,1,0:T(8,128)(2,1)} %broadcast_in_dim.95), calls=%async_computation.1 | async-start | bytes 1572864 | tf_op jit(solution)/shard_map/all_to_all | solution.py:177
  41.0 0.5 and_select_fusion.22
  41.7 0.7 add.605
  42.3 0.7 collective-permute-start.10
  43.1 0.6 eq.132
  43.7 10.1 %collective-permute-start.4 = (bf16[16,9216]{1,0:T(8,128)(2,1)}, bf16[16,9216]{1,0:T(8,128)(2,1)S(1)}, u32[]{:S(2)}, u32[]{:S(2)}) collective-permute-start(bf16[16,9216]{1,0:T(8,128)(2,1)} %get-tuple-element.21), channel_id=1, source_target_pairs={{0,5},{1,6},{2,7},{3,0},{4,1},{5,2},{6,3},{7,4},{8,13},{9,14},{10,... | collective-permute-start | bytes 884744 | tf_op jit(solution)/shard_map/ppermute | solution.py:31
  53.9 1.0 collective-permute-start.5
  54.9 0.7 pad_maximum_fusion
  55.6 1.5 collective-permute-start.11
  57.1 0.6 and_compare_fusion.2
  57.7 4.8 %collective-permute-done.4.refs_5_ = bf16[16,9216]{1,0:T(8,128)(2,1)S(1)} collective-permute-done((bf16[16,9216]{1,0:T(8,128)(2,1)}, bf16[16,9216]{1,0:T(8,128)(2,1)S(1)}, u32[]{:S(2)}, u32[]{:S(2)}) %collective-permute-start.4) | collective-permute-done | bytes 294944 | tf_op jit(solution)/shard_map/ppermute | solution.py:31
  62.5 5.4 %collective-permute-done.5.refs_6_ = bf16[16,9216]{1,0:T(8,128)(2,1)S(1)} collective-permute-done((bf16[16,9216]{1,0:T(8,128)(2,1)}, bf16[16,9216]{1,0:T(8,128)(2,1)S(1)}, u32[]{:S(2)}, u32[]{:S(2)}) %collective-permute-start.5) | collective-permute-done | bytes 294944 | tf_op jit(solution)/shard_map/ppermute | solution.py:31
  67.8 0.7 copy-done.8
  68.5 1.9 %collective-permute-done.6.refs_7_ = bf16[16,9216]{1,0:T(8,128)(2,1)} collective-permute-done((bf16[16,9216]{1,0:T(8,128)(2,1)}, bf16[16,9216]{1,0:T(8,128)(2,1)}, u32[]{:S(2)}, u32[]{:S(2)}) %collective-permute-start.6) | collective-permute-done | bytes 294944 | tf_op jit(solution)/shard_map/ppermute | solution.py:31
  70.4 0.9 copy-done.2
  71.3 5.1 %partial.1 = (bf16[16,8,2304]{2,1,0:T(8,128)(2,1)}, f32[4,96,384]{2,1,0:T(8,128)}, bf16[96,384]{1,0:T(8,128)(2,1)}, bf16[96,384]{1,0:T(8,128)(2,1)}, bf16[4,96,384]{2,1,0:T(8,128)(2,1)}) custom-call(s32[2]{0:T(128)} %get-tuple-element.32.s_ref, bf16[8,96,512]{2,1,0:T(8,128)(2,1)} %copy-done.2, bf16[16,9216]{1,0:T(8,128)(2,1)} %get-tuple-element.26.refs_0_, ...), custom_call_target="tpu_custom_call" | custom-call | tf_op jit(solution)/shard_map/partial/pallas_call | solution.py:194
  76.4 7.4 %all-to-all-start.2 = ((bf16[16,8,2304]{2,1,0:T(8,128)(2,1)}), bf16[16,8,2304]{2,1,0:T(8,128)(2,1)S(1)}, u32[]{:S(2)}, u32[]{:S(2)}) async-start(bf16[16,8,2304]{2,1,0:T(8,128)(2,1)} %get-tuple-element.10), calls=%async_computation.2 | async-start | bytes 1179648 | tf_op jit(solution)/shard_map/all_to_all | solution.py:213
  83.9 0.1 broadcast_select_fusion
  83.9 3.5 %collective-permute-start.12 = (bf16[2,96,512]{2,1,0:T(8,128)(2,1)S(1)}, bf16[2,96,512]{2,1,0:T(8,128)(2,1)S(1)}, u32[]{:S(2)}, u32[]{:S(2)}) collective-permute-start(bf16[2,96,512]{2,1,0:T(8,128)(2,1)S(1)} %broadcast_select_fusion), channel_id=1, source_target_pairs={{0,32},{8,40},{16,48},{24,56},{32,0},{40,8},{48,16},{56,24},{64,96... | collective-permute-start | bytes 589832 | tf_op jit(solution)/shard_map/ppermute | solution.py:188
  87.5 11.5 %collective-permute-done.12 = bf16[2,96,512]{2,1,0:T(8,128)(2,1)S(1)} collective-permute-done((bf16[2,96,512]{2,1,0:T(8,128)(2,1)S(1)}, bf16[2,96,512]{2,1,0:T(8,128)(2,1)S(1)}, u32[]{:S(2)}, u32[]{:S(2)}) %collective-permute-start.12) | collective-permute-done | bytes 196640 | tf_op jit(solution)/shard_map/ppermute | solution.py:188
  99.0 0.1 broadcast_select_fusion.1
  99.1 3.1 %collective-permute-start.13 = (bf16[2,96,512]{2,1,0:T(8,128)(2,1)S(1)}, bf16[2,96,512]{2,1,0:T(8,128)(2,1)}, u32[]{:S(2)}, u32[]{:S(2)}) collective-permute-start(bf16[2,96,512]{2,1,0:T(8,128)(2,1)S(1)} %broadcast_select_fusion.1), channel_id=1, source_target_pairs={{0,64},{8,72},{16,80},{24,88},{32,96},{40,104},{48,112},{56,120},{... | collective-permute-start | bytes 589832 | tf_op jit(solution)/shard_map/ppermute | solution.py:188
  102.2 1.2 fusion.1
  103.3 3.6 %all-to-all-start.3 = ((bf16[16,8,2304]{2,1,0:T(8,128)(2,1)}), bf16[16,8,2304]{2,1,0:T(8,128)(2,1)S(1)}, u32[]{:S(2)}, u32[]{:S(2)}) async-start(bf16[16,8,2304]{2,1,0:T(8,128)(2,1)} %fusion.1), calls=%async_computation.3 | async-start | bytes 1179648 | tf_op jit(solution)/shard_map/all_to_all | solution.py:229
  106.9 0.1 and_select_fusion.2
  107.0 0.4 collective-permute-start.7
  107.4 5.1 %collective-permute-start.8 = (bf16[96,384]{1,0:T(8,128)(2,1)}, bf16[96,384]{1,0:T(8,128)(2,1)S(1)}, u32[]{:S(2)}, u32[]{:S(2)}) collective-permute-start(bf16[96,384]{1,0:T(8,128)(2,1)} %get-tuple-element.13), channel_id=1, source_target_pairs={{0,120},{8,0},{16,8},{24,16},{32,24},{40,32},{48,40},{56,48},{64,5... | collective-permute-start | bytes 221192 | tf_op jit(solution)/shard_map/ppermute | solution.py:31
  112.5 3.4 %collective-permute-start.9 = (bf16[4,96,384]{2,1,0:T(8,128)(2,1)}, bf16[4,96,384]{2,1,0:T(8,128)(2,1)S(1)}, u32[]{:S(2)}, u32[]{:S(2)}) collective-permute-start(bf16[4,96,384]{2,1,0:T(8,128)(2,1)} %get-tuple-element.14), channel_id=1, source_target_pairs={{0,64},{8,72},{16,80},{24,88},{32,96},{40,104},{48,112},{56,120},{... | collective-permute-start | bytes 884744 | tf_op jit(solution)/shard_map/ppermute | solution.py:31
  115.8 1.1 broadcast_select_fusion.2.p_ref
  116.9 0.1 collective-permute-start.14
  117.0 3.7 %collective-permute-done.7.prev_ref = bf16[96,384]{1,0:T(8,128)(2,1)S(1)} collective-permute-done((bf16[96,384]{1,0:T(8,128)(2,1)}, bf16[96,384]{1,0:T(8,128)(2,1)S(1)}, u32[]{:S(2)}, u32[]{:S(2)}) %collective-permute-start.7) | collective-permute-done | bytes 73760 | tf_op jit(solution)/shard_map/ppermute | solution.py:31
  120.7 0.6 copy-done.11
  121.4 0.7 copy-done.9
  122.0 2.8 %collective-permute-done.9.far_ref = bf16[4,96,384]{2,1,0:T(8,128)(2,1)S(1)} collective-permute-done((bf16[4,96,384]{2,1,0:T(8,128)(2,1)}, bf16[4,96,384]{2,1,0:T(8,128)(2,1)S(1)}, u32[]{:S(2)}, u32[]{:S(2)}) %collective-permute-start.9) | collective-permute-done | bytes 294944 | tf_op jit(solution)/shard_map/ppermute | solution.py:31
  124.9 0.7 copy-done.6
  125.6 0.2 copy-done.3
  125.8 3.7 %product.1 = bf16[384,1152]{1,0:T(8,128)(2,1)} custom-call(s32[1]{0:T(128)} %bitcast.c_ref, bf16[16,8,2304]{2,1,0:T(8,128)(2,1)} %copy-done.3, f32[4,96,384]{2,1,0:T(8,128)} %get-tuple-element.11.own_ref, bf16[96,384]{1,0:T(8,128)(2,1)} %copy-done.10, bf16[96,384]{1,0:T(8,128)(2,1)} %copy-done.11, bf16[4,96,384]{2,1,0:T(8,128)(2,1)} %copy-done.6, ...), custom_call_target="tpu_custom_call" | custom-call | tf_op jit(solution)/shard_map/product/pallas_call | solution.py:231
  129.5 5.4 %all-to-all-start.4 = ((bf16[8,48,1152]{2,1,0:T(8,128)(2,1)}), bf16[8,48,1152]{2,1,0:T(8,128)(2,1)S(1)}, u32[]{:S(2)}, u32[]{:S(2)}) async-start(bf16[8,48,1152]{2,1,0:T(8,128)(2,1)} %bitcast.21), calls=%async_computation.4 | async-start | bytes 1769472 | tf_op jit(solution)/shard_map/all_to_all | solution.py:239
  134.9 0.3 select_reduce_fusion
  135.3 0.7 copy.16.j_ref
  136.0 11.7 %all-to-all-done.4.r_ref = bf16[8,48,1152]{2,1,0:T(8,128)(2,1)S(1)} async-done(((bf16[8,48,1152]{2,1,0:T(8,128)(2,1)}), bf16[8,48,1152]{2,1,0:T(8,128)(2,1)S(1)}, u32[]{:S(2)}, u32[]{:S(2)}) %all-to-all-start.4) | async-done | bytes 884768 | tf_op jit(solution)/shard_map/all_to_all | solution.py:239
  147.6 0.9 copy-done.1
  148.6 3.7 %place.1 = f32[48,6144]{1,0:T(8,128)} custom-call(s32[8,12]{1,0:T(8,128)} %copy.16.j_ref, bf16[8,48,1152]{2,1,0:T(8,128)(2,1)} %copy-done.1), custom_call_target="tpu_custom_call" | custom-call | tf_op jit(solution)/shard_map/place/pallas_call | solution.py:247
  (73 shorter events, 0.8 us)
Async XLA Ops:
  0.0 12.2 %copy-start = (bf16[8,16,9216]{2,1,0:T(8,128)(2,1)S(1)}, bf16[8,16,9216]{2,1,0:T(8,128)(2,1)}, u32[]{:S(2)}) copy-start(bf16[8,16,9216]{2,1,0:T(8,128)(2,1)} %param.6) | copy-start | bytes 7077892
  6.0 6.1 %copy-start.13 = (s32[8,16]{1,0:T(8,128)S(1)}, s32[8,16]{1,0:T(8,128)}, u32[]{:S(2)}) copy-start(s32[8,16]{1,0:T(8,128)} %param.7) | copy-start | bytes 1540
  6.0 19.3 %all-to-all-start = ((bf16[8,360,128]{2,1,0:T(8,128)(2,1)}), bf16[8,360,128]{2,1,0:T(8,128)(2,1)S(1)}, u32[]{:S(2)}, u32[]{:S(2)}) async-start(bf16[8,360,128]{2,1,0:T(8,128)(2,1)} %reshape.955), calls=%async_computation | async-start | bytes 1474560 | tf_op jit(solution)/shard_map/all_to_all | solution.py:162
  14.4 39.5 %collective-permute-start = (bf16[16,9216]{1,0:T(8,128)(2,1)}, bf16[16,9216]{1,0:T(8,128)(2,1)}, u32[]{:S(2)}, u32[]{:S(2)}) collective-permute-start(bf16[16,9216]{1,0:T(8,128)(2,1)} %get-tuple-element.25), channel_id=1, source_target_pairs={{0,1},{1,2},{2,3},{3,4},{4,5},{5,6},{6,7},{7,0},{8,9},{9,10},{10,1... | collective-permute-start | bytes 884744 | tf_op jit(solution)/shard_map/ppermute | solution.py:31
  16.5 38.4 %collective-permute-start.1 = (bf16[16,9216]{1,0:T(8,128)(2,1)}, bf16[16,9216]{1,0:T(8,128)(2,1)}, u32[]{:S(2)}, u32[]{:S(2)}) collective-permute-start(bf16[16,9216]{1,0:T(8,128)(2,1)} %get-tuple-element.24), channel_id=1, source_target_pairs={{0,2},{1,3},{2,4},{3,5},{4,6},{5,7},{6,0},{7,1},{8,10},{9,11},{10,... | collective-permute-start | bytes 884744 | tf_op jit(solution)/shard_map/ppermute | solution.py:31
  17.9 37.7 %collective-permute-start.2 = (bf16[16,9216]{1,0:T(8,128)(2,1)}, bf16[16,9216]{1,0:T(8,128)(2,1)}, u32[]{:S(2)}, u32[]{:S(2)}) collective-permute-start(bf16[16,9216]{1,0:T(8,128)(2,1)} %get-tuple-element.23), channel_id=1, source_target_pairs={{0,3},{1,4},{2,5},{3,6},{4,7},{5,0},{6,1},{7,2},{8,11},{9,12},{10,... | collective-permute-start | bytes 884744 | tf_op jit(solution)/shard_map/ppermute | solution.py:31
  20.0 37.7 %collective-permute-start.3 = (bf16[16,9216]{1,0:T(8,128)(2,1)}, bf16[16,9216]{1,0:T(8,128)(2,1)}, u32[]{:S(2)}, u32[]{:S(2)}) collective-permute-start(bf16[16,9216]{1,0:T(8,128)(2,1)} %get-tuple-element.22), channel_id=1, source_target_pairs={{0,4},{1,5},{2,6},{3,7},{4,0},{5,1},{6,2},{7,3},{8,12},{9,13},{10,... | collective-permute-start | bytes 884744 | tf_op jit(solution)/shard_map/ppermute | solution.py:31
  25.8 15.2 %copy-start.14 = (s32[2]{0:T(128)S(1)}, s32[2]{0:T(128)}, u32[]{:S(2)}) copy-start(s32[2]{0:T(128)} %param.10) | copy-start | bytes 28
  25.8 15.8 %copy-start.12 = (s32[64]{0:T(128)S(1)}, s32[64]{0:T(128)}, u32[]{:S(2)}) copy-start(s32[64]{0:T(128)} %param.11) | copy-start | bytes 772
  26.8 43.7 %all-to-all-start.1 = ((bf16[8,96,512]{2,1,0:T(8,128)(2,1)}), bf16[8,96,512]{2,1,0:T(8,128)(2,1)S(1)}, u32[]{:S(2)}, u32[]{:S(2)}) async-start(bf16[8,96,512]{2,1,0:T(8,128)(2,1)} %broadcast_in_dim.95), calls=%async_computation.1 | async-start | bytes 1572864 | tf_op jit(solution)/shard_map/all_to_all | solution.py:177
  42.3 1.4 collective-permute-start.10
  43.7 18.7 %collective-permute-start.4 = (bf16[16,9216]{1,0:T(8,128)(2,1)}, bf16[16,9216]{1,0:T(8,128)(2,1)S(1)}, u32[]{:S(2)}, u32[]{:S(2)}) collective-permute-start(bf16[16,9216]{1,0:T(8,128)(2,1)} %get-tuple-element.21), channel_id=1, source_target_pairs={{0,5},{1,6},{2,7},{3,0},{4,1},{5,2},{6,3},{7,4},{8,13},{9,14},{10,... | collective-permute-start | bytes 884744 | tf_op jit(solution)/shard_map/ppermute | solution.py:31
  53.9 13.9 %collective-permute-start.5 = (bf16[16,9216]{1,0:T(8,128)(2,1)}, bf16[16,9216]{1,0:T(8,128)(2,1)S(1)}, u32[]{:S(2)}, u32[]{:S(2)}) collective-permute-start(bf16[16,9216]{1,0:T(8,128)(2,1)} %get-tuple-element.20), channel_id=1, source_target_pairs={{0,6},{1,7},{2,0},{3,1},{4,2},{5,3},{6,4},{7,5},{8,14},{9,15},{10,... | collective-permute-start | bytes 884744 | tf_op jit(solution)/shard_map/ppermute | solution.py:31
  54.9 15.5 %collective-permute-start.6 = (bf16[16,9216]{1,0:T(8,128)(2,1)}, bf16[16,9216]{1,0:T(8,128)(2,1)}, u32[]{:S(2)}, u32[]{:S(2)}) collective-permute-start(bf16[16,9216]{1,0:T(8,128)(2,1)} %get-tuple-element.19), channel_id=1, source_target_pairs={{0,7},{1,0},{2,1},{3,2},{4,3},{5,4},{6,5},{7,6},{8,15},{9,8},{10,9... | collective-permute-start | bytes 884744 | tf_op jit(solution)/shard_map/ppermute | solution.py:31
  55.6 28.2 %collective-permute-start.11 = (bf16[2,96,512]{2,1,0:T(8,128)(2,1)}, bf16[2,96,512]{2,1,0:T(8,128)(2,1)S(1)}, u32[]{:S(2)}, u32[]{:S(2)}) collective-permute-start(bf16[2,96,512]{2,1,0:T(8,128)(2,1)} %pad_maximum_fusion), channel_id=1, source_target_pairs={{0,16},{8,24},{16,0},{24,8},{32,48},{40,56},{48,32},{56,40},{64,80... | collective-permute-start | bytes 589832 | tf_op jit(solution)/shard_map/ppermute | solution.py:188
  62.5 5.4 %copy-start.7 = (bf16[16,9216]{1,0:T(8,128)(2,1)}, bf16[16,9216]{1,0:T(8,128)(2,1)S(1)}, u32[]{:S(2)}) copy-start(bf16[16,9216]{1,0:T(8,128)(2,1)S(1)} %collective-permute-done.4.refs_5_) | copy-start | bytes 884740
  67.8 0.7 copy-start.8
  70.4 0.9 copy-start.2
  76.4 25.8 %copy-start.16 = (s32[128]{0:T(128)S(1)}, s32[128]{0:T(128)}, u32[]{:S(2)}) copy-start(s32[128]{0:T(128)} %add.605) | copy-start | bytes 1540
  76.4 25.8 %copy-start.17 = (s32[128]{0:T(128)S(1)}, s32[128]{0:T(128)}, u32[]{:S(2)}) copy-start(s32[128]{0:T(128)} %eq.132) | copy-start | bytes 1540
  76.4 25.7 %all-to-all-start.2 = ((bf16[16,8,2304]{2,1,0:T(8,128)(2,1)}), bf16[16,8,2304]{2,1,0:T(8,128)(2,1)S(1)}, u32[]{:S(2)}, u32[]{:S(2)}) async-start(bf16[16,8,2304]{2,1,0:T(8,128)(2,1)} %get-tuple-element.10), calls=%async_computation.2 | async-start | bytes 1179648 | tf_op jit(solution)/shard_map/all_to_all | solution.py:213
  83.9 15.0 %collective-permute-start.12 = (bf16[2,96,512]{2,1,0:T(8,128)(2,1)S(1)}, bf16[2,96,512]{2,1,0:T(8,128)(2,1)S(1)}, u32[]{:S(2)}, u32[]{:S(2)}) collective-permute-start(bf16[2,96,512]{2,1,0:T(8,128)(2,1)S(1)} %broadcast_select_fusion), channel_id=1, source_target_pairs={{0,32},{8,40},{16,48},{24,56},{32,0},{40,8},{48,16},{56,24},{64,96... | collective-permute-start | bytes 589832 | tf_op jit(solution)/shard_map/ppermute | solution.py:188
  87.5 19.5 %copy-start.18 = (s32[8]{0:T(128)}, s32[8]{0:T(128)S(1)}, u32[]{:S(2)}) copy-start(s32[8]{0:T(128)S(1)} %fusion.28) | copy-start | bytes 100
  99.1 4.3 %copy-start.5 = (bf16[2,96,512]{2,1,0:T(8,128)(2,1)}, bf16[2,96,512]{2,1,0:T(8,128)(2,1)S(1)}, u32[]{:S(2)}) copy-start(bf16[2,96,512]{2,1,0:T(8,128)(2,1)S(1)} %broadcast_select_fusion.1) | copy-start | bytes 589828
  99.1 16.7 %copy-start.15 = (pred[2]{0:T(512)(128)(4,1)S(1)}, pred[2]{0:T(512)(128)(4,1)}, u32[]{:S(2)}) copy-start(pred[2]{0:T(512)(128)(4,1)} %get-tuple-element.29) | copy-start | bytes 10
  99.1 16.7 %collective-permute-start.13 = (bf16[2,96,512]{2,1,0:T(8,128)(2,1)S(1)}, bf16[2,96,512]{2,1,0:T(8,128)(2,1)}, u32[]{:S(2)}, u32[]{:S(2)}) collective-permute-start(bf16[2,96,512]{2,1,0:T(8,128)(2,1)S(1)} %broadcast_select_fusion.1), channel_id=1, source_target_pairs={{0,64},{8,72},{16,80},{24,88},{32,96},{40,104},{48,112},{56,120},{... | collective-permute-start | bytes 589832 | tf_op jit(solution)/shard_map/ppermute | solution.py:188
  103.3 21.6 %all-to-all-start.3 = ((bf16[16,8,2304]{2,1,0:T(8,128)(2,1)}), bf16[16,8,2304]{2,1,0:T(8,128)(2,1)S(1)}, u32[]{:S(2)}, u32[]{:S(2)}) async-start(bf16[16,8,2304]{2,1,0:T(8,128)(2,1)} %fusion.1), calls=%async_computation.3 | async-start | bytes 1179648 | tf_op jit(solution)/shard_map/all_to_all | solution.py:229
  107.0 13.7 %collective-permute-start.7 = (bf16[96,384]{1,0:T(8,128)(2,1)}, bf16[96,384]{1,0:T(8,128)(2,1)S(1)}, u32[]{:S(2)}, u32[]{:S(2)}) collective-permute-start(bf16[96,384]{1,0:T(8,128)(2,1)} %get-tuple-element.12), channel_id=1, source_target_pairs={{0,8},{8,16},{16,24},{24,32},{32,40},{40,48},{48,56},{56,64},{64,7... | collective-permute-start | bytes 221192 | tf_op jit(solution)/shard_map/ppermute | solution.py:31
  107.4 13.3 %collective-permute-start.8 = (bf16[96,384]{1,0:T(8,128)(2,1)}, bf16[96,384]{1,0:T(8,128)(2,1)S(1)}, u32[]{:S(2)}, u32[]{:S(2)}) collective-permute-start(bf16[96,384]{1,0:T(8,128)(2,1)} %get-tuple-element.13), channel_id=1, source_target_pairs={{0,120},{8,0},{16,8},{24,16},{32,24},{40,32},{48,40},{56,48},{64,5... | collective-permute-start | bytes 221192 | tf_op jit(solution)/shard_map/ppermute | solution.py:31
  112.5 12.4 %collective-permute-start.9 = (bf16[4,96,384]{2,1,0:T(8,128)(2,1)}, bf16[4,96,384]{2,1,0:T(8,128)(2,1)S(1)}, u32[]{:S(2)}, u32[]{:S(2)}) collective-permute-start(bf16[4,96,384]{2,1,0:T(8,128)(2,1)} %get-tuple-element.14), channel_id=1, source_target_pairs={{0,64},{8,72},{16,80},{24,88},{32,96},{40,104},{48,112},{56,120},{... | collective-permute-start | bytes 884744 | tf_op jit(solution)/shard_map/ppermute | solution.py:31
  116.9 8.0 %copy-start.4 = (bf16[2,96,512]{2,1,0:T(8,128)(2,1)}, bf16[2,96,512]{2,1,0:T(8,128)(2,1)S(1)}, u32[]{:S(2)}) copy-start(bf16[2,96,512]{2,1,0:T(8,128)(2,1)S(1)} %broadcast_select_fusion.2.p_ref) | copy-start | bytes 589828
  116.9 3.8 %collective-permute-start.14 = (bf16[2,96,512]{2,1,0:T(8,128)(2,1)S(1)}, bf16[2,96,512]{2,1,0:T(8,128)(2,1)S(1)}, u32[]{:S(2)}, u32[]{:S(2)}) collective-permute-start(bf16[2,96,512]{2,1,0:T(8,128)(2,1)S(1)} %broadcast_select_fusion.2.p_ref), channel_id=1, source_target_pairs={{0,8},{8,0},{16,24},{24,16},{32,40},{40,32},{48,56},{56,48},{64,72... | collective-permute-start | bytes 589832 | tf_op jit(solution)/shard_map/ppermute | solution.py:191
  120.7 4.2 %copy-start.10 = (bf16[96,384]{1,0:T(8,128)(2,1)}, bf16[96,384]{1,0:T(8,128)(2,1)S(1)}, u32[]{:S(2)}) copy-start(bf16[96,384]{1,0:T(8,128)(2,1)S(1)} %collective-permute-done.7.prev_ref) | copy-start | bytes 221188
  120.7 0.6 copy-start.11
  121.4 0.7 copy-start.9
  124.9 0.7 copy-start.6
  124.9 0.9 copy-start.3
  129.5 5.7 %copy-start.19 = (s32[8]{0:T(128)S(1)}, s32[8]{0:T(128)}, u32[]{:S(2)}) copy-start(s32[8]{0:T(128)} %copy-done.18) | copy-start | bytes 100
  129.5 18.1 %all-to-all-start.4 = ((bf16[8,48,1152]{2,1,0:T(8,128)(2,1)}), bf16[8,48,1152]{2,1,0:T(8,128)(2,1)S(1)}, u32[]{:S(2)}, u32[]{:S(2)}) async-start(bf16[8,48,1152]{2,1,0:T(8,128)(2,1)} %bitcast.21), calls=%async_computation.4 | async-start | bytes 1769472 | tf_op jit(solution)/shard_map/all_to_all | solution.py:239
  147.6 0.9 copy-start.1

commit v3 on v2

--- a/solution.py
+++ b/solution.py
@@ -88,7 +88,7 @@
             x_ref[j, :, pp * WIDE : (pp + 1) * WIDE] = chunk[e].astype(BF16)
 
 
-def product_kernel(c_ref, r_ref, own_ref, prev_ref, next_ref, far_ref, p_ref, o_ref, x_ref, scr):
+def product_kernel(c_ref, r_ref, own_ref, prev_ref, next_ref, far_ref, p_ref, o_ref, near_ref, cross_ref, x_ref, scr):
     for octet in range(BS // 8):
         rows = []
         for e in range(8):
@@ -105,8 +105,10 @@
     for sec in range(2):
         rights = []
         for e in range(2):
-            here = c_ref[0] == e
-            rights.append(jnp.where(here, p_ref[sec], o_ref[sec])[:, : USLOTS * BS])
+            keeper = c_ref[1] == 1
+            mine = jnp.where(keeper, p_ref[sec], o_ref[sec])
+            theirs = jnp.where(keeper, near_ref[sec], cross_ref[sec])
+            rights.append(jnp.where(c_ref[0] == e, mine, theirs)[:, : USLOTS * BS])
         for t in range(4):
             outs = []
             for e in range(2):
@@ -140,6 +142,7 @@
 
 VMEM = pl.BlockSpec(memory_space=pltpu.VMEM)
 SMEM = pl.BlockSpec(memory_space=pltpu.SMEM)
+ANY = pl.BlockSpec(memory_space=pl.ANY)
 
 
 def inner(a_blocks, a_mask, p_blocks, p_mask, section_owner, agg_order):
@@ -175,20 +178,23 @@
     mine = mine.reshape(USLOTS, BS, BS).transpose(1, 0, 2).reshape(BS, USLOTS * BS)
     mine = jnp.pad(mine, ((0, 0), (0, PW - USLOTS * BS)))
     p_rows = lax.all_to_all(jnp.broadcast_to(mine[None], (COLS, BS, PW)), "col", 0, 0, tiled=True)
-    pairs = [
-        (r * COLS + c, (r ^ 1) * COLS + (c ^ 1))
-        for r in range(ROWS)
-        for c in range(COLS)
-        if r % 2 != c % 2
-    ]
-    other = lax.ppermute(mine, ("row", "col"), pairs)
-    start = jnp.where(row % 2 == col % 2, mine, other)
-    chosen = jnp.stack([start, start])
+    chosen = jnp.stack([mine, mine])
     for bit in range(3):
         moved = lax.ppermute(chosen, "row", [(r, r ^ (2 << bit)) for r in range(ROWS)])
         wrong = (((row // 2) ^ section_owner) >> bit) & 1
         chosen = jnp.where(wrong[:, None, None] == 1, moved, chosen)
-    swapped = lax.ppermute(chosen, "row", [(r, r ^ 1) for r in range(ROWS)])
+    held = [
+        (r, c) for r in range(ROWS) for c in range(COLS) if r % 2 == c % 2
+    ]
+    lent = [
+        (r, c) for r in range(ROWS) for c in range(COLS) if r % 2 != c % 2
+    ]
+
+    def swap(givers, over_core, over_col):
+        pairs = [(r * COLS + c, (r ^ over_core) * COLS + (c ^ over_col)) for r, c in givers]
+        return lax.ppermute(chosen, ("row", "col"), pairs)
+
+    swaps = swap(held, 1, 0), swap(lent, 0, 1), swap(lent, 1, 1)
 
     away = (col - section_owner) % COLS
     spread, own, prev_part, next_part, far_part = pl.pallas_call(
@@ -200,7 +206,7 @@
             jax.ShapeDtypeStruct((BS, WIDE), BF16),
             jax.ShapeDtypeStruct((4, BS, WIDE), BF16),
         ),
-        in_specs=[SMEM, VMEM] + [pl.BlockSpec(memory_space=pl.ANY)] * COLS,
+        in_specs=[SMEM, VMEM] + [ANY] * COLS,
         out_specs=(VMEM,) * 5,
         scratch_shapes=[
             pltpu.VMEM((BR, BS, WIDE), F32),
@@ -228,14 +234,17 @@
     back = jnp.where(is_low, total - high, high).astype(BF16).reshape(ROWS, BR, LANES)
     back = lax.all_to_all(back, "row", 0, 0, tiled=True)
 
+    parity = jnp.stack([col % 2, (row % 2 == col % 2).astype(jnp.int32)])
     outs = pl.pallas_call(
         product_kernel,
         out_shape=jax.ShapeDtypeStruct((4 * BS, OUTSLOTS * BS), BF16),
-        in_specs=[SMEM] + [VMEM] * 7,
+        in_specs=[SMEM] + [VMEM] * 9,
         out_specs=VMEM,
-        scratch_shapes=[pltpu.VMEM((BR, BS, WIDE), F32)],
+        scratch_shapes=[
+            pltpu.VMEM((BR, BS, WIDE), F32),
+        ],
         name="product",
-    )((row % 2)[None], back, own, from_prev, from_next, from_far, chosen, swapped)
+    )(parity, back, own, from_prev, from_next, from_far, chosen, *swaps)
     outs = lax.all_to_all(outs.reshape(COLS, 4 * BS // COLS, OUTSLOTS * BS), "col", 0, 0, tiled=True)
 
     c_id = jnp.arange(COLS, dtype=jnp.int32)[:, None]

time: 153 us -> 150 us (0.980)
  waiting for transfers between devices: 44.9 us -> 41.5 us
  starting transfers between devices: 73.1 us -> 71.3 us
    ppermute x3, waiting for transfers between devices: 11.5 us -> 0.01 us  [inner(): lax.ppermute(chosen, 'row', [(r, r ^ 2 << bit) for r in range(ROWS)])]
    all_to_all x1, waiting for transfers between devices: 0.01 us -> 7.73 us  [inner(): spread = lax.all_to_all(spread, 'row', 0, 0, tiled=True)]
    ppermute x10, starting transfers between devices: 27.6 us -> 22.7 us  [shift(): lax.ppermute(value, axis, [(i, (i + by) % size) for i in range(size)])]
    ppermute x2 -> x3, starting transfers between devices: 0.74 us -> 5.5 us  [swap(): return lax.ppermute(chosen, ('row', 'col'), pairs)]
    all_to_all x1, waiting for transfers between devices: 11.7 us -> 14.7 us  [inner(): lax.all_to_all(outs.reshape(COLS, 4 * BS // COLS, OUTSLOTS * BS), 'col',...]
    all_to_all x1, starting transfers between devices: 5.39 us -> 3.56 us  [inner(): lax.all_to_all(outs.reshape(COLS, 4 * BS // COLS, OUTSLOTS * BS), 'col',...]
    ppermute x10, waiting for transfers between devices: 18.6 us -> 16.7 us  [shift(): lax.ppermute(value, axis, [(i, (i + by) % size) for i in range(size)])]
  transfers between devices with their start and end apart: 20 -> 21, of which waited for: 8 -> 8; matrix products, arithmetic and copies ran while one was open for 7% -> 8% of each run, Pallas kernels for 3% -> 3%
where the time goes in v3:
time: 150 us; the launch traced here: 148 us
  starting transfers between devices  71.3 us (48%)
  waiting for transfers between devices  41.5 us (28%)
  Pallas kernels  12.5 us (8%)
  local copies, waits for them, and re-layouts  10.9 us (7%)
  other arithmetic  7 us (5%)
  matrix products  4.85 us (3%)
    ppermute x10, starting transfers between devices, shift(): lax.ppermute(value, axis, [(i, (i + by) % size) for i in range(size)])  22.7 us
    ppermute x10, waiting for transfers between devices, shift(): lax.ppermute(value, axis, [(i, (i + by) % size) for i in range(size)])  16.7 us
    all_to_all x1, waiting for transfers between devices, inner(): lax.all_to_all(outs.reshape(COLS, 4 * BS // COLS, OUTSLOTS * BS), 'col',...  14.7 us
    all_to_all x1, starting transfers between devices, inner(): lax.all_to_all(jnp.broadcast_to(mine[None], (COLS, BS, PW)), 'col', 0, 0,...  14.3 us
    ppermute x3, starting transfers between devices, inner(): lax.ppermute(chosen, 'row', [(r, r ^ 2 << bit) for r in range(ROWS)])  8.06 us
    all_to_all x1, waiting for transfers between devices, inner(): spread = lax.all_to_all(spread, 'row', 0, 0, tiled=True)  7.73 us
    all_to_all x1, starting transfers between devices, inner(): spread = lax.all_to_all(spread, 'row', 0, 0, tiled=True)  7.47 us
    all_to_all x1, starting transfers between devices, inner(): lax.all_to_all(compact.reshape(COLS, USLOTS * area // 128, 128), 'col', 0...  6.07 us
  transfers between devices with their start and end apart: 21, of which 8 were waited for; matrix products, arithmetic and copies ran while one was open for 8% of the time, Pallas kernels for 3%

profile of v3, /device:TPU:0, one launch (start us, length us, event | category | flops | bytes accessed | tf_op | source)
XLA Modules:
  0.0 148.4 jit_solution(681334865389466829)
XLA Ops:
  0.1 1.0 select_reduce_fusion.1
  1.2 0.1 copy.12
  1.2 0.7 broadcast_compare_fusion
  2.0 0.1 and_reduce_fusion
  2.1 0.1 copy.13
  2.2 1.8 %convolution_convert_fusion.1 = bf16[8,5,9216]{2,1,0:T(8,128)(2,1)S(1)} fusion(bf16[8,8,9216]{2,1,0:T(8,128)(2,1)} %param.8, s32[8]{0:T(128)S(1)} %iota_add_fusion.1, s32[8,5]{1,0:T(8,128)S(1)} %copy.12, pred[8,8]{1,0:T(8,128)(4,1)S(1)} %broadcast_compare_fusion, pred[8,5]{1,0:T(8,128)(4,1)S(1)} %copy.13), kind=kOutput, calls=%fused_computation.1 | convolution fusion | flops 6267840 | bytes 1917224 | tf_op jit(solution)/shard_map/iuj,ijf->iuf/dot_general | solution.py:161
  4.0 2.0 %reshape.955 = bf16[8,360,128]{2,1,0:T(8,128)(2,1)} reshape(bf16[8,5,9216]{2,1,0:T(8,128)(2,1)S(1)} %convolution_convert_fusion.1) | data formatting | bytes 1474560 | tf_op jit(solution)/shard_map/reshape | solution.py:165
  6.0 6.1 %all-to-all-start = ((bf16[8,360,128]{2,1,0:T(8,128)(2,1)}), bf16[8,360,128]{2,1,0:T(8,128)(2,1)S(1)}, u32[]{:S(2)}, u32[]{:S(2)}) async-start(bf16[8,360,128]{2,1,0:T(8,128)(2,1)} %reshape.955), calls=%async_computation | async-start | bytes 1474560 | tf_op jit(solution)/shard_map/all_to_all | solution.py:165
  12.2 0.8 convolution_convert_fusion
  13.0 1.5 fusion.54
  14.5 2.0 %collective-permute-start = (bf16[16,9216]{1,0:T(8,128)(2,1)}, bf16[16,9216]{1,0:T(8,128)(2,1)}, u32[]{:S(2)}, u32[]{:S(2)}) collective-permute-start(bf16[16,9216]{1,0:T(8,128)(2,1)} %get-tuple-element.25), channel_id=1, source_target_pairs={{0,1},{1,2},{2,3},{3,4},{4,5},{5,6},{6,7},{7,0},{8,9},{9,10},{10,1... | collective-permute-start | bytes 884744 | tf_op jit(solution)/shard_map/ppermute | solution.py:31
  16.5 1.4 collective-permute-start.1
  18.0 2.1 %collective-permute-start.2 = (bf16[16,9216]{1,0:T(8,128)(2,1)}, bf16[16,9216]{1,0:T(8,128)(2,1)}, u32[]{:S(2)}, u32[]{:S(2)}) collective-permute-start(bf16[16,9216]{1,0:T(8,128)(2,1)} %get-tuple-element.23), channel_id=1, source_target_pairs={{0,3},{1,4},{2,5},{3,6},{4,7},{5,0},{6,1},{7,2},{8,11},{9,12},{10,... | collective-permute-start | bytes 884744 | tf_op jit(solution)/shard_map/ppermute | solution.py:31
  20.0 2.1 %collective-permute-start.3 = (bf16[16,9216]{1,0:T(8,128)(2,1)}, bf16[16,9216]{1,0:T(8,128)(2,1)}, u32[]{:S(2)}, u32[]{:S(2)}) collective-permute-start(bf16[16,9216]{1,0:T(8,128)(2,1)} %get-tuple-element.22), channel_id=1, source_target_pairs={{0,4},{1,5},{2,6},{3,7},{4,0},{5,1},{6,2},{7,3},{8,12},{9,13},{10,... | collective-permute-start | bytes 884744 | tf_op jit(solution)/shard_map/ppermute | solution.py:31
  22.3 0.6 and_select_fusion.22
  22.9 2.3 %all-to-all-done = bf16[8,360,128]{2,1,0:T(8,128)(2,1)S(1)} async-done(((bf16[8,360,128]{2,1,0:T(8,128)(2,1)}), bf16[8,360,128]{2,1,0:T(8,128)(2,1)S(1)}, u32[]{:S(2)}, u32[]{:S(2)}) %all-to-all-start) | async-done | bytes 737312 | tf_op jit(solution)/shard_map/all_to_all | solution.py:165
  25.3 0.1 reduce_sum.32
  25.4 0.1 reshape.956
  25.5 0.1 copy.14
  25.7 0.1 copy.15
  25.8 0.9 broadcast_in_dim.93
  26.7 14.3 %all-to-all-start.1 = ((bf16[8,96,512]{2,1,0:T(8,128)(2,1)}), bf16[8,96,512]{2,1,0:T(8,128)(2,1)S(1)}, u32[]{:S(2)}, u32[]{:S(2)}) async-start(bf16[8,96,512]{2,1,0:T(8,128)(2,1)} %broadcast_in_dim.93), calls=%async_computation.1 | async-start | bytes 1572864 | tf_op jit(solution)/shard_map/all_to_all | solution.py:180
  41.0 1.6 %collective-permute-start.10 = (bf16[2,96,512]{2,1,0:T(8,128)(2,1)S(1)}, bf16[2,96,512]{2,1,0:T(8,128)(2,1)S(1)}, u32[]{:S(2)}, u32[]{:S(2)}) collective-permute-start(bf16[2,96,512]{2,1,0:T(8,128)(2,1)S(1)} %pad_maximum_fusion), channel_id=1, source_target_pairs={{0,16},{8,24},{16,0},{24,8},{32,48},{40,56},{48,32},{56,40},{64,80... | collective-permute-start | bytes 589832 | tf_op jit(solution)/shard_map/ppermute | solution.py:183
  42.6 0.5 and_compare_fusion.2
  43.2 4.4 %collective-permute-start.4 = (bf16[16,9216]{1,0:T(8,128)(2,1)}, bf16[16,9216]{1,0:T(8,128)(2,1)S(1)}, u32[]{:S(2)}, u32[]{:S(2)}) collective-permute-start(bf16[16,9216]{1,0:T(8,128)(2,1)} %get-tuple-element.21), channel_id=1, source_target_pairs={{0,5},{1,6},{2,7},{3,0},{4,1},{5,2},{6,3},{7,4},{8,13},{9,14},{10,... | collective-permute-start | bytes 884744 | tf_op jit(solution)/shard_map/ppermute | solution.py:31
  47.6 1.2 collective-permute-start.5
  48.8 2.2 %collective-permute-start.6 = (bf16[16,9216]{1,0:T(8,128)(2,1)}, bf16[16,9216]{1,0:T(8,128)(2,1)}, u32[]{:S(2)}, u32[]{:S(2)}) collective-permute-start(bf16[16,9216]{1,0:T(8,128)(2,1)} %get-tuple-element.19), channel_id=1, source_target_pairs={{0,7},{1,0},{2,1},{3,2},{4,3},{5,4},{6,5},{7,6},{8,15},{9,8},{10,9... | collective-permute-start | bytes 884744 | tf_op jit(solution)/shard_map/ppermute | solution.py:31
  50.9 0.8 broadcast_select_fusion
  51.7 3.0 %collective-permute-start.11 = (bf16[2,96,512]{2,1,0:T(8,128)(2,1)}, bf16[2,96,512]{2,1,0:T(8,128)(2,1)}, u32[]{:S(2)}, u32[]{:S(2)}) collective-permute-start(bf16[2,96,512]{2,1,0:T(8,128)(2,1)} %broadcast_select_fusion), channel_id=1, source_target_pairs={{0,32},{8,40},{16,48},{24,56},{32,0},{40,8},{48,16},{56,24},{64,96... | collective-permute-start | bytes 589832 | tf_op jit(solution)/shard_map/ppermute | solution.py:183
  54.7 4.9 %collective-permute-done.4.refs_5_ = bf16[16,9216]{1,0:T(8,128)(2,1)S(1)} collective-permute-done((bf16[16,9216]{1,0:T(8,128)(2,1)}, bf16[16,9216]{1,0:T(8,128)(2,1)S(1)}, u32[]{:S(2)}, u32[]{:S(2)}) %collective-permute-start.4) | collective-permute-done | bytes 294944 | tf_op jit(solution)/shard_map/ppermute | solution.py:31
  59.6 0.7 copy-done.6
  60.4 0.7 copy-done.7
  61.1 4.0 %collective-permute-done.6.refs_7_ = bf16[16,9216]{1,0:T(8,128)(2,1)} collective-permute-done((bf16[16,9216]{1,0:T(8,128)(2,1)}, bf16[16,9216]{1,0:T(8,128)(2,1)}, u32[]{:S(2)}, u32[]{:S(2)}) %collective-permute-start.6) | collective-permute-done | bytes 294944 | tf_op jit(solution)/shard_map/ppermute | solution.py:31
  65.0 0.9 copy-done.2
  65.9 5.0 %partial.1 = (bf16[16,8,2304]{2,1,0:T(8,128)(2,1)}, f32[4,96,384]{2,1,0:T(8,128)}, bf16[96,384]{1,0:T(8,128)(2,1)}, bf16[96,384]{1,0:T(8,128)(2,1)}, bf16[4,96,384]{2,1,0:T(8,128)(2,1)}) custom-call(s32[2]{0:T(128)} %get-tuple-element.34.s_ref, bf16[8,96,512]{2,1,0:T(8,128)(2,1)} %copy-done.2, bf16[16,9216]{1,0:T(8,128)(2,1)} %get-tuple-element.26.refs_0_, ...), custom_call_target="tpu_custom_call" | custom-call | tf_op jit(solution)/shard_map/partial/pallas_call | solution.py:200
  71.0 7.5 %all-to-all-start.2 = ((bf16[16,8,2304]{2,1,0:T(8,128)(2,1)}), bf16[16,8,2304]{2,1,0:T(8,128)(2,1)}, u32[]{:S(2)}, u32[]{:S(2)}) async-start(bf16[16,8,2304]{2,1,0:T(8,128)(2,1)} %get-tuple-element.10), calls=%async_computation.2 | async-start | bytes 1179648 | tf_op jit(solution)/shard_map/all_to_all | solution.py:219
  78.5 0.7 and_select_fusion.2
  79.1 1.0 broadcast_select_fusion.1
  80.2 3.5 %collective-permute-start.12 = (bf16[2,96,512]{2,1,0:T(8,128)(2,1)S(1)}, bf16[2,96,512]{2,1,0:T(8,128)(2,1)S(1)}, u32[]{:S(2)}, u32[]{:S(2)}) collective-permute-start(bf16[2,96,512]{2,1,0:T(8,128)(2,1)S(1)} %broadcast_select_fusion.1), channel_id=1, source_target_pairs={{0,64},{8,72},{16,80},{24,88},{32,96},{40,104},{48,112},{56,120},{... | collective-permute-start | bytes 589832 | tf_op jit(solution)/shard_map/ppermute | solution.py:183
  83.6 0.1 add.606
  83.7 0.1 eq.133
  83.8 7.7 %all-to-all-done.2 = bf16[16,8,2304]{2,1,0:T(8,128)(2,1)} async-done(((bf16[16,8,2304]{2,1,0:T(8,128)(2,1)}), bf16[16,8,2304]{2,1,0:T(8,128)(2,1)}, u32[]{:S(2)}, u32[]{:S(2)}) %all-to-all-start.2) | async-done | bytes 589856 | tf_op jit(solution)/shard_map/all_to_all | solution.py:219
  91.5 2.2 %fusion.1 = bf16[16,8,2304]{2,1,0:T(8,128)(2,1)} fusion(bf16[16,8,2304]{2,1,0:T(8,128)(2,1)} %all-to-all-done.2, pred[128]{0:T(512)(128)(4,1)S(1)} %fusion.52, s32[128]{0:T(128)S(1)} %add.606, s32[128]{0:T(128)S(1)} %eq.133), kind=kOutput, calls=%fused_computation.4 | convolution fusion | flops 76693504 | bytes 1180800 | tf_op jit(solution)/shard_map/dot_general | solution.py:229
  93.8 3.7 %all-to-all-start.3 = ((bf16[16,8,2304]{2,1,0:T(8,128)(2,1)}), bf16[16,8,2304]{2,1,0:T(8,128)(2,1)S(1)}, u32[]{:S(2)}, u32[]{:S(2)}) async-start(bf16[16,8,2304]{2,1,0:T(8,128)(2,1)} %fusion.1), calls=%async_computation.3 | async-start | bytes 1179648 | tf_op jit(solution)/shard_map/all_to_all | solution.py:235
  97.5 0.1 broadcast_select_fusion.2.p_ref
  97.6 2.9 %collective-permute-start.13 = (bf16[2,96,512]{2,1,0:T(8,128)(2,1)S(1)}, bf16[2,96,512]{2,1,0:T(8,128)(2,1)}, u32[]{:S(2)}, u32[]{:S(2)}) collective-permute-start(bf16[2,96,512]{2,1,0:T(8,128)(2,1)S(1)} %broadcast_select_fusion.2.p_ref), channel_id=1, source_target_pairs={{0,8},{2,10},{4,12},{6,14},{9,1},{11,3},{13,5},{15,7},{16,24},{18,... | collective-permute-start | bytes 589832 | tf_op jit(solution)/shard_map/ppermute | solution.py:195
  100.5 1.3 collective-permute-start.14
  101.8 1.3 collective-permute-start.15
  103.1 4.1 %collective-permute-start.7 = (bf16[96,384]{1,0:T(8,128)(2,1)}, bf16[96,384]{1,0:T(8,128)(2,1)S(1)}, u32[]{:S(2)}, u32[]{:S(2)}) collective-permute-start(bf16[96,384]{1,0:T(8,128)(2,1)} %get-tuple-element.12), channel_id=1, source_target_pairs={{0,8},{8,16},{16,24},{24,32},{32,40},{40,48},{48,56},{56,64},{64,7... | collective-permute-start | bytes 221192 | tf_op jit(solution)/shard_map/ppermute | solution.py:31
  107.2 3.2 %collective-permute-start.9 = (bf16[4,96,384]{2,1,0:T(8,128)(2,1)}, bf16[4,96,384]{2,1,0:T(8,128)(2,1)S(1)}, u32[]{:S(2)}, u32[]{:S(2)}) collective-permute-start(bf16[4,96,384]{2,1,0:T(8,128)(2,1)} %get-tuple-element.14), channel_id=1, source_target_pairs={{0,64},{8,72},{16,80},{24,88},{32,96},{40,104},{48,112},{56,120},{... | collective-permute-start | bytes 884744 | tf_op jit(solution)/shard_map/ppermute | solution.py:31
  110.4 4.1 %collective-permute-done.7.prev_ref = bf16[96,384]{1,0:T(8,128)(2,1)S(1)} collective-permute-done((bf16[96,384]{1,0:T(8,128)(2,1)}, bf16[96,384]{1,0:T(8,128)(2,1)S(1)}, u32[]{:S(2)}, u32[]{:S(2)}) %collective-permute-start.7) | collective-permute-done | bytes 73760 | tf_op jit(solution)/shard_map/ppermute | solution.py:31
  114.5 0.7 pad_add_fusion.6.c_ref
  115.2 1.6 %collective-permute-done.8.next_ref = bf16[96,384]{1,0:T(8,128)(2,1)S(1)} collective-permute-done((bf16[96,384]{1,0:T(8,128)(2,1)}, bf16[96,384]{1,0:T(8,128)(2,1)S(1)}, u32[]{:S(2)}, u32[]{:S(2)}) %collective-permute-start.8) | collective-permute-done | bytes 73760 | tf_op jit(solution)/shard_map/ppermute | solution.py:31
  116.8 0.6 copy-done.9
  117.4 2.2 %collective-permute-done.9.far_ref = bf16[4,96,384]{2,1,0:T(8,128)(2,1)S(1)} collective-permute-done((bf16[4,96,384]{2,1,0:T(8,128)(2,1)}, bf16[4,96,384]{2,1,0:T(8,128)(2,1)S(1)}, u32[]{:S(2)}, u32[]{:S(2)}) %collective-permute-start.9) | collective-permute-done | bytes 294944 | tf_op jit(solution)/shard_map/ppermute | solution.py:31
  119.6 0.7 copy-done.5
  120.3 0.3 copy-done.3
  120.6 3.8 %product.1 = bf16[384,1152]{1,0:T(8,128)(2,1)} custom-call(s32[2]{0:T(128)} %pad_add_fusion.6.c_ref, bf16[16,8,2304]{2,1,0:T(8,128)(2,1)} %copy-done.3, f32[4,96,384]{2,1,0:T(8,128)} %get-tuple-element.11.own_ref, bf16[96,384]{1,0:T(8,128)(2,1)} %copy-done.8, bf16[96,384]{1,0:T(8,128)(2,1)} %copy-done.9, bf16[4,96,384]{2,1,0:T(8,128)(2,1)} %copy-done.5, ...), custom_call_target="tpu_custom_call" | custom-call | tf_op jit(solution)/shard_map/product/pallas_call | solution.py:238
  124.4 3.6 %all-to-all-start.4 = ((bf16[8,48,1152]{2,1,0:T(8,128)(2,1)}), bf16[8,48,1152]{2,1,0:T(8,128)(2,1)S(1)}, u32[]{:S(2)}, u32[]{:S(2)}) async-start(bf16[8,48,1152]{2,1,0:T(8,128)(2,1)} %bitcast.22), calls=%async_computation.4 | async-start | bytes 1769472 | tf_op jit(solution)/shard_map/all_to_all | solution.py:248
  128.0 0.3 select_reduce_fusion
  128.4 0.7 copy.16.j_ref
  129.1 14.7 %all-to-all-done.4.r_ref = bf16[8,48,1152]{2,1,0:T(8,128)(2,1)S(1)} async-done(((bf16[8,48,1152]{2,1,0:T(8,128)(2,1)}), bf16[8,48,1152]{2,1,0:T(8,128)(2,1)S(1)}, u32[]{:S(2)}, u32[]{:S(2)}) %all-to-all-start.4) | async-done | bytes 884768 | tf_op jit(solution)/shard_map/all_to_all | solution.py:248
  143.8 0.9 copy-done.1
  144.7 3.7 %place.1 = f32[48,6144]{1,0:T(8,128)} custom-call(s32[8,12]{1,0:T(8,128)} %copy.16.j_ref, bf16[8,48,1152]{2,1,0:T(8,128)(2,1)} %copy-done.1), custom_call_target="tpu_custom_call" | custom-call | tf_op jit(solution)/shard_map/place/pallas_call | solution.py:256
  (75 shorter events, 0.8 us)
Async XLA Ops:
  0.0 12.2 %copy-start = (bf16[8,16,9216]{2,1,0:T(8,128)(2,1)S(1)}, bf16[8,16,9216]{2,1,0:T(8,128)(2,1)}, u32[]{:S(2)}) copy-start(bf16[8,16,9216]{2,1,0:T(8,128)(2,1)} %param.6) | copy-start | bytes 7077892
  6.0 6.1 %copy-start.13 = (s32[8,16]{1,0:T(8,128)S(1)}, s32[8,16]{1,0:T(8,128)}, u32[]{:S(2)}) copy-start(s32[8,16]{1,0:T(8,128)} %param.7) | copy-start | bytes 1540
  6.0 19.3 %all-to-all-start = ((bf16[8,360,128]{2,1,0:T(8,128)(2,1)}), bf16[8,360,128]{2,1,0:T(8,128)(2,1)S(1)}, u32[]{:S(2)}, u32[]{:S(2)}) async-start(bf16[8,360,128]{2,1,0:T(8,128)(2,1)} %reshape.955), calls=%async_computation | async-start | bytes 1474560 | tf_op jit(solution)/shard_map/all_to_all | solution.py:165
  13.0 9.1 %copy-start.11 = (s32[64]{0:T(128)S(1)}, s32[64]{0:T(128)}, u32[]{:S(2)}) copy-start(s32[64]{0:T(128)} %param.11) | copy-start | bytes 772
  13.0 9.3 %copy-start.15 = (s32[2]{0:T(128)S(1)}, s32[2]{0:T(128)}, u32[]{:S(2)}) copy-start(s32[2]{0:T(128)} %param.10) | copy-start | bytes 28
  14.5 28.7 %collective-permute-start = (bf16[16,9216]{1,0:T(8,128)(2,1)}, bf16[16,9216]{1,0:T(8,128)(2,1)}, u32[]{:S(2)}, u32[]{:S(2)}) collective-permute-start(bf16[16,9216]{1,0:T(8,128)(2,1)} %get-tuple-element.25), channel_id=1, source_target_pairs={{0,1},{1,2},{2,3},{3,4},{4,5},{5,6},{6,7},{7,0},{8,9},{9,10},{10,1... | collective-permute-start | bytes 884744 | tf_op jit(solution)/shard_map/ppermute | solution.py:31
  16.5 31.1 %collective-permute-start.1 = (bf16[16,9216]{1,0:T(8,128)(2,1)}, bf16[16,9216]{1,0:T(8,128)(2,1)}, u32[]{:S(2)}, u32[]{:S(2)}) collective-permute-start(bf16[16,9216]{1,0:T(8,128)(2,1)} %get-tuple-element.24), channel_id=1, source_target_pairs={{0,2},{1,3},{2,4},{3,5},{4,6},{5,7},{6,0},{7,1},{8,10},{9,11},{10,... | collective-permute-start | bytes 884744 | tf_op jit(solution)/shard_map/ppermute | solution.py:31
  18.0 33.7 %collective-permute-start.2 = (bf16[16,9216]{1,0:T(8,128)(2,1)}, bf16[16,9216]{1,0:T(8,128)(2,1)}, u32[]{:S(2)}, u32[]{:S(2)}) collective-permute-start(bf16[16,9216]{1,0:T(8,128)(2,1)} %get-tuple-element.23), channel_id=1, source_target_pairs={{0,3},{1,4},{2,5},{3,6},{4,7},{5,0},{6,1},{7,2},{8,11},{9,12},{10,... | collective-permute-start | bytes 884744 | tf_op jit(solution)/shard_map/ppermute | solution.py:31
  20.0 34.7 %collective-permute-start.3 = (bf16[16,9216]{1,0:T(8,128)(2,1)}, bf16[16,9216]{1,0:T(8,128)(2,1)}, u32[]{:S(2)}, u32[]{:S(2)}) collective-permute-start(bf16[16,9216]{1,0:T(8,128)(2,1)} %get-tuple-element.22), channel_id=1, source_target_pairs={{0,4},{1,5},{2,6},{3,7},{4,0},{5,1},{6,2},{7,3},{8,12},{9,13},{10,... | collective-permute-start | bytes 884744 | tf_op jit(solution)/shard_map/ppermute | solution.py:31
  26.7 38.3 %all-to-all-start.1 = ((bf16[8,96,512]{2,1,0:T(8,128)(2,1)}), bf16[8,96,512]{2,1,0:T(8,128)(2,1)S(1)}, u32[]{:S(2)}, u32[]{:S(2)}) async-start(bf16[8,96,512]{2,1,0:T(8,128)(2,1)} %broadcast_in_dim.93), calls=%async_computation.1 | async-start | bytes 1572864 | tf_op jit(solution)/shard_map/all_to_all | solution.py:180
  41.0 7.7 %collective-permute-start.10 = (bf16[2,96,512]{2,1,0:T(8,128)(2,1)S(1)}, bf16[2,96,512]{2,1,0:T(8,128)(2,1)S(1)}, u32[]{:S(2)}, u32[]{:S(2)}) collective-permute-start(bf16[2,96,512]{2,1,0:T(8,128)(2,1)S(1)} %pad_maximum_fusion), channel_id=1, source_target_pairs={{0,16},{8,24},{16,0},{24,8},{32,48},{40,56},{48,32},{56,40},{64,80... | collective-permute-start | bytes 589832 | tf_op jit(solution)/shard_map/ppermute | solution.py:183
  43.2 16.5 %collective-permute-start.4 = (bf16[16,9216]{1,0:T(8,128)(2,1)}, bf16[16,9216]{1,0:T(8,128)(2,1)S(1)}, u32[]{:S(2)}, u32[]{:S(2)}) collective-permute-start(bf16[16,9216]{1,0:T(8,128)(2,1)} %get-tuple-element.21), channel_id=1, source_target_pairs={{0,5},{1,6},{2,7},{3,0},{4,1},{5,2},{6,3},{7,4},{8,13},{9,14},{10,... | collective-permute-start | bytes 884744 | tf_op jit(solution)/shard_map/ppermute | solution.py:31
  47.6 12.1 %collective-permute-start.5 = (bf16[16,9216]{1,0:T(8,128)(2,1)}, bf16[16,9216]{1,0:T(8,128)(2,1)S(1)}, u32[]{:S(2)}, u32[]{:S(2)}) collective-permute-start(bf16[16,9216]{1,0:T(8,128)(2,1)} %get-tuple-element.20), channel_id=1, source_target_pairs={{0,6},{1,7},{2,0},{3,1},{4,2},{5,3},{6,4},{7,5},{8,14},{9,15},{10,... | collective-permute-start | bytes 884744 | tf_op jit(solution)/shard_map/ppermute | solution.py:31
  48.8 16.3 %collective-permute-start.6 = (bf16[16,9216]{1,0:T(8,128)(2,1)}, bf16[16,9216]{1,0:T(8,128)(2,1)}, u32[]{:S(2)}, u32[]{:S(2)}) collective-permute-start(bf16[16,9216]{1,0:T(8,128)(2,1)} %get-tuple-element.19), channel_id=1, source_target_pairs={{0,7},{1,0},{2,1},{3,2},{4,3},{5,4},{6,5},{7,6},{8,15},{9,8},{10,9... | collective-permute-start | bytes 884744 | tf_op jit(solution)/shard_map/ppermute | solution.py:31
  50.9 27.5 %copy-start.18 = (s32[8]{0:T(128)}, s32[8]{0:T(128)S(1)}, u32[]{:S(2)}) copy-start(s32[8]{0:T(128)S(1)} %fusion.28) | copy-start | bytes 100
  51.7 27.4 %collective-permute-start.11 = (bf16[2,96,512]{2,1,0:T(8,128)(2,1)}, bf16[2,96,512]{2,1,0:T(8,128)(2,1)}, u32[]{:S(2)}, u32[]{:S(2)}) collective-permute-start(bf16[2,96,512]{2,1,0:T(8,128)(2,1)} %broadcast_select_fusion), channel_id=1, source_target_pairs={{0,32},{8,40},{16,48},{24,56},{32,0},{40,8},{48,16},{56,24},{64,96... | collective-permute-start | bytes 589832 | tf_op jit(solution)/shard_map/ppermute | solution.py:183
  59.6 0.7 copy-start.6
  60.4 0.7 copy-start.7
  65.0 0.9 copy-start.2
  71.0 20.6 %all-to-all-start.2 = ((bf16[16,8,2304]{2,1,0:T(8,128)(2,1)}), bf16[16,8,2304]{2,1,0:T(8,128)(2,1)}, u32[]{:S(2)}, u32[]{:S(2)}) async-start(bf16[16,8,2304]{2,1,0:T(8,128)(2,1)} %get-tuple-element.10), calls=%async_computation.2 | async-start | bytes 1179648 | tf_op jit(solution)/shard_map/all_to_all | solution.py:219
  80.2 17.4 %collective-permute-start.12 = (bf16[2,96,512]{2,1,0:T(8,128)(2,1)S(1)}, bf16[2,96,512]{2,1,0:T(8,128)(2,1)S(1)}, u32[]{:S(2)}, u32[]{:S(2)}) collective-permute-start(bf16[2,96,512]{2,1,0:T(8,128)(2,1)S(1)} %broadcast_select_fusion.1), channel_id=1, source_target_pairs={{0,64},{8,72},{16,80},{24,88},{32,96},{40,104},{48,112},{56,120},{... | collective-permute-start | bytes 589832 | tf_op jit(solution)/shard_map/ppermute | solution.py:183
  83.8 13.7 %copy-start.17 = (pred[2]{0:T(512)(128)(4,1)S(1)}, pred[2]{0:T(512)(128)(4,1)}, u32[]{:S(2)}) copy-start(pred[2]{0:T(512)(128)(4,1)} %get-tuple-element.31) | copy-start | bytes 10
  93.8 16.6 %copy-start.10 = (s32[8,2,1]{0,2,1:T(1,128)S(1)}, s32[8,2,1]{0,2,1:T(1,128)}, u32[]{:S(2)}) copy-start(s32[8,2,1]{0,2,1:T(1,128)} %get-tuple-element.18) | copy-start | bytes 196
  93.8 25.8 %all-to-all-start.3 = ((bf16[16,8,2304]{2,1,0:T(8,128)(2,1)}), bf16[16,8,2304]{2,1,0:T(8,128)(2,1)S(1)}, u32[]{:S(2)}, u32[]{:S(2)}) async-start(bf16[16,8,2304]{2,1,0:T(8,128)(2,1)} %fusion.1), calls=%async_computation.3 | async-start | bytes 1179648 | tf_op jit(solution)/shard_map/all_to_all | solution.py:235
  97.6 22.0 %copy-start.4 = (bf16[2,96,512]{2,1,0:T(8,128)(2,1)}, bf16[2,96,512]{2,1,0:T(8,128)(2,1)S(1)}, u32[]{:S(2)}) copy-start(bf16[2,96,512]{2,1,0:T(8,128)(2,1)S(1)} %broadcast_select_fusion.2.p_ref) | copy-start | bytes 589828
  97.6 19.2 %collective-permute-start.13 = (bf16[2,96,512]{2,1,0:T(8,128)(2,1)S(1)}, bf16[2,96,512]{2,1,0:T(8,128)(2,1)}, u32[]{:S(2)}, u32[]{:S(2)}) collective-permute-start(bf16[2,96,512]{2,1,0:T(8,128)(2,1)S(1)} %broadcast_select_fusion.2.p_ref), channel_id=1, source_target_pairs={{0,8},{2,10},{4,12},{6,14},{9,1},{11,3},{13,5},{15,7},{16,24},{18,... | collective-permute-start | bytes 589832 | tf_op jit(solution)/shard_map/ppermute | solution.py:195
  100.5 16.3 %collective-permute-start.14 = (bf16[2,96,512]{2,1,0:T(8,128)(2,1)S(1)}, bf16[2,96,512]{2,1,0:T(8,128)(2,1)}, u32[]{:S(2)}, u32[]{:S(2)}) collective-permute-start(bf16[2,96,512]{2,1,0:T(8,128)(2,1)S(1)} %broadcast_select_fusion.2.p_ref), channel_id=1, source_target_pairs={{1,0},{3,2},{5,4},{7,6},{8,9},{10,11},{12,13},{14,15},{17,16},{19,... | collective-permute-start | bytes 589832 | tf_op jit(solution)/shard_map/ppermute | solution.py:195
  101.8 15.0 %collective-permute-start.15 = (bf16[2,96,512]{2,1,0:T(8,128)(2,1)S(1)}, bf16[2,96,512]{2,1,0:T(8,128)(2,1)}, u32[]{:S(2)}, u32[]{:S(2)}) collective-permute-start(bf16[2,96,512]{2,1,0:T(8,128)(2,1)S(1)} %broadcast_select_fusion.2.p_ref), channel_id=1, source_target_pairs={{1,8},{3,10},{5,12},{7,14},{8,1},{10,3},{12,5},{14,7},{17,24},{19,... | collective-permute-start | bytes 589832 | tf_op jit(solution)/shard_map/ppermute | solution.py:195
  103.1 11.4 %collective-permute-start.7 = (bf16[96,384]{1,0:T(8,128)(2,1)}, bf16[96,384]{1,0:T(8,128)(2,1)S(1)}, u32[]{:S(2)}, u32[]{:S(2)}) collective-permute-start(bf16[96,384]{1,0:T(8,128)(2,1)} %get-tuple-element.12), channel_id=1, source_target_pairs={{0,8},{8,16},{16,24},{24,32},{32,40},{40,48},{48,56},{56,64},{64,7... | collective-permute-start | bytes 221192 | tf_op jit(solution)/shard_map/ppermute | solution.py:31
  107.2 12.4 %collective-permute-start.9 = (bf16[4,96,384]{2,1,0:T(8,128)(2,1)}, bf16[4,96,384]{2,1,0:T(8,128)(2,1)S(1)}, u32[]{:S(2)}, u32[]{:S(2)}) collective-permute-start(bf16[4,96,384]{2,1,0:T(8,128)(2,1)} %get-tuple-element.14), channel_id=1, source_target_pairs={{0,64},{8,72},{16,80},{24,88},{32,96},{40,104},{48,112},{56,120},{... | collective-permute-start | bytes 884744 | tf_op jit(solution)/shard_map/ppermute | solution.py:31
  114.5 5.1 %copy-start.8 = (bf16[96,384]{1,0:T(8,128)(2,1)}, bf16[96,384]{1,0:T(8,128)(2,1)S(1)}, u32[]{:S(2)}) copy-start(bf16[96,384]{1,0:T(8,128)(2,1)S(1)} %collective-permute-done.7.prev_ref) | copy-start | bytes 221188
  114.5 2.3 %collective-permute-start.8 = (bf16[96,384]{1,0:T(8,128)(2,1)}, bf16[96,384]{1,0:T(8,128)(2,1)S(1)}, u32[]{:S(2)}, u32[]{:S(2)}) collective-permute-start(bf16[96,384]{1,0:T(8,128)(2,1)} %get-tuple-element.13), channel_id=1, source_target_pairs={{0,120},{8,0},{16,8},{24,16},{32,24},{40,32},{48,40},{56,48},{64,5... | collective-permute-start | bytes 221192 | tf_op jit(solution)/shard_map/ppermute | solution.py:31
  116.8 0.6 copy-start.9
  119.6 0.7 copy-start.5
  119.6 1.0 copy-start.3
  124.4 3.6 %copy-start.14 = (s32[8,2,1]{0,2,1:T(1,128)S(1)}, s32[8,2,1]{0,2,1:T(1,128)}, u32[]{:S(2)}) copy-start(s32[8,2,1]{0,2,1:T(1,128)} %get-tuple-element.17) | copy-start | bytes 196
  124.4 3.6 %copy-start.12 = (s32[64]{0:T(128)S(1)}, s32[64]{0:T(128)}, u32[]{:S(2)}) copy-start(s32[64]{0:T(128)} %param.11) | copy-start | bytes 772
  124.4 3.9 %copy-start.19 = (s32[8]{0:T(128)S(1)}, s32[8]{0:T(128)}, u32[]{:S(2)}) copy-start(s32[8]{0:T(128)} %copy-done.18) | copy-start | bytes 100
  124.4 3.9 %copy-start.16 = (s32[2]{0:T(128)S(1)}, s32[2]{0:T(128)}, u32[]{:S(2)}) copy-start(s32[2]{0:T(128)} %get-tuple-element.35) | copy-start | bytes 28
  124.4 19.4 %all-to-all-start.4 = ((bf16[8,48,1152]{2,1,0:T(8,128)(2,1)}), bf16[8,48,1152]{2,1,0:T(8,128)(2,1)S(1)}, u32[]{:S(2)}, u32[]{:S(2)}) async-start(bf16[8,48,1152]{2,1,0:T(8,128)(2,1)} %bitcast.22), calls=%async_computation.4 | async-start | bytes 1769472 | tf_op jit(solution)/shard_map/all_to_all | solution.py:248
  143.8 0.9 copy-start.1

commit v4 on v3

--- a/solution.py
+++ b/solution.py
@@ -126,7 +126,7 @@
             x_ref[span, base + 5 * BS : base + 6 * BS] = outs[1][:, 4 * BS :].astype(BF16)
 
 
-def place_kernel(j_ref, r_ref, out_ref, acc):
+def place_kernel(j_ref, r_ref, out_ref, acc, whole, sem):
     acc[...] = jnp.zeros_like(acc)
 
     def step(c, carry):
@@ -136,8 +136,16 @@
         return carry
 
     lax.fori_loop(0, COLS, step, 0)
-    for block in range(NCB):
-        out_ref[:, block * BS : (block + 1) * BS] = acc[block]
+    span = NCB // 4 * BS
+    copies = []
+    for part in range(4):
+        for block in range(part * NCB // 4, (part + 1) * NCB // 4):
+            whole[:, block * BS : (block + 1) * BS] = acc[block]
+        at = slice(part * span, (part + 1) * span)
+        copies.append(pltpu.make_async_copy(whole.at[:, at], out_ref.at[:, at], sem.at[part]))
+        copies[part].start()
+    for copy in copies:
+        copy.wait()
 
 
 VMEM = pl.BlockSpec(memory_space=pltpu.VMEM)
@@ -257,8 +265,13 @@
         place_kernel,
         out_shape=jax.ShapeDtypeStruct((4 * BS // COLS, NCB * BS), F32),
         in_specs=[SMEM, VMEM],
-        out_specs=VMEM,
-        scratch_shapes=[pltpu.VMEM((NCB, 4 * BS // COLS, BS), F32)],
+        out_specs=ANY,
+        scratch_shapes=[
+            pltpu.VMEM((NCB, 4 * BS // COLS, BS), F32),
+            pltpu.VMEM((4 * BS // COLS, NCB * BS), F32),
+            pltpu.SemaphoreType.DMA((4,)),
+        ],
+        compiler_params=pltpu.CompilerParams(vmem_limit_bytes=16 << 20),
         name="place",
     )(j_table, outs)
 

time: 150 us -> 148 us (0.987)
  local copies, waits for them, and re-layouts: 10.9 us -> 9.36 us
    unnamed x40 -> x38, local copies, waits for them, and re-layouts: 4.83 us -> 3.92 us
where the time goes in v4:
time: 148 us; the launch traced here: 147 us
  starting transfers between devices  71.3 us (48%)
  waiting for transfers between devices  42.1 us (28%)
  Pallas kernels  11.8 us (8%)
  local copies, waits for them, and re-layouts  9.36 us (6%)
  other arithmetic  6.97 us (5%)
  matrix products  4.85 us (3%)
    ppermute x10, starting transfers between devices, shift(): lax.ppermute(value, axis, [(i, (i + by) % size) for i in range(size)])  22.7 us
    ppermute x10, waiting for transfers between devices, shift(): lax.ppermute(value, axis, [(i, (i + by) % size) for i in range(size)])  16.8 us
    all_to_all x1, waiting for transfers between devices, inner(): lax.all_to_all(outs.reshape(COLS, 4 * BS // COLS, OUTSLOTS * BS), 'col',...  15.3 us
    all_to_all x1, starting transfers between devices, inner(): lax.all_to_all(jnp.broadcast_to(mine[None], (COLS, BS, PW)), 'col', 0, 0,...  14.3 us
    ppermute x3, starting transfers between devices, inner(): lax.ppermute(chosen, 'row', [(r, r ^ 2 << bit) for r in range(ROWS)])  8.06 us
    all_to_all x1, waiting for transfers between devices, inner(): spread = lax.all_to_all(spread, 'row', 0, 0, tiled=True)  7.73 us
    all_to_all x1, starting transfers between devices, inner(): spread = lax.all_to_all(spread, 'row', 0, 0, tiled=True)  7.47 us
    all_to_all x1, starting transfers between devices, inner(): lax.all_to_all(compact.reshape(COLS, USLOTS * area // 128, 128), 'col', 0...  6.07 us
  transfers between devices with their start and end apart: 21, of which 8 were waited for; matrix products, arithmetic and copies ran while one was open for 8% of the time, Pallas kernels for 3%

profile of v4, /device:TPU:0, one launch (start us, length us, event | category | flops | bytes accessed | tf_op | source)
XLA Modules:
  0.0 146.7 jit_solution(1028000278207537625)
XLA Ops:
  0.1 1.0 select_reduce_fusion.1
  1.2 0.1 copy.12
  1.2 0.7 broadcast_compare_fusion
  2.0 0.1 and_reduce_fusion
  2.1 0.1 copy.13
  2.2 1.8 %convolution_convert_fusion.1 = bf16[8,5,9216]{2,1,0:T(8,128)(2,1)S(1)} fusion(bf16[8,8,9216]{2,1,0:T(8,128)(2,1)} %param.8, s32[8]{0:T(128)S(1)} %iota_add_fusion.1, s32[8,5]{1,0:T(8,128)S(1)} %copy.12, pred[8,8]{1,0:T(8,128)(4,1)S(1)} %broadcast_compare_fusion, pred[8,5]{1,0:T(8,128)(4,1)S(1)} %copy.13), kind=kOutput, calls=%fused_computation.1 | convolution fusion | flops 6267840 | bytes 1917224 | tf_op jit(solution)/shard_map/iuj,ijf->iuf/dot_general | solution.py:169
  4.0 2.0 %reshape.955 = bf16[8,360,128]{2,1,0:T(8,128)(2,1)} reshape(bf16[8,5,9216]{2,1,0:T(8,128)(2,1)S(1)} %convolution_convert_fusion.1) | data formatting | bytes 1474560 | tf_op jit(solution)/shard_map/reshape | solution.py:173
  6.0 6.1 %all-to-all-start = ((bf16[8,360,128]{2,1,0:T(8,128)(2,1)}), bf16[8,360,128]{2,1,0:T(8,128)(2,1)S(1)}, u32[]{:S(2)}, u32[]{:S(2)}) async-start(bf16[8,360,128]{2,1,0:T(8,128)(2,1)} %reshape.955), calls=%async_computation | async-start | bytes 1474560 | tf_op jit(solution)/shard_map/all_to_all | solution.py:173
  12.2 0.8 convolution_convert_fusion
  13.0 1.5 fusion.54
  14.5 2.0 %collective-permute-start = (bf16[16,9216]{1,0:T(8,128)(2,1)}, bf16[16,9216]{1,0:T(8,128)(2,1)}, u32[]{:S(2)}, u32[]{:S(2)}) collective-permute-start(bf16[16,9216]{1,0:T(8,128)(2,1)} %get-tuple-element.25), channel_id=1, source_target_pairs={{0,1},{1,2},{2,3},{3,4},{4,5},{5,6},{6,7},{7,0},{8,9},{9,10},{10,1... | collective-permute-start | bytes 884744 | tf_op jit(solution)/shard_map/ppermute | solution.py:31
  16.5 1.4 collective-permute-start.1
  18.0 2.1 %collective-permute-start.2 = (bf16[16,9216]{1,0:T(8,128)(2,1)}, bf16[16,9216]{1,0:T(8,128)(2,1)}, u32[]{:S(2)}, u32[]{:S(2)}) collective-permute-start(bf16[16,9216]{1,0:T(8,128)(2,1)} %get-tuple-element.23), channel_id=1, source_target_pairs={{0,3},{1,4},{2,5},{3,6},{4,7},{5,0},{6,1},{7,2},{8,11},{9,12},{10,... | collective-permute-start | bytes 884744 | tf_op jit(solution)/shard_map/ppermute | solution.py:31
  20.0 2.1 %collective-permute-start.3 = (bf16[16,9216]{1,0:T(8,128)(2,1)}, bf16[16,9216]{1,0:T(8,128)(2,1)}, u32[]{:S(2)}, u32[]{:S(2)}) collective-permute-start(bf16[16,9216]{1,0:T(8,128)(2,1)} %get-tuple-element.22), channel_id=1, source_target_pairs={{0,4},{1,5},{2,6},{3,7},{4,0},{5,1},{6,2},{7,3},{8,12},{9,13},{10,... | collective-permute-start | bytes 884744 | tf_op jit(solution)/shard_map/ppermute | solution.py:31
  22.1 0.1 reshape.954
  22.3 0.6 and_select_fusion.22
  23.0 2.3 %all-to-all-done = bf16[8,360,128]{2,1,0:T(8,128)(2,1)S(1)} async-done(((bf16[8,360,128]{2,1,0:T(8,128)(2,1)}), bf16[8,360,128]{2,1,0:T(8,128)(2,1)S(1)}, u32[]{:S(2)}, u32[]{:S(2)}) %all-to-all-start) | async-done | bytes 737312 | tf_op jit(solution)/shard_map/all_to_all | solution.py:173
  25.3 0.1 reduce_sum.32
  25.4 0.1 reshape.956
  25.5 0.1 copy.14
  25.7 0.1 copy.15
  25.8 0.9 broadcast_in_dim.93
  26.7 14.3 %all-to-all-start.1 = ((bf16[8,96,512]{2,1,0:T(8,128)(2,1)}), bf16[8,96,512]{2,1,0:T(8,128)(2,1)S(1)}, u32[]{:S(2)}, u32[]{:S(2)}) async-start(bf16[8,96,512]{2,1,0:T(8,128)(2,1)} %broadcast_in_dim.93), calls=%async_computation.1 | async-start | bytes 1572864 | tf_op jit(solution)/shard_map/all_to_all | solution.py:188
  41.0 1.6 %collective-permute-start.10 = (bf16[2,96,512]{2,1,0:T(8,128)(2,1)S(1)}, bf16[2,96,512]{2,1,0:T(8,128)(2,1)S(1)}, u32[]{:S(2)}, u32[]{:S(2)}) collective-permute-start(bf16[2,96,512]{2,1,0:T(8,128)(2,1)S(1)} %pad_maximum_fusion), channel_id=1, source_target_pairs={{0,16},{8,24},{16,0},{24,8},{32,48},{40,56},{48,32},{56,40},{64,80... | collective-permute-start | bytes 589832 | tf_op jit(solution)/shard_map/ppermute | solution.py:191
  42.6 0.5 and_compare_fusion.2
  43.2 4.4 %collective-permute-start.4 = (bf16[16,9216]{1,0:T(8,128)(2,1)}, bf16[16,9216]{1,0:T(8,128)(2,1)S(1)}, u32[]{:S(2)}, u32[]{:S(2)}) collective-permute-start(bf16[16,9216]{1,0:T(8,128)(2,1)} %get-tuple-element.21), channel_id=1, source_target_pairs={{0,5},{1,6},{2,7},{3,0},{4,1},{5,2},{6,3},{7,4},{8,13},{9,14},{10,... | collective-permute-start | bytes 884744 | tf_op jit(solution)/shard_map/ppermute | solution.py:31
  47.6 1.2 collective-permute-start.5
  48.8 2.2 %collective-permute-start.6 = (bf16[16,9216]{1,0:T(8,128)(2,1)}, bf16[16,9216]{1,0:T(8,128)(2,1)}, u32[]{:S(2)}, u32[]{:S(2)}) collective-permute-start(bf16[16,9216]{1,0:T(8,128)(2,1)} %get-tuple-element.19), channel_id=1, source_target_pairs={{0,7},{1,0},{2,1},{3,2},{4,3},{5,4},{6,5},{7,6},{8,15},{9,8},{10,9... | collective-permute-start | bytes 884744 | tf_op jit(solution)/shard_map/ppermute | solution.py:31
  50.9 0.8 broadcast_select_fusion
  51.7 3.0 %collective-permute-start.11 = (bf16[2,96,512]{2,1,0:T(8,128)(2,1)}, bf16[2,96,512]{2,1,0:T(8,128)(2,1)}, u32[]{:S(2)}, u32[]{:S(2)}) collective-permute-start(bf16[2,96,512]{2,1,0:T(8,128)(2,1)} %broadcast_select_fusion), channel_id=1, source_target_pairs={{0,32},{8,40},{16,48},{24,56},{32,0},{40,8},{48,16},{56,24},{64,96... | collective-permute-start | bytes 589832 | tf_op jit(solution)/shard_map/ppermute | solution.py:191
  54.7 4.9 %collective-permute-done.4.refs_5_ = bf16[16,9216]{1,0:T(8,128)(2,1)S(1)} collective-permute-done((bf16[16,9216]{1,0:T(8,128)(2,1)}, bf16[16,9216]{1,0:T(8,128)(2,1)S(1)}, u32[]{:S(2)}, u32[]{:S(2)}) %collective-permute-start.4) | collective-permute-done | bytes 294944 | tf_op jit(solution)/shard_map/ppermute | solution.py:31
  59.6 0.7 copy-done.5
  60.4 0.7 copy-done.6
  61.1 4.0 %collective-permute-done.6.refs_7_ = bf16[16,9216]{1,0:T(8,128)(2,1)} collective-permute-done((bf16[16,9216]{1,0:T(8,128)(2,1)}, bf16[16,9216]{1,0:T(8,128)(2,1)}, u32[]{:S(2)}, u32[]{:S(2)}) %collective-permute-start.6) | collective-permute-done | bytes 294944 | tf_op jit(solution)/shard_map/ppermute | solution.py:31
  65.0 0.9 copy-done.1
  65.9 5.1 %partial.1 = (bf16[16,8,2304]{2,1,0:T(8,128)(2,1)}, f32[4,96,384]{2,1,0:T(8,128)}, bf16[96,384]{1,0:T(8,128)(2,1)}, bf16[96,384]{1,0:T(8,128)(2,1)}, bf16[4,96,384]{2,1,0:T(8,128)(2,1)}) custom-call(s32[2]{0:T(128)} %get-tuple-element.34.s_ref, bf16[8,96,512]{2,1,0:T(8,128)(2,1)} %copy-done.1, bf16[16,9216]{1,0:T(8,128)(2,1)} %get-tuple-element.26.refs_0_, ...), custom_call_target="tpu_custom_call" | custom-call | tf_op jit(solution)/shard_map/partial/pallas_call | solution.py:208
  71.0 7.5 %all-to-all-start.2 = ((bf16[16,8,2304]{2,1,0:T(8,128)(2,1)}), bf16[16,8,2304]{2,1,0:T(8,128)(2,1)}, u32[]{:S(2)}, u32[]{:S(2)}) async-start(bf16[16,8,2304]{2,1,0:T(8,128)(2,1)} %get-tuple-element.10), calls=%async_computation.2 | async-start | bytes 1179648 | tf_op jit(solution)/shard_map/all_to_all | solution.py:227
  78.5 0.7 and_select_fusion.2
  79.1 1.0 broadcast_select_fusion.1
  80.2 3.5 %collective-permute-start.12 = (bf16[2,96,512]{2,1,0:T(8,128)(2,1)S(1)}, bf16[2,96,512]{2,1,0:T(8,128)(2,1)S(1)}, u32[]{:S(2)}, u32[]{:S(2)}) collective-permute-start(bf16[2,96,512]{2,1,0:T(8,128)(2,1)S(1)} %broadcast_select_fusion.1), channel_id=1, source_target_pairs={{0,64},{8,72},{16,80},{24,88},{32,96},{40,104},{48,112},{56,120},{... | collective-permute-start | bytes 589832 | tf_op jit(solution)/shard_map/ppermute | solution.py:191
  83.6 0.1 add.606
  83.7 0.1 eq.133
  83.8 7.7 %all-to-all-done.2 = bf16[16,8,2304]{2,1,0:T(8,128)(2,1)} async-done(((bf16[16,8,2304]{2,1,0:T(8,128)(2,1)}), bf16[16,8,2304]{2,1,0:T(8,128)(2,1)}, u32[]{:S(2)}, u32[]{:S(2)}) %all-to-all-start.2) | async-done | bytes 589856 | tf_op jit(solution)/shard_map/all_to_all | solution.py:227
  91.5 2.2 %fusion.1 = bf16[16,8,2304]{2,1,0:T(8,128)(2,1)} fusion(bf16[16,8,2304]{2,1,0:T(8,128)(2,1)} %all-to-all-done.2, pred[128]{0:T(512)(128)(4,1)S(1)} %fusion.52, s32[128]{0:T(128)S(1)} %add.606, s32[128]{0:T(128)S(1)} %eq.133), kind=kOutput, calls=%fused_computation.4 | convolution fusion | flops 76693504 | bytes 1180800 | tf_op jit(solution)/shard_map/dot_general | solution.py:237
  93.8 3.7 %all-to-all-start.3 = ((bf16[16,8,2304]{2,1,0:T(8,128)(2,1)}), bf16[16,8,2304]{2,1,0:T(8,128)(2,1)S(1)}, u32[]{:S(2)}, u32[]{:S(2)}) async-start(bf16[16,8,2304]{2,1,0:T(8,128)(2,1)} %fusion.1), calls=%async_computation.3 | async-start | bytes 1179648 | tf_op jit(solution)/shard_map/all_to_all | solution.py:243
  97.5 0.1 broadcast_select_fusion.2.p_ref
  97.6 2.9 %collective-permute-start.13 = (bf16[2,96,512]{2,1,0:T(8,128)(2,1)S(1)}, bf16[2,96,512]{2,1,0:T(8,128)(2,1)}, u32[]{:S(2)}, u32[]{:S(2)}) collective-permute-start(bf16[2,96,512]{2,1,0:T(8,128)(2,1)S(1)} %broadcast_select_fusion.2.p_ref), channel_id=1, source_target_pairs={{0,8},{2,10},{4,12},{6,14},{9,1},{11,3},{13,5},{15,7},{16,24},{18,... | collective-permute-start | bytes 589832 | tf_op jit(solution)/shard_map/ppermute | solution.py:203
  100.5 1.3 collective-permute-start.14
  101.8 1.3 collective-permute-start.15
  103.1 4.1 %collective-permute-start.7 = (bf16[96,384]{1,0:T(8,128)(2,1)}, bf16[96,384]{1,0:T(8,128)(2,1)S(1)}, u32[]{:S(2)}, u32[]{:S(2)}) collective-permute-start(bf16[96,384]{1,0:T(8,128)(2,1)} %get-tuple-element.12), channel_id=1, source_target_pairs={{0,8},{8,16},{16,24},{24,32},{32,40},{40,48},{48,56},{56,64},{64,7... | collective-permute-start | bytes 221192 | tf_op jit(solution)/shard_map/ppermute | solution.py:31
  107.2 3.2 %collective-permute-start.9 = (bf16[4,96,384]{2,1,0:T(8,128)(2,1)}, bf16[4,96,384]{2,1,0:T(8,128)(2,1)S(1)}, u32[]{:S(2)}, u32[]{:S(2)}) collective-permute-start(bf16[4,96,384]{2,1,0:T(8,128)(2,1)} %get-tuple-element.14), channel_id=1, source_target_pairs={{0,64},{8,72},{16,80},{24,88},{32,96},{40,104},{48,112},{56,120},{... | collective-permute-start | bytes 884744 | tf_op jit(solution)/shard_map/ppermute | solution.py:31
  110.4 4.1 %collective-permute-done.7.prev_ref = bf16[96,384]{1,0:T(8,128)(2,1)S(1)} collective-permute-done((bf16[96,384]{1,0:T(8,128)(2,1)}, bf16[96,384]{1,0:T(8,128)(2,1)S(1)}, u32[]{:S(2)}, u32[]{:S(2)}) %collective-permute-start.7) | collective-permute-done | bytes 73760 | tf_op jit(solution)/shard_map/ppermute | solution.py:31
  114.5 0.6 pad_add_fusion.6.c_ref
  115.2 1.7 %collective-permute-done.8.next_ref = bf16[96,384]{1,0:T(8,128)(2,1)S(1)} collective-permute-done((bf16[96,384]{1,0:T(8,128)(2,1)}, bf16[96,384]{1,0:T(8,128)(2,1)S(1)}, u32[]{:S(2)}, u32[]{:S(2)}) %collective-permute-start.8) | collective-permute-done | bytes 73760 | tf_op jit(solution)/shard_map/ppermute | solution.py:31
  116.8 0.6 copy-done.8
  117.4 2.2 %collective-permute-done.9.far_ref = bf16[4,96,384]{2,1,0:T(8,128)(2,1)S(1)} collective-permute-done((bf16[4,96,384]{2,1,0:T(8,128)(2,1)}, bf16[4,96,384]{2,1,0:T(8,128)(2,1)S(1)}, u32[]{:S(2)}, u32[]{:S(2)}) %collective-permute-start.9) | collective-permute-done | bytes 294944 | tf_op jit(solution)/shard_map/ppermute | solution.py:31
  119.6 0.7 copy-done.4
  120.3 0.2 copy-done.2
  120.6 3.8 %product.1 = bf16[384,1152]{1,0:T(8,128)(2,1)} custom-call(s32[2]{0:T(128)} %pad_add_fusion.6.c_ref, bf16[16,8,2304]{2,1,0:T(8,128)(2,1)} %copy-done.2, f32[4,96,384]{2,1,0:T(8,128)} %get-tuple-element.11.own_ref, bf16[96,384]{1,0:T(8,128)(2,1)} %copy-done.7, bf16[96,384]{1,0:T(8,128)(2,1)} %copy-done.8, bf16[4,96,384]{2,1,0:T(8,128)(2,1)} %copy-done.4, ...), custom_call_target="tpu_custom_call" | custom-call | tf_op jit(solution)/shard_map/product/pallas_call | solution.py:246
  124.4 3.6 %all-to-all-start.4 = ((bf16[8,48,1152]{2,1,0:T(8,128)(2,1)}), bf16[8,48,1152]{2,1,0:T(8,128)(2,1)S(1)}, u32[]{:S(2)}, u32[]{:S(2)}) async-start(bf16[8,48,1152]{2,1,0:T(8,128)(2,1)} %bitcast.22), calls=%async_computation.4 | async-start | bytes 1769472 | tf_op jit(solution)/shard_map/all_to_all | solution.py:256
  128.0 0.3 select_reduce_fusion
  128.4 0.1 copy.16.j_ref
  128.5 15.3 %all-to-all-done.4.r_ref = bf16[8,48,1152]{2,1,0:T(8,128)(2,1)S(1)} async-done(((bf16[8,48,1152]{2,1,0:T(8,128)(2,1)}), bf16[8,48,1152]{2,1,0:T(8,128)(2,1)S(1)}, u32[]{:S(2)}, u32[]{:S(2)}) %all-to-all-start.4) | async-done | bytes 884768 | tf_op jit(solution)/shard_map/all_to_all | solution.py:256
  143.8 2.9 %place.1 = f32[48,6144]{1,0:T(8,128)} custom-call(s32[8,12]{1,0:T(8,128)S(1)} %copy.16.j_ref, bf16[8,48,1152]{2,1,0:T(8,128)(2,1)S(1)} %all-to-all-done.4.r_ref), custom_call_target="tpu_custom_call" | custom-call | tf_op jit(solution)/shard_map/place/pallas_call | solution.py:264
  (73 shorter events, 0.7 us)
Async XLA Ops:
  0.0 12.2 %copy-start = (bf16[8,16,9216]{2,1,0:T(8,128)(2,1)S(1)}, bf16[8,16,9216]{2,1,0:T(8,128)(2,1)}, u32[]{:S(2)}) copy-start(bf16[8,16,9216]{2,1,0:T(8,128)(2,1)} %param.6) | copy-start | bytes 7077892
  6.0 6.1 %copy-start.12 = (s32[8,16]{1,0:T(8,128)S(1)}, s32[8,16]{1,0:T(8,128)}, u32[]{:S(2)}) copy-start(s32[8,16]{1,0:T(8,128)} %param.7) | copy-start | bytes 1540
  6.0 19.3 %all-to-all-start = ((bf16[8,360,128]{2,1,0:T(8,128)(2,1)}), bf16[8,360,128]{2,1,0:T(8,128)(2,1)S(1)}, u32[]{:S(2)}, u32[]{:S(2)}) async-start(bf16[8,360,128]{2,1,0:T(8,128)(2,1)} %reshape.955), calls=%async_computation | async-start | bytes 1474560 | tf_op jit(solution)/shard_map/all_to_all | solution.py:173
  13.0 9.1 %copy-start.10 = (s32[64]{0:T(128)S(1)}, s32[64]{0:T(128)}, u32[]{:S(2)}) copy-start(s32[64]{0:T(128)} %param.11) | copy-start | bytes 772
  13.0 9.3 %copy-start.14 = (s32[2]{0:T(128)S(1)}, s32[2]{0:T(128)}, u32[]{:S(2)}) copy-start(s32[2]{0:T(128)} %param.10) | copy-start | bytes 28
  14.5 28.7 %collective-permute-start = (bf16[16,9216]{1,0:T(8,128)(2,1)}, bf16[16,9216]{1,0:T(8,128)(2,1)}, u32[]{:S(2)}, u32[]{:S(2)}) collective-permute-start(bf16[16,9216]{1,0:T(8,128)(2,1)} %get-tuple-element.25), channel_id=1, source_target_pairs={{0,1},{1,2},{2,3},{3,4},{4,5},{5,6},{6,7},{7,0},{8,9},{9,10},{10,1... | collective-permute-start | bytes 884744 | tf_op jit(solution)/shard_map/ppermute | solution.py:31
  16.5 31.1 %collective-permute-start.1 = (bf16[16,9216]{1,0:T(8,128)(2,1)}, bf16[16,9216]{1,0:T(8,128)(2,1)}, u32[]{:S(2)}, u32[]{:S(2)}) collective-permute-start(bf16[16,9216]{1,0:T(8,128)(2,1)} %get-tuple-element.24), channel_id=1, source_target_pairs={{0,2},{1,3},{2,4},{3,5},{4,6},{5,7},{6,0},{7,1},{8,10},{9,11},{10,... | collective-permute-start | bytes 884744 | tf_op jit(solution)/shard_map/ppermute | solution.py:31
  18.0 33.7 %collective-permute-start.2 = (bf16[16,9216]{1,0:T(8,128)(2,1)}, bf16[16,9216]{1,0:T(8,128)(2,1)}, u32[]{:S(2)}, u32[]{:S(2)}) collective-permute-start(bf16[16,9216]{1,0:T(8,128)(2,1)} %get-tuple-element.23), channel_id=1, source_target_pairs={{0,3},{1,4},{2,5},{3,6},{4,7},{5,0},{6,1},{7,2},{8,11},{9,12},{10,... | collective-permute-start | bytes 884744 | tf_op jit(solution)/shard_map/ppermute | solution.py:31
  20.0 34.7 %collective-permute-start.3 = (bf16[16,9216]{1,0:T(8,128)(2,1)}, bf16[16,9216]{1,0:T(8,128)(2,1)}, u32[]{:S(2)}, u32[]{:S(2)}) collective-permute-start(bf16[16,9216]{1,0:T(8,128)(2,1)} %get-tuple-element.22), channel_id=1, source_target_pairs={{0,4},{1,5},{2,6},{3,7},{4,0},{5,1},{6,2},{7,3},{8,12},{9,13},{10,... | collective-permute-start | bytes 884744 | tf_op jit(solution)/shard_map/ppermute | solution.py:31
  26.7 38.3 %all-to-all-start.1 = ((bf16[8,96,512]{2,1,0:T(8,128)(2,1)}), bf16[8,96,512]{2,1,0:T(8,128)(2,1)S(1)}, u32[]{:S(2)}, u32[]{:S(2)}) async-start(bf16[8,96,512]{2,1,0:T(8,128)(2,1)} %broadcast_in_dim.93), calls=%async_computation.1 | async-start | bytes 1572864 | tf_op jit(solution)/shard_map/all_to_all | solution.py:188
  41.0 7.7 %collective-permute-start.10 = (bf16[2,96,512]{2,1,0:T(8,128)(2,1)S(1)}, bf16[2,96,512]{2,1,0:T(8,128)(2,1)S(1)}, u32[]{:S(2)}, u32[]{:S(2)}) collective-permute-start(bf16[2,96,512]{2,1,0:T(8,128)(2,1)S(1)} %pad_maximum_fusion), channel_id=1, source_target_pairs={{0,16},{8,24},{16,0},{24,8},{32,48},{40,56},{48,32},{56,40},{64,80... | collective-permute-start | bytes 589832 | tf_op jit(solution)/shard_map/ppermute | solution.py:191
  43.2 16.5 %collective-permute-start.4 = (bf16[16,9216]{1,0:T(8,128)(2,1)}, bf16[16,9216]{1,0:T(8,128)(2,1)S(1)}, u32[]{:S(2)}, u32[]{:S(2)}) collective-permute-start(bf16[16,9216]{1,0:T(8,128)(2,1)} %get-tuple-element.21), channel_id=1, source_target_pairs={{0,5},{1,6},{2,7},{3,0},{4,1},{5,2},{6,3},{7,4},{8,13},{9,14},{10,... | collective-permute-start | bytes 884744 | tf_op jit(solution)/shard_map/ppermute | solution.py:31
  47.6 12.1 %collective-permute-start.5 = (bf16[16,9216]{1,0:T(8,128)(2,1)}, bf16[16,9216]{1,0:T(8,128)(2,1)S(1)}, u32[]{:S(2)}, u32[]{:S(2)}) collective-permute-start(bf16[16,9216]{1,0:T(8,128)(2,1)} %get-tuple-element.20), channel_id=1, source_target_pairs={{0,6},{1,7},{2,0},{3,1},{4,2},{5,3},{6,4},{7,5},{8,14},{9,15},{10,... | collective-permute-start | bytes 884744 | tf_op jit(solution)/shard_map/ppermute | solution.py:31
  48.8 16.3 %collective-permute-start.6 = (bf16[16,9216]{1,0:T(8,128)(2,1)}, bf16[16,9216]{1,0:T(8,128)(2,1)}, u32[]{:S(2)}, u32[]{:S(2)}) collective-permute-start(bf16[16,9216]{1,0:T(8,128)(2,1)} %get-tuple-element.19), channel_id=1, source_target_pairs={{0,7},{1,0},{2,1},{3,2},{4,3},{5,4},{6,5},{7,6},{8,15},{9,8},{10,9... | collective-permute-start | bytes 884744 | tf_op jit(solution)/shard_map/ppermute | solution.py:31
  50.9 27.5 %copy-start.17 = (s32[8]{0:T(128)}, s32[8]{0:T(128)S(1)}, u32[]{:S(2)}) copy-start(s32[8]{0:T(128)S(1)} %fusion.28) | copy-start | bytes 100
  51.7 27.4 %collective-permute-start.11 = (bf16[2,96,512]{2,1,0:T(8,128)(2,1)}, bf16[2,96,512]{2,1,0:T(8,128)(2,1)}, u32[]{:S(2)}, u32[]{:S(2)}) collective-permute-start(bf16[2,96,512]{2,1,0:T(8,128)(2,1)} %broadcast_select_fusion), channel_id=1, source_target_pairs={{0,32},{8,40},{16,48},{24,56},{32,0},{40,8},{48,16},{56,24},{64,96... | collective-permute-start | bytes 589832 | tf_op jit(solution)/shard_map/ppermute | solution.py:191
  59.6 0.7 copy-start.5
  60.4 0.7 copy-start.6
  65.0 0.9 copy-start.1
  71.0 20.6 %all-to-all-start.2 = ((bf16[16,8,2304]{2,1,0:T(8,128)(2,1)}), bf16[16,8,2304]{2,1,0:T(8,128)(2,1)}, u32[]{:S(2)}, u32[]{:S(2)}) async-start(bf16[16,8,2304]{2,1,0:T(8,128)(2,1)} %get-tuple-element.10), calls=%async_computation.2 | async-start | bytes 1179648 | tf_op jit(solution)/shard_map/all_to_all | solution.py:227
  80.2 17.4 %collective-permute-start.12 = (bf16[2,96,512]{2,1,0:T(8,128)(2,1)S(1)}, bf16[2,96,512]{2,1,0:T(8,128)(2,1)S(1)}, u32[]{:S(2)}, u32[]{:S(2)}) collective-permute-start(bf16[2,96,512]{2,1,0:T(8,128)(2,1)S(1)} %broadcast_select_fusion.1), channel_id=1, source_target_pairs={{0,64},{8,72},{16,80},{24,88},{32,96},{40,104},{48,112},{56,120},{... | collective-permute-start | bytes 589832 | tf_op jit(solution)/shard_map/ppermute | solution.py:191
  83.8 13.7 %copy-start.16 = (pred[2]{0:T(512)(128)(4,1)S(1)}, pred[2]{0:T(512)(128)(4,1)}, u32[]{:S(2)}) copy-start(pred[2]{0:T(512)(128)(4,1)} %get-tuple-element.31) | copy-start | bytes 10
  93.8 16.6 %copy-start.9 = (s32[8,2,1]{0,2,1:T(1,128)S(1)}, s32[8,2,1]{0,2,1:T(1,128)}, u32[]{:S(2)}) copy-start(s32[8,2,1]{0,2,1:T(1,128)} %get-tuple-element.18) | copy-start | bytes 196
  93.8 25.8 %all-to-all-start.3 = ((bf16[16,8,2304]{2,1,0:T(8,128)(2,1)}), bf16[16,8,2304]{2,1,0:T(8,128)(2,1)S(1)}, u32[]{:S(2)}, u32[]{:S(2)}) async-start(bf16[16,8,2304]{2,1,0:T(8,128)(2,1)} %fusion.1), calls=%async_computation.3 | async-start | bytes 1179648 | tf_op jit(solution)/shard_map/all_to_all | solution.py:243
  97.6 22.0 %copy-start.3 = (bf16[2,96,512]{2,1,0:T(8,128)(2,1)}, bf16[2,96,512]{2,1,0:T(8,128)(2,1)S(1)}, u32[]{:S(2)}) copy-start(bf16[2,96,512]{2,1,0:T(8,128)(2,1)S(1)} %broadcast_select_fusion.2.p_ref) | copy-start | bytes 589828
  97.6 19.2 %collective-permute-start.13 = (bf16[2,96,512]{2,1,0:T(8,128)(2,1)S(1)}, bf16[2,96,512]{2,1,0:T(8,128)(2,1)}, u32[]{:S(2)}, u32[]{:S(2)}) collective-permute-start(bf16[2,96,512]{2,1,0:T(8,128)(2,1)S(1)} %broadcast_select_fusion.2.p_ref), channel_id=1, source_target_pairs={{0,8},{2,10},{4,12},{6,14},{9,1},{11,3},{13,5},{15,7},{16,24},{18,... | collective-permute-start | bytes 589832 | tf_op jit(solution)/shard_map/ppermute | solution.py:203
  100.5 16.3 %collective-permute-start.14 = (bf16[2,96,512]{2,1,0:T(8,128)(2,1)S(1)}, bf16[2,96,512]{2,1,0:T(8,128)(2,1)}, u32[]{:S(2)}, u32[]{:S(2)}) collective-permute-start(bf16[2,96,512]{2,1,0:T(8,128)(2,1)S(1)} %broadcast_select_fusion.2.p_ref), channel_id=1, source_target_pairs={{1,0},{3,2},{5,4},{7,6},{8,9},{10,11},{12,13},{14,15},{17,16},{19,... | collective-permute-start | bytes 589832 | tf_op jit(solution)/shard_map/ppermute | solution.py:203
  101.8 15.0 %collective-permute-start.15 = (bf16[2,96,512]{2,1,0:T(8,128)(2,1)S(1)}, bf16[2,96,512]{2,1,0:T(8,128)(2,1)}, u32[]{:S(2)}, u32[]{:S(2)}) collective-permute-start(bf16[2,96,512]{2,1,0:T(8,128)(2,1)S(1)} %broadcast_select_fusion.2.p_ref), channel_id=1, source_target_pairs={{1,8},{3,10},{5,12},{7,14},{8,1},{10,3},{12,5},{14,7},{17,24},{19,... | collective-permute-start | bytes 589832 | tf_op jit(solution)/shard_map/ppermute | solution.py:203
  103.1 11.4 %collective-permute-start.7 = (bf16[96,384]{1,0:T(8,128)(2,1)}, bf16[96,384]{1,0:T(8,128)(2,1)S(1)}, u32[]{:S(2)}, u32[]{:S(2)}) collective-permute-start(bf16[96,384]{1,0:T(8,128)(2,1)} %get-tuple-element.12), channel_id=1, source_target_pairs={{0,8},{8,16},{16,24},{24,32},{32,40},{40,48},{48,56},{56,64},{64,7... | collective-permute-start | bytes 221192 | tf_op jit(solution)/shard_map/ppermute | solution.py:31
  107.2 12.4 %collective-permute-start.9 = (bf16[4,96,384]{2,1,0:T(8,128)(2,1)}, bf16[4,96,384]{2,1,0:T(8,128)(2,1)S(1)}, u32[]{:S(2)}, u32[]{:S(2)}) collective-permute-start(bf16[4,96,384]{2,1,0:T(8,128)(2,1)} %get-tuple-element.14), channel_id=1, source_target_pairs={{0,64},{8,72},{16,80},{24,88},{32,96},{40,104},{48,112},{56,120},{... | collective-permute-start | bytes 884744 | tf_op jit(solution)/shard_map/ppermute | solution.py:31
  114.5 5.1 %copy-start.7 = (bf16[96,384]{1,0:T(8,128)(2,1)}, bf16[96,384]{1,0:T(8,128)(2,1)S(1)}, u32[]{:S(2)}) copy-start(bf16[96,384]{1,0:T(8,128)(2,1)S(1)} %collective-permute-done.7.prev_ref) | copy-start | bytes 221188
  114.5 2.3 %collective-permute-start.8 = (bf16[96,384]{1,0:T(8,128)(2,1)}, bf16[96,384]{1,0:T(8,128)(2,1)S(1)}, u32[]{:S(2)}, u32[]{:S(2)}) collective-permute-start(bf16[96,384]{1,0:T(8,128)(2,1)} %get-tuple-element.13), channel_id=1, source_target_pairs={{0,120},{8,0},{16,8},{24,16},{32,24},{40,32},{48,40},{56,48},{64,5... | collective-permute-start | bytes 221192 | tf_op jit(solution)/shard_map/ppermute | solution.py:31
  116.8 0.6 copy-start.8
  119.6 0.7 copy-start.4
  119.6 1.0 copy-start.2
  124.4 3.6 %copy-start.13 = (s32[8,2,1]{0,2,1:T(1,128)S(1)}, s32[8,2,1]{0,2,1:T(1,128)}, u32[]{:S(2)}) copy-start(s32[8,2,1]{0,2,1:T(1,128)} %get-tuple-element.17) | copy-start | bytes 196
  124.4 3.6 %copy-start.11 = (s32[64]{0:T(128)S(1)}, s32[64]{0:T(128)}, u32[]{:S(2)}) copy-start(s32[64]{0:T(128)} %param.11) | copy-start | bytes 772
  124.4 3.9 %copy-start.18 = (s32[8]{0:T(128)S(1)}, s32[8]{0:T(128)}, u32[]{:S(2)}) copy-start(s32[8]{0:T(128)} %copy-done.17) | copy-start | bytes 100
  124.4 3.9 %copy-start.15 = (s32[2]{0:T(128)S(1)}, s32[2]{0:T(128)}, u32[]{:S(2)}) copy-start(s32[2]{0:T(128)} %get-tuple-element.35) | copy-start | bytes 28
  124.4 19.4 %all-to-all-start.4 = ((bf16[8,48,1152]{2,1,0:T(8,128)(2,1)}), bf16[8,48,1152]{2,1,0:T(8,128)(2,1)S(1)}, u32[]{:S(2)}, u32[]{:S(2)}) async-start(bf16[8,48,1152]{2,1,0:T(8,128)(2,1)} %bitcast.22), calls=%async_computation.4 | async-start | bytes 1769472 | tf_op jit(solution)/shard_map/all_to_all | solution.py:256
